TPU v7x, 256 devices: a whole 4x4x8 slice. The times are simulated.
256 devices in a mesh: section: 4 (over x), space: 64 (over z, y, core).
Axes of the slice: x: 4, y: 4, z: 8, core: 2. Of those that a mesh axis runs over, the one named last changes fastest.
Arguments:
- encoder_inputs: bfloat16 [4, 1, 128, 256, 2, 64], P('section', None, None, 'space'), may hold values from -6 to 6
- upper_inputs: bfloat16 [4, 1, 128, 256, 2, 64], P('section', None, None, 'space'), may hold values from -6 to 6
- output_cotangent: bfloat16 [1, 128, 256, 2, 64], P(None, None, 'space'), may hold values from -6 to 6
- weights: bfloat16 [4, 4, 3, 128, 1152], P('section'), may hold values from -0.15625 to 0.15625
- biases: float32 [4, 4, 128], P('section'), may hold values from -3 to 3
Outputs:
- encoder_grad: bfloat16 [4, 1, 128, 256, 2, 64], P('section', None, None, 'space')
- upper_grad: bfloat16 [4, 1, 128, 256, 2, 64], P('section', None, None, 'space')
- weight_grad: float32 [4, 4, 3, 128, 1152], P('section')
- bias_grad: float32 [4, 4, 128], P('section')
All inputs are finite; a program needn't handle non-finite values.
Results may differ from a plain program's by a relative error of at most 0.018.
Values may be sent and summed in bfloat16 or wider, within the bound.
No kernel may reach another device: no remote copies, remote signals or barrier semaphores. Data moves between devices by JAX's collectives and lax.ppermute only.
A program may use at most 64 MiB of HBM per device.

v0:
```python
import jax
import jax.numpy as jnp
from jax import lax
from jax.experimental import pallas as pl
from jax.experimental.pallas import tpu as pltpu
from jax.sharding import PartitionSpec as P


C = 128
Y = 2
Z = 64
W = Y * C
SPACE = 64
SECTIONS = 4
ROWS = 4
CELLS = ROWS * Z
BF = jnp.bfloat16
F32 = jnp.float32
VMEM = pl.BlockSpec(memory_space=pltpu.VMEM)
ANY = pl.BlockSpec(memory_space=pl.ANY)
SMEM = pl.BlockSpec(memory_space=pltpu.SMEM)


def z_shifts(value):
    count = value.shape[0]
    wide = value.astype(F32)
    depth = lax.broadcasted_iota(jnp.int32, (count, W), 0) % Z
    below = jnp.where(depth == 0, 0.0, pltpu.roll(wide, 1, 0)).astype(BF)
    above = jnp.where(depth == Z - 1, 0.0, pltpu.roll(wide, count - 1, 0)).astype(BF)
    return below, value, above


def tap(w, a, b, c):
    lane = (3 * b + c) * C
    return w[a, :, lane : lane + C]


def row_mask(count, first, place):
    row = lax.broadcasted_iota(jnp.int32, (count * Z, W), 0) // Z + (first + ROWS * place)
    return (row >= 0) & (row < SPACE * ROWS)


def conv(value, w, out_rows):
    stacked = jnp.concatenate(z_shifts(value), axis=1)
    total = None
    for a in range(3):
        kernel = jnp.concatenate(
            [
                jnp.concatenate([tap(w, a, y_in - y_out + 1, c) for c in range(3) for y_in in range(Y)], axis=1)
                for y_out in range(Y)
            ],
            axis=0,
        )
        part = lax.dot_general(
            stacked[a * Z : (a + out_rows) * Z],
            kernel,
            (((1,), (1,)), ((), ())),
            preferred_element_type=F32,
        )
        total = part if total is None else total + part
    return total


def conv_adjoint(value, w, out_rows):
    below, same, above = z_shifts(value)
    stacked = jnp.concatenate([above, same, below], axis=1)
    total = None
    for a in range(3):
        kernel = jnp.concatenate(
            [
                jnp.concatenate([tap(w, a, y_in - y_out + 1, c) for y_in in range(Y)], axis=1)
                for c in range(3)
                for y_out in range(Y)
            ],
            axis=0,
        )
        part = jnp.dot(
            stacked[(2 - a) * Z : (2 - a + out_rows) * Z], kernel, preferred_element_type=F32
        )
        total = part if total is None else total + part
    return total


def gated(pre):
    logistic = jax.nn.sigmoid(pre)
    return pre * logistic, logistic * (1.0 + pre * (1.0 - logistic))


def middle(value, halo, keep):
    return value[(halo - keep) * Z : (halo + ROWS + keep) * Z]


def encode_kernel(place_ref, w_ref, bias_ref, far_left, left, own, right, far_right, *outs):
    v_ref, h_ref, s1_ref, s2_ref, out_ref = outs
    inputs = jnp.concatenate(
        [far_left[...], left[...], own[...], right[...], far_right[...]], axis=0
    )
    v_ref[...] = middle(inputs, 6, 1)
    act, slope = gated(conv(inputs, w_ref.at[0], 14) + bias_ref[0:1, :])
    s1_ref[...] = middle(slope, 5, 1)
    act = jnp.where(row_mask(14, -5, place_ref[0]), act, 0.0).astype(BF)
    h_ref[...] = middle(act, 5, 1)
    act, slope = gated(conv(act, w_ref.at[1], 12) + bias_ref[1:2, :])
    s2_ref[...] = middle(slope, 4, 2)
    out_ref[...] = act.astype(BF)


def decode_kernel(place_ref, w_ref, bias_ref, enc_ref, left, own, right, *outs):
    v_ref, h_ref, s1_ref, s2_ref = outs
    place = place_ref[0]
    upper = jnp.concatenate([left[0:CELLS], own[0:CELLS], right[0:CELLS]], axis=0)
    act = enc_ref[...].astype(F32) + upper.astype(F32)
    act = jnp.where(row_mask(12, -4, place), act, 0.0).astype(BF)
    v_ref[...] = middle(act, 4, 1)
    act, slope = gated(conv(act, w_ref.at[2], 10) + bias_ref[2:3, :])
    s1_ref[...] = middle(slope, 3, 1)
    act = jnp.where(row_mask(10, -3, place), act, 0.0).astype(BF)
    h_ref[...] = middle(act, 3, 1)
    _, slope = gated(conv(act, w_ref.at[3], 8) + bias_ref[3:4, :])
    s2_ref[...] = middle(slope, 2, 2)


def sds(rows, dtype):
    return jax.ShapeDtypeStruct((rows * Z, W), dtype)


def forward(kernel, more, *args):
    return pl.pallas_call(
        kernel,
        out_shape=[sds(6, BF), sds(6, BF), sds(6, F32), sds(8, F32)] + more,
        in_specs=[SMEM] + [VMEM] * (len(args) - 1),
        out_specs=[VMEM] * (4 + len(more)),
        compiler_params=pltpu.CompilerParams(vmem_limit_bytes=16 << 20),
        cost_estimate=pl.CostEstimate(flops=3 * 10**9, bytes_accessed=5 << 20, transcendentals=0),
    )(*args)


def tick_kernel(layer, turn, seeded, place_ref, w_ref, *refs):
    names = list(refs)
    s1_ref, s2_ref = names[0:2]
    cots = [names[2:5]]
    rest = names[5:]
    if seeded == "sum":
        cots.append(rest[0:3])
        rest = rest[3:]
    outs = rest[-5:]
    place = place_ref[0]

    def run():
        def window(three):
            low, mid, high = (ref[...] for ref in three)
            return jnp.concatenate([low, mid, high], axis=0)

        g = window(cots[0]).astype(F32)
        if len(cots) > 1:
            g = (g + window(cots[1]).astype(F32)).astype(BF).astype(F32)
        second = (g * s2_ref[...]).astype(BF)
        outs[0][...] = second[2 * Z : 2 * Z + CELLS]
        first = conv_adjoint(second, w_ref.at[layer + 1], 6) * s1_ref[...]
        first = jnp.where(row_mask(6, -1, place), first, 0.0).astype(BF)
        outs[1][...] = first[Z : Z + CELLS]
        grad = conv_adjoint(first, w_ref.at[layer], 4).astype(BF)
        outs[2][...] = grad
        outs[3][...] = grad[0 : 2 * Z]
        outs[4][...] = grad[CELLS - 2 * Z : CELLS]

    if turn is None:
        run()
        return

    def carry():
        for out, ref in zip(outs, rest[:5]):
            out[...] = ref[...]

    mine = place_ref[1] == turn
    pl.when(mine)(run)
    pl.when(jnp.logical_not(mine))(carry)


def tick(layer, turn, place, weights, slopes, cot, skip=None, state=None):
    args = [place, weights, *slopes, *cot]
    seeded = "plain"
    if skip is not None:
        args += list(skip)
        seeded = "sum"
    if state is not None:
        args += list(state)
    return pl.pallas_call(
        lambda *refs: tick_kernel(layer, turn, seeded, *refs),
        out_shape=[sds(4, BF)] * 3 + [sds(2, BF)] * 2,
        in_specs=[SMEM] + [VMEM] * (len(args) - 1),
        out_specs=[VMEM] * 5,
        compiler_params=pltpu.CompilerParams(vmem_limit_bytes=16 << 20),
        cost_estimate=pl.CostEstimate(flops=3 * 10**9, bytes_accessed=4 << 20, transcendentals=0),
        name="tick",
    )(*args)


PARTS = 4
PIECES = 8
USED = 27 * C // PARTS
PIECE = 112
PART = PIECES * PIECE
GRID_AXES = ("section", "space")


def shifted(source_section, by, step):
    pairs = []
    for place in range(SPACE):
        if 0 <= place + step < SPACE:
            source = source_section * SPACE + place
            pairs.append((source, source + by * SPACE + step))
    return pairs


def hand_on(state, source_section, by):
    grad, low, high = state[2:5]
    middle = lax.ppermute(grad, GRID_AXES, shifted(source_section, by, 0))
    before = lax.ppermute(high, GRID_AXES, shifted(source_section, by, 1))
    after = lax.ppermute(low, GRID_AXES, shifted(source_section, by, -1))
    return (before, middle, after)


def beside(array, step):
    pairs = [(place, place + step) for place in range(SPACE) if 0 <= place + step < SPACE]
    return lax.ppermute(array, "space", pairs)


def weight_kernel(group, place_ref, *refs):
    section = place_ref[1]

    @pl.when((section >= group[0]) & (section <= group[-1]))
    def _():
        weight_body(place_ref[0] % 2, *refs)


def weight_body(core, u1_ref, v1_ref, u2_ref, v2_ref, keep_ref, send_ref, held):
    for layer, (u_ref, v_ref) in enumerate(((u1_ref, v1_ref), (u2_ref, v2_ref))):
        grads = u_ref[...]
        wide = grads.astype(F32)
        turned = wide.T.astype(BF)
        stacked = jnp.concatenate(z_shifts(v_ref[...]), axis=1)
        for a in range(3):
            product = jnp.dot(
                turned, stacked[a * Z : a * Z + CELLS], preferred_element_type=F32
            )

            def block(y_out, c, y_in):
                lane = (c * Y + y_in) * C
                return product[y_out * C : (y_out + 1) * C, lane : lane + C]

            for c in range(3):
                blocks = (block(1, c, 0), block(0, c, 0) + block(1, c, 1), block(0, c, 1))
                for b in range(3):
                    value = blocks[b].astype(BF)
                    row = (9 * a + 3 * b + c) * (C // PARTS)
                    for part in range(PARTS):
                        held[layer, part, row : row + C // PARTS, :] = value[
                            part * (C // PARTS) : (part + 1) * (C // PARTS)
                        ]
        sums = jnp.sum(wide, axis=0, keepdims=True)
        sums = sums[:, 0:C] + sums[:, C : 2 * C]
        for part in range(PARTS):
            held[layer, part, USED:PART, :] = jnp.broadcast_to(sums, (PART - USED, C)).astype(BF)
    keep_ref[...] = held[core]
    send_ref[...] = held[1 - core]


def weight_terms(place, group, u1, v1, u2, v2):
    shape = jax.ShapeDtypeStruct((PARTS, PART, C), BF)
    return pl.pallas_call(
        lambda *refs: weight_kernel(group, *refs),
        out_shape=[shape, shape],
        in_specs=[SMEM] + [VMEM] * 4,
        out_specs=[VMEM] * 2,
        scratch_shapes=[pltpu.VMEM((2, PARTS, PART, C), BF)],
        compiler_params=pltpu.CompilerParams(vmem_limit_bytes=16 << 20),
        cost_estimate=pl.CostEstimate(flops=2 * 10**9, bytes_accessed=4 << 20, transcendentals=0),
        name="weights",
    )(place, u1, v1, u2, v2)


def split_kernel(ways, spot, count, place_ref, *refs):
    owns, arrived, outs, total = refs[:count], refs[count : -1 - ways], refs[-1 - ways : -1], refs[-1]
    _, _, rows, _ = total.shape
    if count == 3:
        total[0:1] = owns[0][...].reshape(1, ways, rows, C)

        @pl.when(place_ref[1] < SECTIONS // 2)
        def _():
            total[1:2] = owns[1][...].reshape(1, ways, rows, C)

        @pl.when(place_ref[1] >= SECTIONS // 2)
        def _():
            total[1:2] = owns[2][...].reshape(1, ways, rows, C)
    else:
        value = owns[0][...].astype(F32)
        for more in arrived:
            value = value + more[...].astype(F32)
        total[...] = value.reshape(total.shape)
    here = spot(place_ref[0])
    outs[0][...] = total[:, here]
    for step in range(1, ways):
        outs[step][...] = total[:, (here + step) % ways].astype(BF)


def split(place, owns, arrived, pair, rows, ways, spot):
    return pl.pallas_call(
        lambda *refs: split_kernel(ways, spot, len(owns), *refs),
        out_shape=[jax.ShapeDtypeStruct((pair, rows, C), F32)]
        + [jax.ShapeDtypeStruct((pair, rows, C), BF)] * (ways - 1),
        in_specs=[SMEM] + [VMEM] * (len(owns) + len(arrived)),
        out_specs=[VMEM] * ways,
        scratch_shapes=[pltpu.VMEM((pair, ways, rows, C), F32)],
        compiler_params=pltpu.CompilerParams(vmem_limit_bytes=8 << 20),
        name="split",
    )(place, *owns, *arrived)


def join_kernel(ways, spot, place_ref, *refs):
    here = spot(place_ref[0])
    out = refs[-1]
    for step in range(ways):
        out[:, (here - step + ways) % ways] = refs[step][...]


def join(place, pieces, spot):
    ways = len(pieces)
    pair, rows, _ = pieces[0].shape
    joined = pl.pallas_call(
        lambda *refs: join_kernel(ways, spot, *refs),
        out_shape=jax.ShapeDtypeStruct((pair, ways, rows, C), BF),
        in_specs=[SMEM] + [VMEM] * ways,
        out_specs=VMEM,
        compiler_params=pltpu.CompilerParams(vmem_limit_bytes=8 << 20),
        name="join",
    )(place, *pieces)
    return joined.reshape(pair, ways * rows, C)


def sum_kernel(*refs):
    value = refs[0][...]
    for ref in refs[1:-1]:
        value = value + ref[...].astype(F32)
    refs[-1][...] = value.astype(refs[-1].dtype)


def added(dtype, *args):
    return pl.pallas_call(
        sum_kernel,
        out_shape=jax.ShapeDtypeStruct(args[0].shape, dtype),
        in_specs=[VMEM] * len(args),
        out_specs=VMEM,
        compiler_params=pltpu.CompilerParams(vmem_limit_bytes=8 << 20),
        name="added",
    )(*args)


def y_of(place):
    return (place // 2) % 4


def z_high(place):
    return place // 16


def z_low(place):
    return (place // 8) % 2


def core_step(place, step):
    return place ^ 1


def y_step(place, step):
    return (place // 8) * 8 + ((place // 2 + step) % 4) * 2 + place % 2


def z_high_step(place, step):
    return (place + 16 * step) % SPACE


def z_low_step(place, step):
    return place ^ 8


def send(array, move, step, group=range(SECTIONS)):
    pairs = [
        (section * SPACE + place, section * SPACE + move(place, step))
        for section in group
        for place in range(SPACE)
    ]
    return lax.ppermute(array, GRID_AXES, pairs)


def first_phases(place, terms, group=range(SECTIONS)):
    keep, given = weight_terms(place, group, *terms)
    arrived = [send(given, core_step, 1, group)]
    pieces = split(place, [keep], arrived, 1, PART, PARTS, y_of)
    arrived = [send(pieces[step], y_step, step, group) for step in (2, 1, 3)]
    return added(F32, pieces[0], *arrived)


def last_phases(place, totals):
    pieces = split(place, totals, [], 2, 2 * PIECE, 4, z_high)
    arrived = [send(pieces[step], z_high_step, step) for step in (2, 1, 3)]
    own = added(F32, pieces[0], *arrived)
    pieces = split(place, [own], [], 2, PIECE, 2, z_low)
    whole = added(BF, pieces[0], send(pieces[1], z_low_step, 1))
    whole = join(place, [whole, send(whole, z_low_step, 1)], z_low)
    moved = {step: send(whole, z_high_step, step) for step in (2, 1, 3)}
    own = join_pair(place, [whole] + [moved[step] for step in range(1, 4)])
    behind = [send(part, y_step, 1) for part in own]
    ahead = [send(part, y_step, 3) for part in own]
    across = [send(behind[0], y_step, 1), send(ahead[1], y_step, 3)]
    return [
        join_y(place, [own[half], behind[half], across[half], ahead[half]]) for half in range(2)
    ]


def join_pair_kernel(place_ref, *refs):
    here = z_high(place_ref[0])
    outs = refs[4:]
    for step in range(4):
        for half in range(2):
            outs[half][(here - step + 4) % 4] = refs[step][half]


def join_pair(place, pieces):
    rows = pieces[0].shape[1]
    shape = jax.ShapeDtypeStruct((4, rows, C), BF)
    joined = pl.pallas_call(
        join_pair_kernel,
        out_shape=[shape, shape],
        in_specs=[SMEM] + [VMEM] * 4,
        out_specs=[VMEM] * 2,
        compiler_params=pltpu.CompilerParams(vmem_limit_bytes=8 << 20),
        name="join_pair",
    )(place, *pieces)
    return [part.reshape(4 * rows, C) for part in joined]


def join_y_kernel(place_ref, *refs):
    here = y_of(place_ref[0])
    for step in range(4):
        refs[4][(here - step + 4) % 4] = refs[step][...]


def join_y(place, pieces):
    return pl.pallas_call(
        join_y_kernel,
        out_shape=jax.ShapeDtypeStruct((PARTS, PART, C), BF),
        in_specs=[SMEM] + [VMEM] * 4,
        out_specs=VMEM,
        compiler_params=pltpu.CompilerParams(vmem_limit_bytes=8 << 20),
        name="join_y",
    )(place, *pieces)


def unpack_kernel(place_ref, enc_ref, dec_ref, *refs):
    weight_ref, bias_ref = refs[-2:]

    def write(ref):
        def one(index, carry):
            part, a = index // 3, index % 3
            rows = pl.ds(pl.multiple_of(part * (C // PARTS), C // PARTS), C // PARTS)
            for j in range(9):
                row = pl.multiple_of((9 * a + j) * (C // PARTS), C // PARTS)
                weight_ref[0, a, rows, j * C : (j + 1) * C] = ref[
                    part, pl.ds(row, C // PARTS), :
                ].astype(F32)
            return carry

        lax.fori_loop(0, 3 * PARTS, one, 0)
        bias_ref[0] = ref[0, USED : USED + 16, :].astype(F32)[0:1]

    encoder = pl.program_id(0) == 0
    pl.when(encoder)(lambda: write(enc_ref))
    pl.when(jnp.logical_not(encoder))(lambda: write(dec_ref))


def unpack(place, flip, parts, onto=()):
    def spot(block, place_ref):
        return 2 * block + (place_ref[0] + flip) % 2

    return pl.pallas_call(
        lambda *refs: unpack_kernel(*refs),
        out_shape=[
            jax.ShapeDtypeStruct((4, 3, C, 9 * C), F32),
            jax.ShapeDtypeStruct((4, 1, C), F32),
        ],
        grid_spec=pltpu.PrefetchScalarGridSpec(
            num_scalar_prefetch=1,
            grid=(2,),
            in_specs=[VMEM] * 2 + [ANY] * len(onto),
            out_specs=[
                pl.BlockSpec((1, 3, C, 9 * C), lambda *at: (spot(*at), 0, 0, 0)),
                pl.BlockSpec((1, 1, C), lambda *at: (spot(*at), 0, 0)),
            ],
        ),
        input_output_aliases={3 + index: index for index in range(len(onto))},
        compiler_params=pltpu.CompilerParams(vmem_limit_bytes=16 << 20),
        name="unpack",
    )(place, *parts, *onto)


def to_cells(block):
    return block.transpose(1, 3, 2, 0).reshape(CELLS, W)


def from_cells(field):
    return field.reshape(ROWS, Z, Y, C).transpose(3, 0, 2, 1)[None, None]


def whole_pass(encoder_inputs, upper_inputs, output_cotangent, weights, biases):
    section = lax.axis_index("section")
    space = lax.axis_index("space")
    place = jnp.stack([space, section]).astype(jnp.int32)
    kernels = weights[0]
    bias_rows = jnp.concatenate([biases[0], biases[0]], axis=1)
    enc = to_cells(encoder_inputs[0, 0])
    far_left = beside(enc[CELLS - 2 * Z :], 2)
    far_right = beside(enc[: 2 * Z], -2)
    left = beside(enc, 1)
    right = beside(enc, -1)
    rest = jnp.concatenate([to_cells(upper_inputs[0, 0]), to_cells(output_cotangent[0])], axis=0)
    rest_left = beside(rest, 1)
    rest_right = beside(rest, -1)
    enc_v, enc_h, enc_s1, enc_s2, enc_out = forward(
        encode_kernel, [sds(12, BF)],
        place, kernels, bias_rows, far_left, left, enc, right, far_right,
    )
    dec_v, dec_h, dec_s1, dec_s2 = forward(
        decode_kernel, [],
        place, kernels, bias_rows, enc_out, rest_left, rest, rest_right,
    )
    cot = (
        rest_left[2 * CELLS - 2 * Z :],
        rest[CELLS:],
        rest_right[CELLS : CELLS + 2 * Z],
    )
    slopes = (dec_s1, dec_s2)
    state = tick(2, None, place, kernels, slopes, cot)
    near = far = None
    for turn in range(1, SECTIONS):
        cot = hand_on(state, turn - 1, 1)
        if turn == 3:
            near = first_phases(place, (state[1], dec_v, state[0], dec_h), range(0, 2))
        state = tick(2, turn, place, kernels, slopes, cot, state=state)
    upper = state
    skip = (beside(upper[4], 1), upper[2], beside(upper[3], -1))
    slopes = (enc_s1, enc_s2)
    state = tick(0, None, place, kernels, slopes, skip)
    for turn in range(SECTIONS - 2, -1, -1):
        cot = hand_on(state, turn + 1, -1)
        if turn == 1:
            far = first_phases(place, (upper[1], dec_v, upper[0], dec_h), range(2, 4))
        state = tick(0, turn, place, kernels, slopes, cot, skip=skip, state=state)
    enc_total = first_phases(place, (state[1], enc_v, state[0], enc_h))
    mine = last_phases(place, [enc_total, near, far])
    other = [send(part, core_step, 1) for part in mine]
    totals = unpack(place, 0, mine)
    weight_total, bias_total = unpack(place, 1, other, totals)
    return (
        from_cells(state[2]),
        from_cells(upper[2]),
        weight_total[None],
        bias_total.reshape(1, 4, C),
    )


def solution(mesh):
    return jax.shard_map(
        whole_pass,
        mesh=mesh,
        in_specs=(
            P("section", None, None, "space", None, None),
            P("section", None, None, "space", None, None),
            P(None, None, "space", None, None),
            P("section", None, None, None, None),
            P("section", None, None),
        ),
        out_specs=(
            P("section", None, None, "space", None, None),
            P("section", None, None, "space", None, None),
            P("section", None, None, None, None),
            P("section", None, None),
        ),
        check_vma=False,
    )
```

profile of v0, /device:TPU:2, one launch (start us, length us, event | category | flops | bytes accessed | tf_op | source)
XLA Modules:
  0.0 291.5 jit_solution(9849997691596720309)
XLA Ops:
  3.0 3.0 %collective-permute-start.1 = (bf16[256,256]{1,0:T(8,128)(2,1)S(1)}, bf16[256,256]{1,0:T(8,128)(2,1)S(1)}, u32[]{:S(2)}, u32[]{:S(2)}) collective-permute-start(bf16[256,256]{1,0:T(8,128)(2,1)S(1)} %bitcast.65), channel_id=1, source_target_pairs={{0,1},{1,2},{2,3},{3,4},{4,5},{5,6},{6,7},{7,8},{8,9},{9,10},{10,1... | collective-permute-start | bytes 393224 | tf_op jit(solution)/shard_map/ppermute | solution.py:226
  7.0 16.7 %collective-permute-start = (bf16[128,256]{1,0:T(8,128)(2,1)S(1)}, bf16[128,256]{1,0:T(8,128)(2,1)S(1)}, u32[]{:S(2)}, u32[]{:S(2)}) collective-permute-start(bf16[128,256]{1,0:T(8,128)(2,1)S(1)} %bitcast.91), channel_id=1, source_target_pairs={{0,2},{1,3},{2,4},{3,5},{4,6},{5,7},{6,8},{7,9},{8,10},{9,11},{10,... | collective-permute-start | bytes 196616 | tf_op jit(solution)/shard_map/ppermute | solution.py:226
  23.8 12.5 %collective-permute-start.3 = (bf16[128,256]{1,0:T(8,128)(2,1)S(1)}, bf16[128,256]{1,0:T(8,128)(2,1)S(1)}, u32[]{:S(2)}, u32[]{:S(2)}) collective-permute-start(bf16[128,256]{1,0:T(8,128)(2,1)S(1)} %bitcast.92), channel_id=1, source_target_pairs={{2,0},{3,1},{4,2},{5,3},{6,4},{7,5},{8,6},{9,7},{10,8},{11,9},{12,... | collective-permute-start | bytes 196616 | tf_op jit(solution)/shard_map/ppermute | solution.py:226
  38.5 13.1 %collective-permute-start.5 = (bf16[512,256]{1,0:T(8,128)(2,1)S(1)}, bf16[512,256]{1,0:T(8,128)(2,1)S(1)}, u32[]{:S(2)}, u32[]{:S(2)}) collective-permute-start(bf16[512,256]{1,0:T(8,128)(2,1)S(1)} %constant_dynamic-update-slice_fusion.own), channel_id=1, source_target_pairs={{1,0},{2,1},{3,2},{4,3},{5,4},{6,5},{7,6},{8,7},{9,8},{10,9},{11,1... | collective-permute-start | bytes 786440 | tf_op jit(solution)/shard_map/ppermute | solution.py:226
  52.5 13.8 %collective-permute-start.4 = (bf16[512,256]{1,0:T(8,128)(2,1)S(1)}, bf16[512,256]{1,0:T(8,128)(2,1)S(1)}, u32[]{:S(2)}, u32[]{:S(2)}) collective-permute-start(bf16[512,256]{1,0:T(8,128)(2,1)S(1)} %constant_dynamic-update-slice_fusion.own), channel_id=1, source_target_pairs={{0,1},{1,2},{2,3},{3,4},{4,5},{5,6},{6,7},{7,8},{8,9},{9,10},{10,1... | collective-permute-start | bytes 786440 | tf_op jit(solution)/shard_map/ppermute | solution.py:226
  66.3 2.0 copy-done
  68.3 4.7 %shard_map.84 = (bf16[384,256]{1,0:T(8,128)(2,1)S(1)}, bf16[384,256]{1,0:T(8,128)(2,1)S(1)}, f32[384,256]{1,0:T(8,128)S(1)}, f32[512,256]{1,0:T(8,128)S(1)}, bf16[768,256]{1,0:T(8,128)(2,1)S(1)}) custom-call(s32[2]{0:T(128)S(1)} %pad_add_fusion.place_ref.refs_0_, bf16[4,3,128,1152]{3,2,1,0:T(8,128)(2,1)S(1)} %bitcast.68, ...), custom_call_target="tpu_custom_call" | custom-call | flops 3000000000 | bytes 5242880 | tf_op jit(solution)/shard_map/pallas_call | solution.py:128
  73.0 3.6 %shard_map.85 = (bf16[384,256]{1,0:T(8,128)(2,1)S(1)}, bf16[384,256]{1,0:T(8,128)(2,1)S(1)}, f32[384,256]{1,0:T(8,128)S(1)}, f32[512,256]{1,0:T(8,128)S(1)}) custom-call(s32[2]{0:T(128)S(1)} %pad_add_fusion.place_ref.refs_0_, bf16[4,3,128,1152]{3,2,1,0:T(8,128)(2,1)S(1)} %bitcast.69, f32[4,256]{1,0:T(4,128)S(1)} %pad_maximum_fusion.bias_ref, ...), custom_call_target="tpu_custom_call" | custom-call | flops 3000000000 | bytes 5242880 | tf_op jit(solution)/shard_map/pallas_call | solution.py:128
  76.6 2.2 tick.8
  82.0 6.2 %collective-permute-done.8.refs_6_ = bf16[128,256]{1,0:T(8,128)(2,1)S(1)} collective-permute-done((bf16[128,256]{1,0:T(8,128)(2,1)S(1)}, bf16[128,256]{1,0:T(8,128)(2,1)S(1)}, u32[]{:S(2)}, u32[]{:S(2)}) %collective-permute-start.8) | collective-permute-done | bytes 65568 | tf_op jit(solution)/shard_map/ppermute | solution.py:220
  88.3 2.2 tick.9
  90.4 1.3 collective-permute-start.10
  93.7 2.6 collective-permute-done.9.refs_4_
  99.5 4.2 %collective-permute-start.15 = (bf16[128,256]{1,0:T(8,128)(2,1)S(1)}, bf16[128,256]{1,0:T(8,128)(2,1)S(1)}, u32[]{:S(2)}, u32[]{:S(2)}) collective-permute-start(bf16[128,256]{1,0:T(8,128)(2,1)S(1)} %get-tuple-element.101), channel_id=1, source_target_pairs={{0,1},{1,2},{2,3},{3,4},{4,5},{5,6},{6,7},{7,8},{8,9},{9,10},{10,1... | collective-permute-start | bytes 196616 | tf_op jit(solution)/shard_map/ppermute | solution.py:226
  105.0 2.8 collective-permute-done.16.refs_6_.refs_9_
  107.8 2.2 tick.12
  116.2 1.7 weights.4
  117.9 5.5 %collective-permute-start.30 = (bf16[4,896,128]{2,1,0:T(8,128)(2,1)S(1)}, bf16[4,896,128]{2,1,0:T(8,128)(2,1)S(1)}, u32[]{:S(2)}, u32[]{:S(2)}) collective-permute-start(bf16[4,896,128]{2,1,0:T(8,128)(2,1)S(1)} %get-tuple-element.133), channel_id=1, source_target_pairs={{0,1},{1,0},{2,3},{3,2},{4,5},{5,4},{6,7},{7,6},{8,9},{9,8},{10,11... | collective-permute-start | bytes 2752520 | tf_op jit(solution)/shard_map/ppermute | solution.py:393
  123.4 16.3 %collective-permute-done.22.refs_6_ = bf16[128,256]{1,0:T(8,128)(2,1)S(1)} collective-permute-done((bf16[128,256]{1,0:T(8,128)(2,1)S(1)}, bf16[128,256]{1,0:T(8,128)(2,1)S(1)}, u32[]{:S(2)}, u32[]{:S(2)}) %collective-permute-start.22) | collective-permute-done | bytes 65568 | tf_op jit(solution)/shard_map/ppermute | solution.py:220
  140.9 2.2 tick.14
  147.7 2.1 collective-permute-done.24.refs_5_
  151.0 1.7 weights.3
  154.4 6.8 %collective-permute-start.31 = (bf16[1,896,128]{2,1,0:T(8,128)(2,1)S(1)}, bf16[1,896,128]{2,1,0:T(8,128)(2,1)S(1)}, u32[]{:S(2)}, u32[]{:S(2)}) collective-permute-start(bf16[1,896,128]{2,1,0:T(8,128)(2,1)S(1)} %get-tuple-element.135), channel_id=1, source_target_pairs={{0,4},{1,5},{2,6},{3,7},{4,0},{5,1},{6,2},{7,3},{8,12},{9,13},{10,... | collective-permute-start | bytes 688136 | tf_op jit(solution)/shard_map/ppermute | solution.py:393
  161.3 4.8 %collective-permute-start.32 = (bf16[1,896,128]{2,1,0:T(8,128)(2,1)S(1)}, bf16[1,896,128]{2,1,0:T(8,128)(2,1)S(1)}, u32[]{:S(2)}, u32[]{:S(2)}) collective-permute-start(bf16[1,896,128]{2,1,0:T(8,128)(2,1)S(1)} %get-tuple-element.136), channel_id=1, source_target_pairs={{0,2},{1,3},{2,4},{3,5},{4,6},{5,7},{6,0},{7,1},{8,10},{9,11},{10,... | collective-permute-start | bytes 688136 | tf_op jit(solution)/shard_map/ppermute | solution.py:393
  166.1 2.2 collective-permute-start.33
  172.3 14.5 %collective-permute-start.27 = (bf16[1,896,128]{2,1,0:T(8,128)(2,1)S(1)}, bf16[1,896,128]{2,1,0:T(8,128)(2,1)S(1)}, u32[]{:S(2)}, u32[]{:S(2)}) collective-permute-start(bf16[1,896,128]{2,1,0:T(8,128)(2,1)S(1)} %get-tuple-element.127), channel_id=1, source_target_pairs={{0,4},{1,5},{2,6},{3,7},{4,0},{5,1},{6,2},{7,3},{8,12},{9,13},{10,... | collective-permute-start | bytes 688136 | tf_op jit(solution)/shard_map/ppermute | solution.py:393
  186.8 1.5 collective-permute-start.28
  188.3 1.8 collective-permute-start.29
  190.3 6.0 %collective-permute-done.27.refs_1_ = bf16[1,896,128]{2,1,0:T(8,128)(2,1)S(1)} collective-permute-done((bf16[1,896,128]{2,1,0:T(8,128)(2,1)S(1)}, bf16[1,896,128]{2,1,0:T(8,128)(2,1)S(1)}, u32[]{:S(2)}, u32[]{:S(2)}) %collective-permute-start.27) | collective-permute-done | bytes 229408 | tf_op jit(solution)/shard_map/ppermute | solution.py:393
  196.3 4.3 %collective-permute-done.28.refs_2_ = bf16[1,896,128]{2,1,0:T(8,128)(2,1)S(1)} collective-permute-done((bf16[1,896,128]{2,1,0:T(8,128)(2,1)S(1)}, bf16[1,896,128]{2,1,0:T(8,128)(2,1)S(1)}, u32[]{:S(2)}, u32[]{:S(2)}) %collective-permute-start.28) | collective-permute-done | bytes 229408 | tf_op jit(solution)/shard_map/ppermute | solution.py:393
  201.4 6.6 %collective-permute-start.38 = (bf16[2,224,128]{2,1,0:T(8,128)(2,1)S(1)}, bf16[2,224,128]{2,1,0:T(8,128)(2,1)S(1)}, u32[]{:S(2)}, u32[]{:S(2)}) collective-permute-start(bf16[2,224,128]{2,1,0:T(8,128)(2,1)S(1)} %get-tuple-element.147), channel_id=1, source_target_pairs={{0,32},{1,33},{2,34},{3,35},{4,36},{5,37},{6,38},{7,39},{8,40},{9,... | collective-permute-start | bytes 344072 | tf_op jit(solution)/shard_map/ppermute | solution.py:393
  209.1 3.0 %collective-permute-start.40 = (bf16[2,224,128]{2,1,0:T(8,128)(2,1)S(1)}, bf16[2,224,128]{2,1,0:T(8,128)(2,1)S(1)}, u32[]{:S(2)}, u32[]{:S(2)}) collective-permute-start(bf16[2,224,128]{2,1,0:T(8,128)(2,1)S(1)} %get-tuple-element.149), channel_id=1, source_target_pairs={{0,48},{1,49},{2,50},{3,51},{4,52},{5,53},{6,54},{7,55},{8,56},{9,... | collective-permute-start | bytes 344072 | tf_op jit(solution)/shard_map/ppermute | solution.py:393
  212.1 2.1 collective-permute-done.38.refs_1_
  214.2 3.7 %collective-permute-done.39.refs_2_ = bf16[2,224,128]{2,1,0:T(8,128)(2,1)S(1)} collective-permute-done((bf16[2,224,128]{2,1,0:T(8,128)(2,1)S(1)}, bf16[2,224,128]{2,1,0:T(8,128)(2,1)S(1)}, u32[]{:S(2)}, u32[]{:S(2)}) %collective-permute-start.39) | collective-permute-done | bytes 114720 | tf_op jit(solution)/shard_map/ppermute | solution.py:393
  220.6 3.4 %collective-permute-done.41.refs_1_ = bf16[2,112,128]{2,1,0:T(8,128)(2,1)S(1)} collective-permute-done((bf16[2,112,128]{2,1,0:T(8,128)(2,1)S(1)}, bf16[2,112,128]{2,1,0:T(8,128)(2,1)S(1)}, u32[]{:S(2)}, u32[]{:S(2)}) %collective-permute-start.41) | collective-permute-done | bytes 57376 | tf_op jit(solution)/shard_map/ppermute | solution.py:393
  224.8 3.4 %collective-permute-done.42.refs_2_ = bf16[2,112,128]{2,1,0:T(8,128)(2,1)S(1)} collective-permute-done((bf16[2,112,128]{2,1,0:T(8,128)(2,1)S(1)}, bf16[2,112,128]{2,1,0:T(8,128)(2,1)S(1)}, u32[]{:S(2)}, u32[]{:S(2)}) %collective-permute-start.42) | collective-permute-done | bytes 57376 | tf_op jit(solution)/shard_map/ppermute | solution.py:393
  228.8 3.8 %collective-permute-start.45 = (bf16[2,224,128]{2,1,0:T(8,128)(2,1)S(1)}, bf16[2,224,128]{2,1,0:T(8,128)(2,1)S(1)}, u32[]{:S(2)}, u32[]{:S(2)}) collective-permute-start(bf16[2,224,128]{2,1,0:T(8,128)(2,1)S(1)} %bitcast.54), channel_id=1, source_target_pairs={{0,48},{1,49},{2,50},{3,51},{4,52},{5,53},{6,54},{7,55},{8,56},{9,... | collective-permute-start | bytes 344072 | tf_op jit(solution)/shard_map/ppermute | solution.py:393
  232.6 1.7 collective-permute-start.44
  235.1 2.0 collective-permute-done.45.refs_3_
  237.1 6.4 %collective-permute-done.44.refs_2_ = bf16[2,224,128]{2,1,0:T(8,128)(2,1)S(1)} collective-permute-done((bf16[2,224,128]{2,1,0:T(8,128)(2,1)S(1)}, bf16[2,224,128]{2,1,0:T(8,128)(2,1)S(1)}, u32[]{:S(2)}, u32[]{:S(2)}) %collective-permute-start.44) | collective-permute-done | bytes 114720 | tf_op jit(solution)/shard_map/ppermute | solution.py:393
  245.2 2.3 collective-permute-start.51
  247.6 4.2 %collective-permute-done.46.refs_1_ = bf16[896,128]{1,0:T(8,128)(2,1)S(1)} collective-permute-done((bf16[896,128]{1,0:T(8,128)(2,1)S(1)}, bf16[896,128]{1,0:T(8,128)(2,1)S(1)}, u32[]{:S(2)}, u32[]{:S(2)}) %collective-permute-start.46) | collective-permute-done | bytes 229408 | tf_op jit(solution)/shard_map/ppermute | solution.py:393
  252.1 10.1 %collective-permute-start.50 = (bf16[896,128]{1,0:T(8,128)(2,1)S(1)}, bf16[896,128]{1,0:T(8,128)(2,1)S(1)}, u32[]{:S(2)}, u32[]{:S(2)}) collective-permute-start(bf16[896,128]{1,0:T(8,128)(2,1)S(1)} %bitcast.59), channel_id=1, source_target_pairs={{0,2},{1,3},{2,4},{3,5},{4,6},{5,7},{6,0},{7,1},{8,10},{9,11},{10,... | collective-permute-start | bytes 688136 | tf_op jit(solution)/shard_map/ppermute | solution.py:393
  262.2 2.7 collective-permute-start.52
  265.7 5.1 %collective-permute-done.50.refs_1_ = bf16[896,128]{1,0:T(8,128)(2,1)S(1)} collective-permute-done((bf16[896,128]{1,0:T(8,128)(2,1)S(1)}, bf16[896,128]{1,0:T(8,128)(2,1)S(1)}, u32[]{:S(2)}, u32[]{:S(2)}) %collective-permute-start.50) | collective-permute-done | bytes 229408 | tf_op jit(solution)/shard_map/ppermute | solution.py:393
  271.5 11.9 %collective-permute-start.53 = (bf16[4,896,128]{2,1,0:T(8,128)(2,1)S(1)}, bf16[4,896,128]{2,1,0:T(8,128)(2,1)}, u32[]{:S(2)}, u32[]{:S(2)}) collective-permute-start(bf16[4,896,128]{2,1,0:T(8,128)(2,1)S(1)} %join_y.3.refs_2_), channel_id=1, source_target_pairs={{0,1},{1,0},{2,3},{3,2},{4,5},{5,4},{6,7},{7,6},{8,9},{9,8},{10,11... | collective-permute-start | bytes 2752520 | tf_op jit(solution)/shard_map/ppermute | solution.py:393
  284.8 2.7 unpack.2
  287.6 3.9 %unpack.3 = (f32[4,3,128,1152]{3,2,1,0:T(8,128)}, f32[4,1,128]{2,1,0:T(1,128)}) custom-call(s32[2]{0:T(128)S(1)} %pad_add_fusion.place_ref.refs_0_, bf16[4,896,128]{2,1,0:T(8,128)(2,1)S(1)} %collective-permute-done.49.refs_1_, bf16[4,896,128]{2,1,0:T(8,128)(2,1)} %collective-permute-done.53.refs_2_, ...), custom_call_target="tpu_custom_call", output_to_operand_aliasing={{0}: (3, {}), {1}: (4, {})} | custom-call | tf_op jit(solution)/shard_map/unpack/pallas_call | solution.py:486
  (113 shorter events, 46.6 us)
Async XLA Ops:
  1.7 64.5 %collective-permute-start.2 = (bf16[256,256]{1,0:T(8,128)(2,1)S(1)}, bf16[256,256]{1,0:T(8,128)(2,1)S(1)}, u32[]{:S(2)}, u32[]{:S(2)}) collective-permute-start(bf16[256,256]{1,0:T(8,128)(2,1)S(1)} %bitcast.64), channel_id=1, source_target_pairs={{1,0},{2,1},{3,2},{4,3},{5,4},{6,5},{7,6},{8,7},{9,8},{10,9},{11,1... | collective-permute-start | bytes 393224 | tf_op jit(solution)/shard_map/ppermute | solution.py:226
  3.0 63.3 %collective-permute-start.1 = (bf16[256,256]{1,0:T(8,128)(2,1)S(1)}, bf16[256,256]{1,0:T(8,128)(2,1)S(1)}, u32[]{:S(2)}, u32[]{:S(2)}) collective-permute-start(bf16[256,256]{1,0:T(8,128)(2,1)S(1)} %bitcast.65), channel_id=1, source_target_pairs={{0,1},{1,2},{2,3},{3,4},{4,5},{5,6},{6,7},{7,8},{8,9},{9,10},{10,1... | collective-permute-start | bytes 393224 | tf_op jit(solution)/shard_map/ppermute | solution.py:226
  7.0 45.4 %collective-permute-start = (bf16[128,256]{1,0:T(8,128)(2,1)S(1)}, bf16[128,256]{1,0:T(8,128)(2,1)S(1)}, u32[]{:S(2)}, u32[]{:S(2)}) collective-permute-start(bf16[128,256]{1,0:T(8,128)(2,1)S(1)} %bitcast.91), channel_id=1, source_target_pairs={{0,2},{1,3},{2,4},{3,5},{4,6},{5,7},{6,8},{7,9},{8,10},{9,11},{10,... | collective-permute-start | bytes 196616 | tf_op jit(solution)/shard_map/ppermute | solution.py:226
  23.8 42.4 %collective-permute-start.3 = (bf16[128,256]{1,0:T(8,128)(2,1)S(1)}, bf16[128,256]{1,0:T(8,128)(2,1)S(1)}, u32[]{:S(2)}, u32[]{:S(2)}) collective-permute-start(bf16[128,256]{1,0:T(8,128)(2,1)S(1)} %bitcast.92), channel_id=1, source_target_pairs={{2,0},{3,1},{4,2},{5,3},{6,4},{7,5},{8,6},{9,7},{10,8},{11,9},{12,... | collective-permute-start | bytes 196616 | tf_op jit(solution)/shard_map/ppermute | solution.py:226
  38.5 34.5 %collective-permute-start.5 = (bf16[512,256]{1,0:T(8,128)(2,1)S(1)}, bf16[512,256]{1,0:T(8,128)(2,1)S(1)}, u32[]{:S(2)}, u32[]{:S(2)}) collective-permute-start(bf16[512,256]{1,0:T(8,128)(2,1)S(1)} %constant_dynamic-update-slice_fusion.own), channel_id=1, source_target_pairs={{1,0},{2,1},{3,2},{4,3},{5,4},{6,5},{7,6},{8,7},{9,8},{10,9},{11,1... | collective-permute-start | bytes 786440 | tf_op jit(solution)/shard_map/ppermute | solution.py:226
  52.5 20.5 %collective-permute-start.4 = (bf16[512,256]{1,0:T(8,128)(2,1)S(1)}, bf16[512,256]{1,0:T(8,128)(2,1)S(1)}, u32[]{:S(2)}, u32[]{:S(2)}) collective-permute-start(bf16[512,256]{1,0:T(8,128)(2,1)S(1)} %constant_dynamic-update-slice_fusion.own), channel_id=1, source_target_pairs={{0,1},{1,2},{2,3},{3,4},{4,5},{5,6},{6,7},{7,8},{8,9},{9,10},{10,1... | collective-permute-start | bytes 786440 | tf_op jit(solution)/shard_map/ppermute | solution.py:226
  78.7 9.5 %collective-permute-start.7 = (bf16[256,256]{1,0:T(8,128)(2,1)S(1)}, bf16[256,256]{1,0:T(8,128)(2,1)S(1)}, u32[]{:S(2)}, u32[]{:S(2)}) collective-permute-start(bf16[256,256]{1,0:T(8,128)(2,1)S(1)} %get-tuple-element.87.refs_9_), channel_id=1, source_target_pairs={{0,64},{1,65},{2,66},{3,67},{4,68},{5,69},{6,70},{7,71},{8,72},{9,... | collective-permute-start | bytes 393224 | tf_op jit(solution)/shard_map/ppermute | solution.py:218
  80.7 7.5 %collective-permute-start.8 = (bf16[128,256]{1,0:T(8,128)(2,1)S(1)}, bf16[128,256]{1,0:T(8,128)(2,1)S(1)}, u32[]{:S(2)}, u32[]{:S(2)}) collective-permute-start(bf16[128,256]{1,0:T(8,128)(2,1)S(1)} %get-tuple-element.88.refs_10_), channel_id=1, source_target_pairs={{1,64},{2,65},{3,66},{4,67},{5,68},{6,69},{7,70},{8,71},{9,72},{10... | collective-permute-start | bytes 196616 | tf_op jit(solution)/shard_map/ppermute | solution.py:220
  90.4 5.8 %collective-permute-start.10 = (bf16[256,256]{1,0:T(8,128)(2,1)S(1)}, bf16[256,256]{1,0:T(8,128)(2,1)S(1)}, u32[]{:S(2)}, u32[]{:S(2)}) collective-permute-start(bf16[256,256]{1,0:T(8,128)(2,1)S(1)} %get-tuple-element.92.refs_9_), channel_id=1, source_target_pairs={{64,128},{65,129},{66,130},{67,131},{68,132},{69,133},{70,134},{71... | collective-permute-start | bytes 393224 | tf_op jit(solution)/shard_map/ppermute | solution.py:218
  91.7 4.5 %collective-permute-start.9 = (bf16[128,256]{1,0:T(8,128)(2,1)S(1)}, bf16[128,256]{1,0:T(8,128)(2,1)S(1)}, u32[]{:S(2)}, u32[]{:S(2)}) collective-permute-start(bf16[128,256]{1,0:T(8,128)(2,1)S(1)} %get-tuple-element.91.refs_11_), channel_id=1, source_target_pairs={{64,129},{65,130},{66,131},{67,132},{68,133},{69,134},{70,135},{71... | collective-permute-start | bytes 196616 | tf_op jit(solution)/shard_map/ppermute | solution.py:219
  93.0 3.2 %collective-permute-start.11 = (bf16[128,256]{1,0:T(8,128)(2,1)S(1)}, bf16[128,256]{1,0:T(8,128)(2,1)S(1)}, u32[]{:S(2)}, u32[]{:S(2)}) collective-permute-start(bf16[128,256]{1,0:T(8,128)(2,1)S(1)} %get-tuple-element.93.refs_10_), channel_id=1, source_target_pairs={{65,128},{66,129},{67,130},{68,131},{69,132},{70,133},{71,134},{72... | collective-permute-start | bytes 196616 | tf_op jit(solution)/shard_map/ppermute | solution.py:220
  99.5 5.5 %collective-permute-start.15 = (bf16[128,256]{1,0:T(8,128)(2,1)S(1)}, bf16[128,256]{1,0:T(8,128)(2,1)S(1)}, u32[]{:S(2)}, u32[]{:S(2)}) collective-permute-start(bf16[128,256]{1,0:T(8,128)(2,1)S(1)} %get-tuple-element.101), channel_id=1, source_target_pairs={{0,1},{1,2},{2,3},{3,4},{4,5},{5,6},{6,7},{7,8},{8,9},{9,10},{10,1... | collective-permute-start | bytes 196616 | tf_op jit(solution)/shard_map/ppermute | solution.py:226
  103.7 4.1 %collective-permute-start.16 = (bf16[128,256]{1,0:T(8,128)(2,1)S(1)}, bf16[128,256]{1,0:T(8,128)(2,1)S(1)}, u32[]{:S(2)}, u32[]{:S(2)}) collective-permute-start(bf16[128,256]{1,0:T(8,128)(2,1)S(1)} %get-tuple-element.103), channel_id=1, source_target_pairs={{1,0},{2,1},{3,2},{4,3},{5,4},{6,5},{7,6},{8,7},{9,8},{10,9},{11,1... | collective-permute-start | bytes 196616 | tf_op jit(solution)/shard_map/ppermute | solution.py:226
  110.0 2.2 collective-permute-start.18
  112.8 10.6 %collective-permute-start.20 = (bf16[128,256]{1,0:T(8,128)(2,1)S(1)}, bf16[128,256]{1,0:T(8,128)(2,1)S(1)}, u32[]{:S(2)}, u32[]{:S(2)}) collective-permute-start(bf16[128,256]{1,0:T(8,128)(2,1)S(1)} %get-tuple-element.109.refs_14_), channel_id=1, source_target_pairs={{128,65},{129,66},{130,67},{131,68},{132,69},{133,70},{134,71},{13... | collective-permute-start | bytes 196616 | tf_op jit(solution)/shard_map/ppermute | solution.py:219
  113.6 26.1 %collective-permute-start.22 = (bf16[128,256]{1,0:T(8,128)(2,1)S(1)}, bf16[128,256]{1,0:T(8,128)(2,1)S(1)}, u32[]{:S(2)}, u32[]{:S(2)}) collective-permute-start(bf16[128,256]{1,0:T(8,128)(2,1)S(1)} %get-tuple-element.111.refs_13_), channel_id=1, source_target_pairs={{129,64},{130,65},{131,66},{132,67},{133,68},{134,69},{135,70},{13... | collective-permute-start | bytes 196616 | tf_op jit(solution)/shard_map/ppermute | solution.py:220
  114.9 26.0 %collective-permute-start.21 = (bf16[256,256]{1,0:T(8,128)(2,1)S(1)}, bf16[256,256]{1,0:T(8,128)(2,1)S(1)}, u32[]{:S(2)}, u32[]{:S(2)}) collective-permute-start(bf16[256,256]{1,0:T(8,128)(2,1)S(1)} %get-tuple-element.110.refs_12_), channel_id=1, source_target_pairs={{128,64},{129,65},{130,66},{131,67},{132,68},{133,69},{134,70},{13... | collective-permute-start | bytes 393224 | tf_op jit(solution)/shard_map/ppermute | solution.py:218
  117.9 35.5 %collective-permute-start.30 = (bf16[4,896,128]{2,1,0:T(8,128)(2,1)S(1)}, bf16[4,896,128]{2,1,0:T(8,128)(2,1)S(1)}, u32[]{:S(2)}, u32[]{:S(2)}) collective-permute-start(bf16[4,896,128]{2,1,0:T(8,128)(2,1)S(1)} %get-tuple-element.133), channel_id=1, source_target_pairs={{0,1},{1,0},{2,3},{3,2},{4,5},{5,4},{6,7},{7,6},{8,9},{9,8},{10,11... | collective-permute-start | bytes 2752520 | tf_op jit(solution)/shard_map/ppermute | solution.py:393
  143.1 4.6 %collective-permute-start.23 = (bf16[128,256]{1,0:T(8,128)(2,1)S(1)}, bf16[128,256]{1,0:T(8,128)(2,1)S(1)}, u32[]{:S(2)}, u32[]{:S(2)}) collective-permute-start(bf16[128,256]{1,0:T(8,128)(2,1)S(1)} %get-tuple-element.114.refs_14_), channel_id=1, source_target_pairs={{64,1},{65,2},{66,3},{67,4},{68,5},{69,6},{70,7},{71,8},{72,9},{73... | collective-permute-start | bytes 196616 | tf_op jit(solution)/shard_map/ppermute | solution.py:219
  144.4 3.3 %collective-permute-start.25 = (bf16[128,256]{1,0:T(8,128)(2,1)S(1)}, bf16[128,256]{1,0:T(8,128)(2,1)S(1)}, u32[]{:S(2)}, u32[]{:S(2)}) collective-permute-start(bf16[128,256]{1,0:T(8,128)(2,1)S(1)} %get-tuple-element.116.refs_13_), channel_id=1, source_target_pairs={{65,0},{66,1},{67,2},{68,3},{69,4},{70,5},{71,6},{72,7},{73,8},{74... | collective-permute-start | bytes 196616 | tf_op jit(solution)/shard_map/ppermute | solution.py:220
  145.1 4.7 %collective-permute-start.24 = (bf16[256,256]{1,0:T(8,128)(2,1)S(1)}, bf16[256,256]{1,0:T(8,128)(2,1)S(1)}, u32[]{:S(2)}, u32[]{:S(2)}) collective-permute-start(bf16[256,256]{1,0:T(8,128)(2,1)S(1)} %get-tuple-element.115.refs_12_), channel_id=1, source_target_pairs={{64,0},{65,1},{66,2},{67,3},{68,4},{69,5},{70,6},{71,7},{72,8},{73... | collective-permute-start | bytes 393224 | tf_op jit(solution)/shard_map/ppermute | solution.py:218
  146.9 21.4 %collective-permute-start.34 = (bf16[4,896,128]{2,1,0:T(8,128)(2,1)S(1)}, bf16[4,896,128]{2,1,0:T(8,128)(2,1)S(1)}, u32[]{:S(2)}, u32[]{:S(2)}) collective-permute-start(bf16[4,896,128]{2,1,0:T(8,128)(2,1)S(1)} %get-tuple-element.141), channel_id=1, source_target_pairs={{128,129},{129,128},{130,131},{131,130},{132,133},{133,132},{134,1... | collective-permute-start | bytes 2752520 | tf_op jit(solution)/shard_map/ppermute | solution.py:393
  152.8 17.2 %collective-permute-start.26 = (bf16[4,896,128]{2,1,0:T(8,128)(2,1)S(1)}, bf16[4,896,128]{2,1,0:T(8,128)(2,1)S(1)}, u32[]{:S(2)}, u32[]{:S(2)}) collective-permute-start(bf16[4,896,128]{2,1,0:T(8,128)(2,1)S(1)} %get-tuple-element.125), channel_id=1, source_target_pairs={{0,1},{1,0},{2,3},{3,2},{4,5},{5,4},{6,7},{7,6},{8,9},{9,8},{10,11... | collective-permute-start | bytes 2752520 | tf_op jit(solution)/shard_map/ppermute | solution.py:393
  154.4 17.2 %collective-permute-start.31 = (bf16[1,896,128]{2,1,0:T(8,128)(2,1)S(1)}, bf16[1,896,128]{2,1,0:T(8,128)(2,1)S(1)}, u32[]{:S(2)}, u32[]{:S(2)}) collective-permute-start(bf16[1,896,128]{2,1,0:T(8,128)(2,1)S(1)} %get-tuple-element.135), channel_id=1, source_target_pairs={{0,4},{1,5},{2,6},{3,7},{4,0},{5,1},{6,2},{7,3},{8,12},{9,13},{10,... | collective-permute-start | bytes 688136 | tf_op jit(solution)/shard_map/ppermute | solution.py:393
  161.3 11.0 %collective-permute-start.32 = (bf16[1,896,128]{2,1,0:T(8,128)(2,1)S(1)}, bf16[1,896,128]{2,1,0:T(8,128)(2,1)S(1)}, u32[]{:S(2)}, u32[]{:S(2)}) collective-permute-start(bf16[1,896,128]{2,1,0:T(8,128)(2,1)S(1)} %get-tuple-element.136), channel_id=1, source_target_pairs={{0,2},{1,3},{2,4},{3,5},{4,6},{5,7},{6,0},{7,1},{8,10},{9,11},{10,... | collective-permute-start | bytes 688136 | tf_op jit(solution)/shard_map/ppermute | solution.py:393
  166.1 20.7 %collective-permute-start.33 = (bf16[1,896,128]{2,1,0:T(8,128)(2,1)S(1)}, bf16[1,896,128]{2,1,0:T(8,128)(2,1)S(1)}, u32[]{:S(2)}, u32[]{:S(2)}) collective-permute-start(bf16[1,896,128]{2,1,0:T(8,128)(2,1)S(1)} %get-tuple-element.137), channel_id=1, source_target_pairs={{0,6},{1,7},{2,0},{3,1},{4,2},{5,3},{6,4},{7,5},{8,14},{9,15},{10,... | collective-permute-start | bytes 688136 | tf_op jit(solution)/shard_map/ppermute | solution.py:393
  169.3 19.0 %collective-permute-start.35 = (bf16[1,896,128]{2,1,0:T(8,128)(2,1)S(1)}, bf16[1,896,128]{2,1,0:T(8,128)(2,1)S(1)}, u32[]{:S(2)}, u32[]{:S(2)}) collective-permute-start(bf16[1,896,128]{2,1,0:T(8,128)(2,1)S(1)} %get-tuple-element.143), channel_id=1, source_target_pairs={{128,132},{129,133},{130,134},{131,135},{132,128},{133,129},{134,1... | collective-permute-start | bytes 688136 | tf_op jit(solution)/shard_map/ppermute | solution.py:393
  170.0 20.2 %collective-permute-start.36 = (bf16[1,896,128]{2,1,0:T(8,128)(2,1)S(1)}, bf16[1,896,128]{2,1,0:T(8,128)(2,1)S(1)}, u32[]{:S(2)}, u32[]{:S(2)}) collective-permute-start(bf16[1,896,128]{2,1,0:T(8,128)(2,1)S(1)} %get-tuple-element.144), channel_id=1, source_target_pairs={{128,130},{129,131},{130,132},{131,133},{132,134},{133,135},{134,1... | collective-permute-start | bytes 688136 | tf_op jit(solution)/shard_map/ppermute | solution.py:393
  171.6 18.6 %collective-permute-start.37 = (bf16[1,896,128]{2,1,0:T(8,128)(2,1)S(1)}, bf16[1,896,128]{2,1,0:T(8,128)(2,1)S(1)}, u32[]{:S(2)}, u32[]{:S(2)}) collective-permute-start(bf16[1,896,128]{2,1,0:T(8,128)(2,1)S(1)} %get-tuple-element.145), channel_id=1, source_target_pairs={{128,134},{129,135},{130,128},{131,129},{132,130},{133,131},{134,1... | collective-permute-start | bytes 688136 | tf_op jit(solution)/shard_map/ppermute | solution.py:393
  172.3 24.0 %collective-permute-start.27 = (bf16[1,896,128]{2,1,0:T(8,128)(2,1)S(1)}, bf16[1,896,128]{2,1,0:T(8,128)(2,1)S(1)}, u32[]{:S(2)}, u32[]{:S(2)}) collective-permute-start(bf16[1,896,128]{2,1,0:T(8,128)(2,1)S(1)} %get-tuple-element.127), channel_id=1, source_target_pairs={{0,4},{1,5},{2,6},{3,7},{4,0},{5,1},{6,2},{7,3},{8,12},{9,13},{10,... | collective-permute-start | bytes 688136 | tf_op jit(solution)/shard_map/ppermute | solution.py:393
  186.8 13.8 %collective-permute-start.28 = (bf16[1,896,128]{2,1,0:T(8,128)(2,1)S(1)}, bf16[1,896,128]{2,1,0:T(8,128)(2,1)S(1)}, u32[]{:S(2)}, u32[]{:S(2)}) collective-permute-start(bf16[1,896,128]{2,1,0:T(8,128)(2,1)S(1)} %get-tuple-element.128), channel_id=1, source_target_pairs={{0,2},{1,3},{2,4},{3,5},{4,6},{5,7},{6,0},{7,1},{8,10},{9,11},{10,... | collective-permute-start | bytes 688136 | tf_op jit(solution)/shard_map/ppermute | solution.py:393
  188.3 12.3 %collective-permute-start.29 = (bf16[1,896,128]{2,1,0:T(8,128)(2,1)S(1)}, bf16[1,896,128]{2,1,0:T(8,128)(2,1)S(1)}, u32[]{:S(2)}, u32[]{:S(2)}) collective-permute-start(bf16[1,896,128]{2,1,0:T(8,128)(2,1)S(1)} %get-tuple-element.129), channel_id=1, source_target_pairs={{0,6},{1,7},{2,0},{3,1},{4,2},{5,3},{6,4},{7,5},{8,14},{9,15},{10,... | collective-permute-start | bytes 688136 | tf_op jit(solution)/shard_map/ppermute | solution.py:393
  201.4 12.8 %collective-permute-start.38 = (bf16[2,224,128]{2,1,0:T(8,128)(2,1)S(1)}, bf16[2,224,128]{2,1,0:T(8,128)(2,1)S(1)}, u32[]{:S(2)}, u32[]{:S(2)}) collective-permute-start(bf16[2,224,128]{2,1,0:T(8,128)(2,1)S(1)} %get-tuple-element.147), channel_id=1, source_target_pairs={{0,32},{1,33},{2,34},{3,35},{4,36},{5,37},{6,38},{7,39},{8,40},{9,... | collective-permute-start | bytes 344072 | tf_op jit(solution)/shard_map/ppermute | solution.py:393
  208.0 10.0 %collective-permute-start.39 = (bf16[2,224,128]{2,1,0:T(8,128)(2,1)S(1)}, bf16[2,224,128]{2,1,0:T(8,128)(2,1)S(1)}, u32[]{:S(2)}, u32[]{:S(2)}) collective-permute-start(bf16[2,224,128]{2,1,0:T(8,128)(2,1)S(1)} %get-tuple-element.148), channel_id=1, source_target_pairs={{0,16},{1,17},{2,18},{3,19},{4,20},{5,21},{6,22},{7,23},{8,24},{9,... | collective-permute-start | bytes 344072 | tf_op jit(solution)/shard_map/ppermute | solution.py:393
  209.1 10.0 %collective-permute-start.40 = (bf16[2,224,128]{2,1,0:T(8,128)(2,1)S(1)}, bf16[2,224,128]{2,1,0:T(8,128)(2,1)S(1)}, u32[]{:S(2)}, u32[]{:S(2)}) collective-permute-start(bf16[2,224,128]{2,1,0:T(8,128)(2,1)S(1)} %get-tuple-element.149), channel_id=1, source_target_pairs={{0,48},{1,49},{2,50},{3,51},{4,52},{5,53},{6,54},{7,55},{8,56},{9,... | collective-permute-start | bytes 344072 | tf_op jit(solution)/shard_map/ppermute | solution.py:393
  219.7 4.3 %collective-permute-start.41 = (bf16[2,112,128]{2,1,0:T(8,128)(2,1)S(1)}, bf16[2,112,128]{2,1,0:T(8,128)(2,1)S(1)}, u32[]{:S(2)}, u32[]{:S(2)}) collective-permute-start(bf16[2,112,128]{2,1,0:T(8,128)(2,1)S(1)} %get-tuple-element.151), channel_id=1, source_target_pairs={{0,8},{1,9},{2,10},{3,11},{4,12},{5,13},{6,14},{7,15},{8,0},{9,1},... | collective-permute-start | bytes 172040 | tf_op jit(solution)/shard_map/ppermute | solution.py:393
  224.0 4.3 %collective-permute-start.42 = (bf16[2,112,128]{2,1,0:T(8,128)(2,1)S(1)}, bf16[2,112,128]{2,1,0:T(8,128)(2,1)S(1)}, u32[]{:S(2)}, u32[]{:S(2)}) collective-permute-start(bf16[2,112,128]{2,1,0:T(8,128)(2,1)S(1)} %added.9.refs_1_), channel_id=1, source_target_pairs={{0,8},{1,9},{2,10},{3,11},{4,12},{5,13},{6,14},{7,15},{8,0},{9,1},... | collective-permute-start | bytes 172040 | tf_op jit(solution)/shard_map/ppermute | solution.py:393
  228.8 8.2 %collective-permute-start.45 = (bf16[2,224,128]{2,1,0:T(8,128)(2,1)S(1)}, bf16[2,224,128]{2,1,0:T(8,128)(2,1)S(1)}, u32[]{:S(2)}, u32[]{:S(2)}) collective-permute-start(bf16[2,224,128]{2,1,0:T(8,128)(2,1)S(1)} %bitcast.54), channel_id=1, source_target_pairs={{0,48},{1,49},{2,50},{3,51},{4,52},{5,53},{6,54},{7,55},{8,56},{9,... | collective-permute-start | bytes 344072 | tf_op jit(solution)/shard_map/ppermute | solution.py:393
  232.6 10.9 %collective-permute-start.44 = (bf16[2,224,128]{2,1,0:T(8,128)(2,1)S(1)}, bf16[2,224,128]{2,1,0:T(8,128)(2,1)S(1)}, u32[]{:S(2)}, u32[]{:S(2)}) collective-permute-start(bf16[2,224,128]{2,1,0:T(8,128)(2,1)S(1)} %bitcast.55), channel_id=1, source_target_pairs={{0,32},{1,33},{2,34},{3,35},{4,36},{5,37},{6,38},{7,39},{8,40},{9,... | collective-permute-start | bytes 344072 | tf_op jit(solution)/shard_map/ppermute | solution.py:393
  234.3 9.2 %collective-permute-start.43 = (bf16[2,224,128]{2,1,0:T(8,128)(2,1)S(1)}, bf16[2,224,128]{2,1,0:T(8,128)(2,1)S(1)}, u32[]{:S(2)}, u32[]{:S(2)}) collective-permute-start(bf16[2,224,128]{2,1,0:T(8,128)(2,1)S(1)} %bitcast.56), channel_id=1, source_target_pairs={{0,16},{1,17},{2,18},{3,19},{4,20},{5,21},{6,22},{7,23},{8,24},{9,... | collective-permute-start | bytes 344072 | tf_op jit(solution)/shard_map/ppermute | solution.py:393
  244.2 7.6 %collective-permute-start.46 = (bf16[896,128]{1,0:T(8,128)(2,1)S(1)}, bf16[896,128]{1,0:T(8,128)(2,1)S(1)}, u32[]{:S(2)}, u32[]{:S(2)}) collective-permute-start(bf16[896,128]{1,0:T(8,128)(2,1)S(1)} %bitcast.61), channel_id=1, source_target_pairs={{0,2},{1,3},{2,4},{3,5},{4,6},{5,7},{6,0},{7,1},{8,10},{9,11},{10,... | collective-permute-start | bytes 688136 | tf_op jit(solution)/shard_map/ppermute | solution.py:393
  245.2 17.1 %collective-permute-start.51 = (bf16[896,128]{1,0:T(8,128)(2,1)S(1)}, bf16[896,128]{1,0:T(8,128)(2,1)S(1)}, u32[]{:S(2)}, u32[]{:S(2)}) collective-permute-start(bf16[896,128]{1,0:T(8,128)(2,1)S(1)} %bitcast.58), channel_id=1, source_target_pairs={{0,6},{1,7},{2,0},{3,1},{4,2},{5,3},{6,4},{7,5},{8,14},{9,15},{10,... | collective-permute-start | bytes 688136 | tf_op jit(solution)/shard_map/ppermute | solution.py:393
  247.5 17.5 %collective-permute-start.48 = (bf16[896,128]{1,0:T(8,128)(2,1)S(1)}, bf16[896,128]{1,0:T(8,128)(2,1)S(1)}, u32[]{:S(2)}, u32[]{:S(2)}) collective-permute-start(bf16[896,128]{1,0:T(8,128)(2,1)S(1)} %bitcast.62), channel_id=1, source_target_pairs={{0,6},{1,7},{2,0},{3,1},{4,2},{5,3},{6,4},{7,5},{8,14},{9,15},{10,... | collective-permute-start | bytes 688136 | tf_op jit(solution)/shard_map/ppermute | solution.py:393
  251.8 13.2 %collective-permute-start.47 = (bf16[896,128]{1,0:T(8,128)(2,1)S(1)}, bf16[896,128]{1,0:T(8,128)(2,1)S(1)}, u32[]{:S(2)}, u32[]{:S(2)}) collective-permute-start(bf16[896,128]{1,0:T(8,128)(2,1)S(1)} %collective-permute-done.46.refs_1_), channel_id=1, source_target_pairs={{0,2},{1,3},{2,4},{3,5},{4,6},{5,7},{6,0},{7,1},{8,10},{9,11},{10,... | collective-permute-start | bytes 688136 | tf_op jit(solution)/shard_map/ppermute | solution.py:393
  252.1 18.7 %collective-permute-start.50 = (bf16[896,128]{1,0:T(8,128)(2,1)S(1)}, bf16[896,128]{1,0:T(8,128)(2,1)S(1)}, u32[]{:S(2)}, u32[]{:S(2)}) collective-permute-start(bf16[896,128]{1,0:T(8,128)(2,1)S(1)} %bitcast.59), channel_id=1, source_target_pairs={{0,2},{1,3},{2,4},{3,5},{4,6},{5,7},{6,0},{7,1},{8,10},{9,11},{10,... | collective-permute-start | bytes 688136 | tf_op jit(solution)/shard_map/ppermute | solution.py:393
  262.2 8.6 %collective-permute-start.52 = (bf16[896,128]{1,0:T(8,128)(2,1)S(1)}, bf16[896,128]{1,0:T(8,128)(2,1)S(1)}, u32[]{:S(2)}, u32[]{:S(2)}) collective-permute-start(bf16[896,128]{1,0:T(8,128)(2,1)S(1)} %collective-permute-done.51.refs_3_), channel_id=1, source_target_pairs={{0,6},{1,7},{2,0},{3,1},{4,2},{5,3},{6,4},{7,5},{8,14},{9,15},{10,... | collective-permute-start | bytes 688136 | tf_op jit(solution)/shard_map/ppermute | solution.py:393
  265.6 21.9 %collective-permute-start.49 = (bf16[4,896,128]{2,1,0:T(8,128)(2,1)S(1)}, bf16[4,896,128]{2,1,0:T(8,128)(2,1)S(1)}, u32[]{:S(2)}, u32[]{:S(2)}) collective-permute-start(bf16[4,896,128]{2,1,0:T(8,128)(2,1)S(1)} %join_y.2.refs_1_), channel_id=1, source_target_pairs={{0,1},{1,0},{2,3},{3,2},{4,5},{5,4},{6,7},{7,6},{8,9},{9,8},{10,11... | collective-permute-start | bytes 2752520 | tf_op jit(solution)/shard_map/ppermute | solution.py:393
  271.5 16.1 %collective-permute-start.53 = (bf16[4,896,128]{2,1,0:T(8,128)(2,1)S(1)}, bf16[4,896,128]{2,1,0:T(8,128)(2,1)}, u32[]{:S(2)}, u32[]{:S(2)}) collective-permute-start(bf16[4,896,128]{2,1,0:T(8,128)(2,1)S(1)} %join_y.3.refs_2_), channel_id=1, source_target_pairs={{0,1},{1,0},{2,3},{3,2},{4,5},{5,4},{6,7},{7,6},{8,9},{9,8},{10,11... | collective-permute-start | bytes 2752520 | tf_op jit(solution)/shard_map/ppermute | solution.py:393
  (8 other events, 38.8 us)
where the time goes:
time: 293 us; the launch traced here: 291 us
  starting transfers between devices  171 us (58%)
  waiting for transfers between devices  73.1 us (25%)
  Pallas kernels  37.3 us (13%)
  local copies, waits for them, and re-layouts  7.68 us (3%)
    ppermute x28, starting transfers between devices, send(): return lax.ppermute(array, GRID_AXES, pairs)  88 us
    ppermute x8, starting transfers between devices, beside(): return lax.ppermute(array, 'space', pairs)  65.9 us
    ppermute x28, waiting for transfers between devices, send(): return lax.ppermute(array, GRID_AXES, pairs)  41.9 us
    ppermute x6, waiting for transfers between devices, hand_on(): after = lax.ppermute(low, GRID_AXES, shifted(source_section, by, -1))  22.5 us
    pallas_call x8, Pallas kernels, tick(): pl.pallas_call(lambda *refs: tick_kernel(layer, turn, seeded, *refs), out...  11.6 us
    pallas_call x2, Pallas kernels, forward(): pl.pallas_call(kernel, out_shape=[sds(6, BF), sds(6, BF), sds(6, F32), sd...  8.25 us
    ppermute x6, starting transfers between devices, hand_on(): middle = lax.ppermute(grad, GRID_AXES, shifted(source_section, by, 0))  6.7 us
    pallas_call x2, Pallas kernels, unpack(): pl.pallas_call(lambda *refs: unpack_kernel(*refs), out_shape=[jax.ShapeDt...  6.61 us
  transfers between devices with their start and end apart: 54, of which 18 were waited for; matrix products, arithmetic and copies ran while one was open for 2% of the time, Pallas kernels for 7%

commit v1 on v0

--- a/solution.py
+++ b/solution.py
@@ -226,15 +226,8 @@
     return lax.ppermute(array, "space", pairs)
 
 
-def weight_kernel(group, place_ref, *refs):
-    section = place_ref[1]
-
-    @pl.when((section >= group[0]) & (section <= group[-1]))
-    def _():
-        weight_body(place_ref[0] % 2, *refs)
-
-
-def weight_body(core, u1_ref, v1_ref, u2_ref, v2_ref, keep_ref, send_ref, held):
+def weight_kernel(place_ref, u1_ref, v1_ref, u2_ref, v2_ref, keep_ref, send_ref, held):
+    core = place_ref[0] % 2
     for layer, (u_ref, v_ref) in enumerate(((u1_ref, v1_ref), (u2_ref, v2_ref))):
         grads = u_ref[...]
         wide = grads.astype(F32)
@@ -266,10 +259,10 @@
     send_ref[...] = held[1 - core]
 
 
-def weight_terms(place, group, u1, v1, u2, v2):
+def weight_terms(place, u1, v1, u2, v2):
     shape = jax.ShapeDtypeStruct((PARTS, PART, C), BF)
     return pl.pallas_call(
-        lambda *refs: weight_kernel(group, *refs),
+        weight_kernel,
         out_shape=[shape, shape],
         in_specs=[SMEM] + [VMEM] * 4,
         out_specs=[VMEM] * 2,
@@ -282,22 +275,13 @@
 
 def split_kernel(ways, spot, count, place_ref, *refs):
     owns, arrived, outs, total = refs[:count], refs[count : -1 - ways], refs[-1 - ways : -1], refs[-1]
-    _, _, rows, _ = total.shape
-    if count == 3:
-        total[0:1] = owns[0][...].reshape(1, ways, rows, C)
-
-        @pl.when(place_ref[1] < SECTIONS // 2)
-        def _():
-            total[1:2] = owns[1][...].reshape(1, ways, rows, C)
-
-        @pl.when(place_ref[1] >= SECTIONS // 2)
-        def _():
-            total[1:2] = owns[2][...].reshape(1, ways, rows, C)
-    else:
-        value = owns[0][...].astype(F32)
+    pair, _, rows, _ = total.shape
+    for index, ref in enumerate(owns):
+        value = ref[...].astype(F32)
         for more in arrived:
             value = value + more[...].astype(F32)
-        total[...] = value.reshape(total.shape)
+        value = value.reshape(pair // count, ways, rows, C)
+        total[index * (pair // count) : (index + 1) * (pair // count)] = value
     here = spot(place_ref[0])
     outs[0][...] = total[:, here]
     for step in range(1, ways):
@@ -384,20 +368,15 @@
     return place ^ 8
 
 
-def send(array, move, step, group=range(SECTIONS)):
-    pairs = [
-        (section * SPACE + place, section * SPACE + move(place, step))
-        for section in group
-        for place in range(SPACE)
-    ]
-    return lax.ppermute(array, GRID_AXES, pairs)
-
-
-def first_phases(place, terms, group=range(SECTIONS)):
-    keep, given = weight_terms(place, group, *terms)
-    arrived = [send(given, core_step, 1, group)]
+def send(array, move, step):
+    return lax.ppermute(array, "space", [(place, move(place, step)) for place in range(SPACE)])
+
+
+def first_phases(place, terms):
+    keep, given = weight_terms(place, *terms)
+    arrived = [send(given, core_step, 1)]
     pieces = split(place, [keep], arrived, 1, PART, PARTS, y_of)
-    arrived = [send(pieces[step], y_step, step, group) for step in (2, 1, 3)]
+    arrived = [send(pieces[step], y_step, step) for step in (2, 1, 3)]
     return added(F32, pieces[0], *arrived)
 
 
@@ -541,11 +520,8 @@
     )
     slopes = (dec_s1, dec_s2)
     state = tick(2, None, place, kernels, slopes, cot)
-    near = far = None
     for turn in range(1, SECTIONS):
         cot = hand_on(state, turn - 1, 1)
-        if turn == 3:
-            near = first_phases(place, (state[1], dec_v, state[0], dec_h), range(0, 2))
         state = tick(2, turn, place, kernels, slopes, cot, state=state)
     upper = state
     skip = (beside(upper[4], 1), upper[2], beside(upper[3], -1))
@@ -554,10 +530,10 @@
     for turn in range(SECTIONS - 2, -1, -1):
         cot = hand_on(state, turn + 1, -1)
         if turn == 1:
-            far = first_phases(place, (upper[1], dec_v, upper[0], dec_h), range(2, 4))
+            dec_total = first_phases(place, (upper[1], dec_v, upper[0], dec_h))
         state = tick(0, turn, place, kernels, slopes, cot, skip=skip, state=state)
     enc_total = first_phases(place, (state[1], enc_v, state[0], enc_h))
-    mine = last_phases(place, [enc_total, near, far])
+    mine = last_phases(place, [enc_total, dec_total])
     other = [send(part, core_step, 1) for part in mine]
     totals = unpack(place, 0, mine)
     weight_total, bias_total = unpack(place, 1, other, totals)

time: 293 us -> 221 us (0.75)
  the two profiles are of different devices: /device:TPU:2 before, /device:TPU:1 now
where the time goes in v1:
time: 221 us; the launch traced here: 220 us
  starting transfers between devices  89.6 us (41%)
  waiting for transfers between devices  86.7 us (39%)
  Pallas kernels  34.2 us (15%)
  local copies, waits for them, and re-layouts  7.68 us (3%)
    ppermute x24, starting transfers between devices, send(): lax.ppermute(array, 'space', [(place, move(place, step)) for place in ran...  48.2 us
    ppermute x24, waiting for transfers between devices, send(): lax.ppermute(array, 'space', [(place, move(place, step)) for place in ran...  41.9 us
    ppermute x6, waiting for transfers between devices, hand_on(): before = lax.ppermute(high, GRID_AXES, shifted(source_section, by, 1))  35 us
    ppermute x8, starting transfers between devices, beside(): return lax.ppermute(array, 'space', pairs)  23.2 us
    pallas_call x8, Pallas kernels, tick(): pl.pallas_call(lambda *refs: tick_kernel(layer, turn, seeded, *refs), out...  10.1 us
    pallas_call x2, Pallas kernels, forward(): pl.pallas_call(kernel, out_shape=[sds(6, BF), sds(6, BF), sds(6, F32), sd...  8.25 us
    ppermute x6, starting transfers between devices, hand_on(): middle = lax.ppermute(grad, GRID_AXES, shifted(source_section, by, 0))  7.09 us
    pallas_call x2, Pallas kernels, unpack(): pl.pallas_call(lambda *refs: unpack_kernel(*refs), out_shape=[jax.ShapeDt...  6.61 us
  transfers between devices with their start and end apart: 50, of which 20 were waited for; matrix products, arithmetic and copies ran while one was open for 2% of the time, Pallas kernels for 8%

profile of v1, /device:TPU:1, one launch (start us, length us, event | category | flops | bytes accessed | tf_op | source)
XLA Modules:
  0.0 220.4 jit_solution(6715294868837016844)
XLA Ops:
  1.7 5.1 %collective-permute-start.2 = (bf16[256,256]{1,0:T(8,128)(2,1)S(1)}, bf16[256,256]{1,0:T(8,128)(2,1)S(1)}, u32[]{:S(2)}, u32[]{:S(2)}) collective-permute-start(bf16[256,256]{1,0:T(8,128)(2,1)S(1)} %bitcast.64), channel_id=1, source_target_pairs={{1,0},{2,1},{3,2},{4,3},{5,4},{6,5},{7,6},{8,7},{9,8},{10,9},{11,1... | collective-permute-start | bytes 393224 | tf_op jit(solution)/shard_map/ppermute | solution.py:226
  6.8 1.9 collective-permute-start.1
  9.7 2.7 %collective-permute-start = (bf16[128,256]{1,0:T(8,128)(2,1)S(1)}, bf16[128,256]{1,0:T(8,128)(2,1)S(1)}, u32[]{:S(2)}, u32[]{:S(2)}) collective-permute-start(bf16[128,256]{1,0:T(8,128)(2,1)S(1)} %bitcast.91), channel_id=1, source_target_pairs={{0,2},{1,3},{2,4},{3,5},{4,6},{5,7},{6,8},{7,9},{8,10},{9,11},{10,... | collective-permute-start | bytes 196616 | tf_op jit(solution)/shard_map/ppermute | solution.py:226
  16.0 1.9 collective-permute-start.5
  18.8 3.7 %collective-permute-start.4 = (bf16[512,256]{1,0:T(8,128)(2,1)S(1)}, bf16[512,256]{1,0:T(8,128)(2,1)S(1)}, u32[]{:S(2)}, u32[]{:S(2)}) collective-permute-start(bf16[512,256]{1,0:T(8,128)(2,1)S(1)} %constant_dynamic-update-slice_fusion.own), channel_id=1, source_target_pairs={{0,1},{1,2},{2,3},{3,4},{4,5},{5,6},{6,7},{7,8},{8,9},{9,10},{10,1... | collective-permute-start | bytes 786440 | tf_op jit(solution)/shard_map/ppermute | solution.py:226
  22.5 2.0 copy-done
  24.5 4.7 %shard_map.84 = (bf16[384,256]{1,0:T(8,128)(2,1)S(1)}, bf16[384,256]{1,0:T(8,128)(2,1)S(1)}, f32[384,256]{1,0:T(8,128)S(1)}, f32[512,256]{1,0:T(8,128)S(1)}, bf16[768,256]{1,0:T(8,128)(2,1)S(1)}) custom-call(s32[2]{0:T(128)S(1)} %pad_add_fusion.place_ref.refs_0_, bf16[4,3,128,1152]{3,2,1,0:T(8,128)(2,1)S(1)} %bitcast.68, ...), custom_call_target="tpu_custom_call" | custom-call | flops 3000000000 | bytes 5242880 | tf_op jit(solution)/shard_map/pallas_call | solution.py:128
  29.3 3.6 %shard_map.85 = (bf16[384,256]{1,0:T(8,128)(2,1)S(1)}, bf16[384,256]{1,0:T(8,128)(2,1)S(1)}, f32[384,256]{1,0:T(8,128)S(1)}, f32[512,256]{1,0:T(8,128)S(1)}) custom-call(s32[2]{0:T(128)S(1)} %pad_add_fusion.place_ref.refs_0_, bf16[4,3,128,1152]{3,2,1,0:T(8,128)(2,1)S(1)} %bitcast.69, f32[4,256]{1,0:T(4,128)S(1)} %pad_maximum_fusion.bias_ref, ...), custom_call_target="tpu_custom_call" | custom-call | flops 3000000000 | bytes 5242880 | tf_op jit(solution)/shard_map/pallas_call | solution.py:128
  32.8 2.2 tick.8
  35.0 3.1 %collective-permute-start.7 = (bf16[256,256]{1,0:T(8,128)(2,1)S(1)}, bf16[256,256]{1,0:T(8,128)(2,1)S(1)}, u32[]{:S(2)}, u32[]{:S(2)}) collective-permute-start(bf16[256,256]{1,0:T(8,128)(2,1)S(1)} %get-tuple-element.81.refs_9_), channel_id=1, source_target_pairs={{0,64},{1,65},{2,66},{3,67},{4,68},{5,69},{6,70},{7,71},{8,72},{9,... | collective-permute-start | bytes 393224 | tf_op jit(solution)/shard_map/ppermute | solution.py:218
  38.1 1.6 collective-permute-start.6
  39.8 1.3 collective-permute-start.8
  48.6 4.6 %collective-permute-start.15 = (bf16[128,256]{1,0:T(8,128)(2,1)S(1)}, bf16[128,256]{1,0:T(8,128)(2,1)S(1)}, u32[]{:S(2)}, u32[]{:S(2)}) collective-permute-start(bf16[128,256]{1,0:T(8,128)(2,1)S(1)} %get-tuple-element.95), channel_id=1, source_target_pairs={{0,1},{1,2},{2,3},{3,4},{4,5},{5,6},{6,7},{7,8},{8,9},{9,10},{10,1... | collective-permute-start | bytes 196616 | tf_op jit(solution)/shard_map/ppermute | solution.py:226
  53.2 1.9 collective-permute-start.16
  55.1 3.6 %collective-permute-done.16.refs_6_.refs_9_ = bf16[128,256]{1,0:T(8,128)(2,1)S(1)} collective-permute-done((bf16[128,256]{1,0:T(8,128)(2,1)S(1)}, bf16[128,256]{1,0:T(8,128)(2,1)S(1)}, u32[]{:S(2)}, u32[]{:S(2)}) %collective-permute-start.16) | collective-permute-done | bytes 65568 | tf_op jit(solution)/shard_map/ppermute | solution.py:226
  58.8 2.1 tick.12
  66.4 1.4 collective-permute-start.23
  70.5 1.7 weights.3
  72.3 34.1 %collective-permute-done.23.refs_4_ = bf16[128,256]{1,0:T(8,128)(2,1)S(1)} collective-permute-done((bf16[128,256]{1,0:T(8,128)(2,1)S(1)}, bf16[128,256]{1,0:T(8,128)(2,1)S(1)}, u32[]{:S(2)}, u32[]{:S(2)}) %collective-permute-start.23) | collective-permute-done | bytes 65568 | tf_op jit(solution)/shard_map/ppermute | solution.py:219
  106.4 5.3 %collective-permute-done.25.refs_6_ = bf16[128,256]{1,0:T(8,128)(2,1)S(1)} collective-permute-done((bf16[128,256]{1,0:T(8,128)(2,1)S(1)}, bf16[128,256]{1,0:T(8,128)(2,1)S(1)}, u32[]{:S(2)}, u32[]{:S(2)}) %collective-permute-start.25) | collective-permute-done | bytes 65568 | tf_op jit(solution)/shard_map/ppermute | solution.py:220
  111.9 2.8 %tick.15 = (bf16[256,256]{1,0:T(8,128)(2,1)S(1)}, bf16[256,256]{1,0:T(8,128)(2,1)S(1)}, bf16[256,256]{1,0:T(8,128)(2,1)S(1)}, bf16[128,256]{1,0:T(8,128)(2,1)}, bf16[128,256]{1,0:T(8,128)(2,1)}) custom-call(s32[2]{0:T(128)S(1)} %pad_add_fusion.place_ref.refs_0_, bf16[4,3,128,1152]{3,2,1,0:T(8,128)(2,1)S(1)} %bitcast.77, ...), custom_call_target="tpu_custom_call" | custom-call | flops 3000000000 | bytes 4194304 | tf_op jit(solution)/shard_map/tick/pallas_call | solution.py:188
  114.7 1.7 weights.2
  117.5 5.7 %collective-permute-start.31 = (bf16[1,896,128]{2,1,0:T(8,128)(2,1)S(1)}, bf16[1,896,128]{2,1,0:T(8,128)(2,1)S(1)}, u32[]{:S(2)}, u32[]{:S(2)}) collective-permute-start(bf16[1,896,128]{2,1,0:T(8,128)(2,1)S(1)} %get-tuple-element.131), channel_id=1, source_target_pairs={{0,4},{1,5},{2,6},{3,7},{4,0},{5,1},{6,2},{7,3},{8,12},{9,13},{10,... | collective-permute-start | bytes 688136 | tf_op jit(solution)/shard_map/ppermute | solution.py:372
  123.5 2.3 %collective-permute-start.33 = (bf16[1,896,128]{2,1,0:T(8,128)(2,1)S(1)}, bf16[1,896,128]{2,1,0:T(8,128)(2,1)S(1)}, u32[]{:S(2)}, u32[]{:S(2)}) collective-permute-start(bf16[1,896,128]{2,1,0:T(8,128)(2,1)S(1)} %get-tuple-element.133), channel_id=1, source_target_pairs={{0,6},{1,7},{2,0},{3,1},{4,2},{5,3},{6,4},{7,5},{8,14},{9,15},{10,... | collective-permute-start | bytes 688136 | tf_op jit(solution)/shard_map/ppermute | solution.py:372
  127.4 1.7 collective-permute-done.31.refs_1_
  129.1 2.4 %collective-permute-start.29 = (bf16[1,896,128]{2,1,0:T(8,128)(2,1)S(1)}, bf16[1,896,128]{2,1,0:T(8,128)(2,1)S(1)}, u32[]{:S(2)}, u32[]{:S(2)}) collective-permute-start(bf16[1,896,128]{2,1,0:T(8,128)(2,1)S(1)} %get-tuple-element.123), channel_id=1, source_target_pairs={{0,6},{1,7},{2,0},{3,1},{4,2},{5,3},{6,4},{7,5},{8,14},{9,15},{10,... | collective-permute-start | bytes 688136 | tf_op jit(solution)/shard_map/ppermute | solution.py:372
  131.6 2.7 %collective-permute-done.32.refs_2_ = bf16[1,896,128]{2,1,0:T(8,128)(2,1)S(1)} collective-permute-done((bf16[1,896,128]{2,1,0:T(8,128)(2,1)S(1)}, bf16[1,896,128]{2,1,0:T(8,128)(2,1)S(1)}, u32[]{:S(2)}, u32[]{:S(2)}) %collective-permute-start.32) | collective-permute-done | bytes 229408 | tf_op jit(solution)/shard_map/ppermute | solution.py:372
  134.3 4.7 %collective-permute-done.27.refs_1_ = bf16[1,896,128]{2,1,0:T(8,128)(2,1)S(1)} collective-permute-done((bf16[1,896,128]{2,1,0:T(8,128)(2,1)S(1)}, bf16[1,896,128]{2,1,0:T(8,128)(2,1)S(1)}, u32[]{:S(2)}, u32[]{:S(2)}) %collective-permute-start.27) | collective-permute-done | bytes 229408 | tf_op jit(solution)/shard_map/ppermute | solution.py:372
  139.0 5.0 %collective-permute-done.28.refs_2_ = bf16[1,896,128]{2,1,0:T(8,128)(2,1)S(1)} collective-permute-done((bf16[1,896,128]{2,1,0:T(8,128)(2,1)S(1)}, bf16[1,896,128]{2,1,0:T(8,128)(2,1)S(1)}, u32[]{:S(2)}, u32[]{:S(2)}) %collective-permute-start.28) | collective-permute-done | bytes 229408 | tf_op jit(solution)/shard_map/ppermute | solution.py:372
  144.8 13.3 %collective-permute-start.34 = (bf16[2,224,128]{2,1,0:T(8,128)(2,1)S(1)}, bf16[2,224,128]{2,1,0:T(8,128)(2,1)S(1)}, u32[]{:S(2)}, u32[]{:S(2)}) collective-permute-start(bf16[2,224,128]{2,1,0:T(8,128)(2,1)S(1)} %get-tuple-element.135), channel_id=1, source_target_pairs={{0,32},{1,33},{2,34},{3,35},{4,36},{5,37},{6,38},{7,39},{8,40},{9,... | collective-permute-start | bytes 344072 | tf_op jit(solution)/shard_map/ppermute | solution.py:372
  158.1 3.6 %collective-permute-start.36 = (bf16[2,224,128]{2,1,0:T(8,128)(2,1)S(1)}, bf16[2,224,128]{2,1,0:T(8,128)(2,1)S(1)}, u32[]{:S(2)}, u32[]{:S(2)}) collective-permute-start(bf16[2,224,128]{2,1,0:T(8,128)(2,1)S(1)} %get-tuple-element.137), channel_id=1, source_target_pairs={{0,48},{1,49},{2,50},{3,51},{4,52},{5,53},{6,54},{7,55},{8,56},{9,... | collective-permute-start | bytes 344072 | tf_op jit(solution)/shard_map/ppermute | solution.py:372
  161.7 3.5 %collective-permute-done.34.refs_1_ = bf16[2,224,128]{2,1,0:T(8,128)(2,1)S(1)} collective-permute-done((bf16[2,224,128]{2,1,0:T(8,128)(2,1)S(1)}, bf16[2,224,128]{2,1,0:T(8,128)(2,1)S(1)}, u32[]{:S(2)}, u32[]{:S(2)}) %collective-permute-start.34) | collective-permute-done | bytes 114720 | tf_op jit(solution)/shard_map/ppermute | solution.py:372
  165.1 2.5 %collective-permute-done.35.refs_2_ = bf16[2,224,128]{2,1,0:T(8,128)(2,1)S(1)} collective-permute-done((bf16[2,224,128]{2,1,0:T(8,128)(2,1)S(1)}, bf16[2,224,128]{2,1,0:T(8,128)(2,1)S(1)}, u32[]{:S(2)}, u32[]{:S(2)}) %collective-permute-start.35) | collective-permute-done | bytes 114720 | tf_op jit(solution)/shard_map/ppermute | solution.py:372
  168.4 3.0 %collective-permute-done.37.refs_1_ = bf16[2,112,128]{2,1,0:T(8,128)(2,1)S(1)} collective-permute-done((bf16[2,112,128]{2,1,0:T(8,128)(2,1)S(1)}, bf16[2,112,128]{2,1,0:T(8,128)(2,1)S(1)}, u32[]{:S(2)}, u32[]{:S(2)}) %collective-permute-start.37) | collective-permute-done | bytes 57376 | tf_op jit(solution)/shard_map/ppermute | solution.py:372
  171.5 3.0 %collective-permute-done.38.refs_2_ = bf16[2,112,128]{2,1,0:T(8,128)(2,1)S(1)} collective-permute-done((bf16[2,112,128]{2,1,0:T(8,128)(2,1)S(1)}, bf16[2,112,128]{2,1,0:T(8,128)(2,1)S(1)}, u32[]{:S(2)}, u32[]{:S(2)}) %collective-permute-start.38) | collective-permute-done | bytes 57376 | tf_op jit(solution)/shard_map/ppermute | solution.py:372
  175.1 1.6 collective-permute-start.41
  176.7 4.7 %collective-permute-start.40 = (bf16[2,224,128]{2,1,0:T(8,128)(2,1)S(1)}, bf16[2,224,128]{2,1,0:T(8,128)(2,1)S(1)}, u32[]{:S(2)}, u32[]{:S(2)}) collective-permute-start(bf16[2,224,128]{2,1,0:T(8,128)(2,1)S(1)} %bitcast.55), channel_id=1, source_target_pairs={{0,32},{1,33},{2,34},{3,35},{4,36},{5,37},{6,38},{7,39},{8,40},{9,... | collective-permute-start | bytes 344072 | tf_op jit(solution)/shard_map/ppermute | solution.py:372
  181.4 1.6 collective-permute-done.41.refs_3_
  182.9 1.5 collective-permute-done.40.refs_2_
  184.4 5.9 %collective-permute-done.39.refs_1_ = bf16[2,224,128]{2,1,0:T(8,128)(2,1)S(1)} collective-permute-done((bf16[2,224,128]{2,1,0:T(8,128)(2,1)S(1)}, bf16[2,224,128]{2,1,0:T(8,128)(2,1)S(1)}, u32[]{:S(2)}, u32[]{:S(2)}) %collective-permute-start.39) | collective-permute-done | bytes 114720 | tf_op jit(solution)/shard_map/ppermute | solution.py:372
  191.0 2.7 %collective-permute-start.47 = (bf16[896,128]{1,0:T(8,128)(2,1)S(1)}, bf16[896,128]{1,0:T(8,128)(2,1)S(1)}, u32[]{:S(2)}, u32[]{:S(2)}) collective-permute-start(bf16[896,128]{1,0:T(8,128)(2,1)S(1)} %bitcast.58), channel_id=1, source_target_pairs={{0,6},{1,7},{2,0},{3,1},{4,2},{5,3},{6,4},{7,5},{8,14},{9,15},{10,... | collective-permute-start | bytes 688136 | tf_op jit(solution)/shard_map/ppermute | solution.py:372
  193.8 3.3 %collective-permute-done.42.refs_1_ = bf16[896,128]{1,0:T(8,128)(2,1)S(1)} collective-permute-done((bf16[896,128]{1,0:T(8,128)(2,1)S(1)}, bf16[896,128]{1,0:T(8,128)(2,1)S(1)}, u32[]{:S(2)}, u32[]{:S(2)}) %collective-permute-start.42) | collective-permute-done | bytes 229408 | tf_op jit(solution)/shard_map/ppermute | solution.py:372
  197.0 2.7 %collective-permute-start.48 = (bf16[896,128]{1,0:T(8,128)(2,1)S(1)}, bf16[896,128]{1,0:T(8,128)(2,1)S(1)}, u32[]{:S(2)}, u32[]{:S(2)}) collective-permute-start(bf16[896,128]{1,0:T(8,128)(2,1)S(1)} %collective-permute-done.47.refs_3_), channel_id=1, source_target_pairs={{0,6},{1,7},{2,0},{3,1},{4,2},{5,3},{6,4},{7,5},{8,14},{9,15},{10,... | collective-permute-start | bytes 688136 | tf_op jit(solution)/shard_map/ppermute | solution.py:372
  199.9 3.5 %collective-permute-done.43.refs_2_ = bf16[896,128]{1,0:T(8,128)(2,1)S(1)} collective-permute-done((bf16[896,128]{1,0:T(8,128)(2,1)S(1)}, bf16[896,128]{1,0:T(8,128)(2,1)S(1)}, u32[]{:S(2)}, u32[]{:S(2)}) %collective-permute-start.43) | collective-permute-done | bytes 229408 | tf_op jit(solution)/shard_map/ppermute | solution.py:372
  204.0 5.8 %collective-permute-start.45 = (bf16[4,896,128]{2,1,0:T(8,128)(2,1)S(1)}, bf16[4,896,128]{2,1,0:T(8,128)(2,1)S(1)}, u32[]{:S(2)}, u32[]{:S(2)}) collective-permute-start(bf16[4,896,128]{2,1,0:T(8,128)(2,1)S(1)} %join_y.2.refs_1_), channel_id=1, source_target_pairs={{0,1},{1,0},{2,3},{3,2},{4,5},{5,4},{6,7},{7,6},{8,9},{9,8},{10,11... | collective-permute-start | bytes 2752520 | tf_op jit(solution)/shard_map/ppermute | solution.py:372
  210.5 1.8 collective-permute-start.49
  213.7 2.7 %unpack.2 = (f32[4,3,128,1152]{3,2,1,0:T(8,128)}, f32[4,1,128]{2,1,0:T(1,128)}) custom-call(s32[2]{0:T(128)S(1)} %pad_add_fusion.place_ref.refs_0_, bf16[4,896,128]{2,1,0:T(8,128)(2,1)S(1)} %join_y.2.refs_1_, bf16[4,896,128]{2,1,0:T(8,128)(2,1)S(1)} %join_y.3.refs_2_), custom_call_target="tpu_custom_call" | custom-call | tf_op jit(solution)/shard_map/unpack/pallas_call | solution.py:465
  216.5 3.9 %unpack.3 = (f32[4,3,128,1152]{3,2,1,0:T(8,128)}, f32[4,1,128]{2,1,0:T(1,128)}) custom-call(s32[2]{0:T(128)S(1)} %pad_add_fusion.place_ref.refs_0_, bf16[4,896,128]{2,1,0:T(8,128)(2,1)S(1)} %collective-permute-done.45.refs_1_, bf16[4,896,128]{2,1,0:T(8,128)(2,1)} %collective-permute-done.49.refs_2_, ...), custom_call_target="tpu_custom_call", output_to_operand_aliasing={{0}: (3, {}), {1}: (4, {})} | custom-call | tf_op jit(solution)/shard_map/unpack/pallas_call | solution.py:465
  (102 shorter events, 31.0 us)
Async XLA Ops:
  1.7 20.8 %collective-permute-start.2 = (bf16[256,256]{1,0:T(8,128)(2,1)S(1)}, bf16[256,256]{1,0:T(8,128)(2,1)S(1)}, u32[]{:S(2)}, u32[]{:S(2)}) collective-permute-start(bf16[256,256]{1,0:T(8,128)(2,1)S(1)} %bitcast.64), channel_id=1, source_target_pairs={{1,0},{2,1},{3,2},{4,3},{5,4},{6,5},{7,6},{8,7},{9,8},{10,9},{11,1... | collective-permute-start | bytes 393224 | tf_op jit(solution)/shard_map/ppermute | solution.py:226
  6.8 15.7 %collective-permute-start.1 = (bf16[256,256]{1,0:T(8,128)(2,1)S(1)}, bf16[256,256]{1,0:T(8,128)(2,1)S(1)}, u32[]{:S(2)}, u32[]{:S(2)}) collective-permute-start(bf16[256,256]{1,0:T(8,128)(2,1)S(1)} %bitcast.65), channel_id=1, source_target_pairs={{0,1},{1,2},{2,3},{3,4},{4,5},{5,6},{6,7},{7,8},{8,9},{9,10},{10,1... | collective-permute-start | bytes 393224 | tf_op jit(solution)/shard_map/ppermute | solution.py:226
  9.7 9.0 %collective-permute-start = (bf16[128,256]{1,0:T(8,128)(2,1)S(1)}, bf16[128,256]{1,0:T(8,128)(2,1)S(1)}, u32[]{:S(2)}, u32[]{:S(2)}) collective-permute-start(bf16[128,256]{1,0:T(8,128)(2,1)S(1)} %bitcast.91), channel_id=1, source_target_pairs={{0,2},{1,3},{2,4},{3,5},{4,6},{5,7},{6,8},{7,9},{8,10},{9,11},{10,... | collective-permute-start | bytes 196616 | tf_op jit(solution)/shard_map/ppermute | solution.py:226
  12.5 10.0 %collective-permute-start.3 = (bf16[128,256]{1,0:T(8,128)(2,1)S(1)}, bf16[128,256]{1,0:T(8,128)(2,1)S(1)}, u32[]{:S(2)}, u32[]{:S(2)}) collective-permute-start(bf16[128,256]{1,0:T(8,128)(2,1)S(1)} %bitcast.92), channel_id=1, source_target_pairs={{2,0},{3,1},{4,2},{5,3},{6,4},{7,5},{8,6},{9,7},{10,8},{11,9},{12,... | collective-permute-start | bytes 196616 | tf_op jit(solution)/shard_map/ppermute | solution.py:226
  16.0 13.3 %collective-permute-start.5 = (bf16[512,256]{1,0:T(8,128)(2,1)S(1)}, bf16[512,256]{1,0:T(8,128)(2,1)S(1)}, u32[]{:S(2)}, u32[]{:S(2)}) collective-permute-start(bf16[512,256]{1,0:T(8,128)(2,1)S(1)} %constant_dynamic-update-slice_fusion.own), channel_id=1, source_target_pairs={{1,0},{2,1},{3,2},{4,3},{5,4},{6,5},{7,6},{8,7},{9,8},{10,9},{11,1... | collective-permute-start | bytes 786440 | tf_op jit(solution)/shard_map/ppermute | solution.py:226
  18.8 10.5 %collective-permute-start.4 = (bf16[512,256]{1,0:T(8,128)(2,1)S(1)}, bf16[512,256]{1,0:T(8,128)(2,1)S(1)}, u32[]{:S(2)}, u32[]{:S(2)}) collective-permute-start(bf16[512,256]{1,0:T(8,128)(2,1)S(1)} %constant_dynamic-update-slice_fusion.own), channel_id=1, source_target_pairs={{0,1},{1,2},{2,3},{3,4},{4,5},{5,6},{6,7},{7,8},{8,9},{9,10},{10,1... | collective-permute-start | bytes 786440 | tf_op jit(solution)/shard_map/ppermute | solution.py:226
  35.0 7.7 %collective-permute-start.7 = (bf16[256,256]{1,0:T(8,128)(2,1)S(1)}, bf16[256,256]{1,0:T(8,128)(2,1)S(1)}, u32[]{:S(2)}, u32[]{:S(2)}) collective-permute-start(bf16[256,256]{1,0:T(8,128)(2,1)S(1)} %get-tuple-element.81.refs_9_), channel_id=1, source_target_pairs={{0,64},{1,65},{2,66},{3,67},{4,68},{5,69},{6,70},{7,71},{8,72},{9,... | collective-permute-start | bytes 393224 | tf_op jit(solution)/shard_map/ppermute | solution.py:218
  38.1 3.9 %collective-permute-start.6 = (bf16[128,256]{1,0:T(8,128)(2,1)S(1)}, bf16[128,256]{1,0:T(8,128)(2,1)S(1)}, u32[]{:S(2)}, u32[]{:S(2)}) collective-permute-start(bf16[128,256]{1,0:T(8,128)(2,1)S(1)} %get-tuple-element.80.refs_11_), channel_id=1, source_target_pairs={{0,65},{1,66},{2,67},{3,68},{4,69},{5,70},{6,71},{7,72},{8,73},{9,... | collective-permute-start | bytes 196616 | tf_op jit(solution)/shard_map/ppermute | solution.py:219
  39.8 2.9 %collective-permute-start.8 = (bf16[128,256]{1,0:T(8,128)(2,1)S(1)}, bf16[128,256]{1,0:T(8,128)(2,1)S(1)}, u32[]{:S(2)}, u32[]{:S(2)}) collective-permute-start(bf16[128,256]{1,0:T(8,128)(2,1)S(1)} %get-tuple-element.82.refs_10_), channel_id=1, source_target_pairs={{1,64},{2,65},{3,66},{4,67},{5,68},{6,69},{7,70},{8,71},{9,72},{10... | collective-permute-start | bytes 196616 | tf_op jit(solution)/shard_map/ppermute | solution.py:220
  43.3 2.0 collective-permute-start.10
  44.0 1.3 collective-permute-start.9
  44.6 0.7 collective-permute-start.11
  45.9 2.0 collective-permute-start.13
  46.6 1.3 collective-permute-start.12
  48.6 6.5 %collective-permute-start.15 = (bf16[128,256]{1,0:T(8,128)(2,1)S(1)}, bf16[128,256]{1,0:T(8,128)(2,1)S(1)}, u32[]{:S(2)}, u32[]{:S(2)}) collective-permute-start(bf16[128,256]{1,0:T(8,128)(2,1)S(1)} %get-tuple-element.95), channel_id=1, source_target_pairs={{0,1},{1,2},{2,3},{3,4},{4,5},{5,6},{6,7},{7,8},{8,9},{9,10},{10,1... | collective-permute-start | bytes 196616 | tf_op jit(solution)/shard_map/ppermute | solution.py:226
  53.2 5.6 %collective-permute-start.16 = (bf16[128,256]{1,0:T(8,128)(2,1)S(1)}, bf16[128,256]{1,0:T(8,128)(2,1)S(1)}, u32[]{:S(2)}, u32[]{:S(2)}) collective-permute-start(bf16[128,256]{1,0:T(8,128)(2,1)S(1)} %get-tuple-element.97), channel_id=1, source_target_pairs={{1,0},{2,1},{3,2},{4,3},{5,4},{6,5},{7,6},{8,7},{9,8},{10,9},{11,1... | collective-permute-start | bytes 196616 | tf_op jit(solution)/shard_map/ppermute | solution.py:226
  60.9 2.2 %collective-permute-start.18 = (bf16[256,256]{1,0:T(8,128)(2,1)S(1)}, bf16[256,256]{1,0:T(8,128)(2,1)S(1)}, u32[]{:S(2)}, u32[]{:S(2)}) collective-permute-start(bf16[256,256]{1,0:T(8,128)(2,1)S(1)} %get-tuple-element.99.refs_12_), channel_id=1, source_target_pairs={{192,128},{193,129},{194,130},{195,131},{196,132},{197,133},{198,1... | collective-permute-start | bytes 393224 | tf_op jit(solution)/shard_map/ppermute | solution.py:218
  61.6 1.5 collective-permute-start.17
  62.5 0.7 collective-permute-start.19
  63.8 2.0 collective-permute-start.21
  64.4 1.3 collective-permute-start.20
  66.4 39.9 %collective-permute-start.23 = (bf16[128,256]{1,0:T(8,128)(2,1)S(1)}, bf16[128,256]{1,0:T(8,128)(2,1)S(1)}, u32[]{:S(2)}, u32[]{:S(2)}) collective-permute-start(bf16[128,256]{1,0:T(8,128)(2,1)S(1)} %get-tuple-element.108.refs_14_), channel_id=1, source_target_pairs={{64,1},{65,2},{66,3},{67,4},{68,5},{69,6},{70,7},{71,8},{72,9},{73... | collective-permute-start | bytes 196616 | tf_op jit(solution)/shard_map/ppermute | solution.py:219
  67.9 43.8 %collective-permute-start.25 = (bf16[128,256]{1,0:T(8,128)(2,1)S(1)}, bf16[128,256]{1,0:T(8,128)(2,1)S(1)}, u32[]{:S(2)}, u32[]{:S(2)}) collective-permute-start(bf16[128,256]{1,0:T(8,128)(2,1)S(1)} %get-tuple-element.110.refs_13_), channel_id=1, source_target_pairs={{65,0},{66,1},{67,2},{68,3},{69,4},{70,5},{71,6},{72,7},{73,8},{74... | collective-permute-start | bytes 196616 | tf_op jit(solution)/shard_map/ppermute | solution.py:220
  69.2 42.7 %collective-permute-start.24 = (bf16[256,256]{1,0:T(8,128)(2,1)S(1)}, bf16[256,256]{1,0:T(8,128)(2,1)S(1)}, u32[]{:S(2)}, u32[]{:S(2)}) collective-permute-start(bf16[256,256]{1,0:T(8,128)(2,1)S(1)} %get-tuple-element.109.refs_12_), channel_id=1, source_target_pairs={{64,0},{65,1},{66,2},{67,3},{68,4},{69,5},{70,6},{71,7},{72,8},{73... | collective-permute-start | bytes 393224 | tf_op jit(solution)/shard_map/ppermute | solution.py:218
  72.2 44.3 %collective-permute-start.30 = (bf16[4,896,128]{2,1,0:T(8,128)(2,1)S(1)}, bf16[4,896,128]{2,1,0:T(8,128)(2,1)S(1)}, u32[]{:S(2)}, u32[]{:S(2)}) collective-permute-start(bf16[4,896,128]{2,1,0:T(8,128)(2,1)S(1)} %get-tuple-element.129), channel_id=1, source_target_pairs={{0,1},{1,0},{2,3},{3,2},{4,5},{5,4},{6,7},{7,6},{8,9},{9,8},{10,11... | collective-permute-start | bytes 2752520 | tf_op jit(solution)/shard_map/ppermute | solution.py:372
  116.4 9.4 %collective-permute-start.26 = (bf16[4,896,128]{2,1,0:T(8,128)(2,1)S(1)}, bf16[4,896,128]{2,1,0:T(8,128)(2,1)S(1)}, u32[]{:S(2)}, u32[]{:S(2)}) collective-permute-start(bf16[4,896,128]{2,1,0:T(8,128)(2,1)S(1)} %get-tuple-element.119), channel_id=1, source_target_pairs={{0,1},{1,0},{2,3},{3,2},{4,5},{5,4},{6,7},{7,6},{8,9},{9,8},{10,11... | collective-permute-start | bytes 2752520 | tf_op jit(solution)/shard_map/ppermute | solution.py:372
  117.5 11.7 %collective-permute-start.31 = (bf16[1,896,128]{2,1,0:T(8,128)(2,1)S(1)}, bf16[1,896,128]{2,1,0:T(8,128)(2,1)S(1)}, u32[]{:S(2)}, u32[]{:S(2)}) collective-permute-start(bf16[1,896,128]{2,1,0:T(8,128)(2,1)S(1)} %get-tuple-element.131), channel_id=1, source_target_pairs={{0,4},{1,5},{2,6},{3,7},{4,0},{5,1},{6,2},{7,3},{8,12},{9,13},{10,... | collective-permute-start | bytes 688136 | tf_op jit(solution)/shard_map/ppermute | solution.py:372
  123.1 11.1 %collective-permute-start.32 = (bf16[1,896,128]{2,1,0:T(8,128)(2,1)S(1)}, bf16[1,896,128]{2,1,0:T(8,128)(2,1)S(1)}, u32[]{:S(2)}, u32[]{:S(2)}) collective-permute-start(bf16[1,896,128]{2,1,0:T(8,128)(2,1)S(1)} %get-tuple-element.132), channel_id=1, source_target_pairs={{0,2},{1,3},{2,4},{3,5},{4,6},{5,7},{6,0},{7,1},{8,10},{9,11},{10,... | collective-permute-start | bytes 688136 | tf_op jit(solution)/shard_map/ppermute | solution.py:372
  123.5 10.8 %collective-permute-start.33 = (bf16[1,896,128]{2,1,0:T(8,128)(2,1)S(1)}, bf16[1,896,128]{2,1,0:T(8,128)(2,1)S(1)}, u32[]{:S(2)}, u32[]{:S(2)}) collective-permute-start(bf16[1,896,128]{2,1,0:T(8,128)(2,1)S(1)} %get-tuple-element.133), channel_id=1, source_target_pairs={{0,6},{1,7},{2,0},{3,1},{4,2},{5,3},{6,4},{7,5},{8,14},{9,15},{10,... | collective-permute-start | bytes 688136 | tf_op jit(solution)/shard_map/ppermute | solution.py:372
  126.7 12.3 %collective-permute-start.27 = (bf16[1,896,128]{2,1,0:T(8,128)(2,1)S(1)}, bf16[1,896,128]{2,1,0:T(8,128)(2,1)S(1)}, u32[]{:S(2)}, u32[]{:S(2)}) collective-permute-start(bf16[1,896,128]{2,1,0:T(8,128)(2,1)S(1)} %get-tuple-element.121), channel_id=1, source_target_pairs={{0,4},{1,5},{2,6},{3,7},{4,0},{5,1},{6,2},{7,3},{8,12},{9,13},{10,... | collective-permute-start | bytes 688136 | tf_op jit(solution)/shard_map/ppermute | solution.py:372
  126.8 17.1 %collective-permute-start.28 = (bf16[1,896,128]{2,1,0:T(8,128)(2,1)S(1)}, bf16[1,896,128]{2,1,0:T(8,128)(2,1)S(1)}, u32[]{:S(2)}, u32[]{:S(2)}) collective-permute-start(bf16[1,896,128]{2,1,0:T(8,128)(2,1)S(1)} %get-tuple-element.122), channel_id=1, source_target_pairs={{0,2},{1,3},{2,4},{3,5},{4,6},{5,7},{6,0},{7,1},{8,10},{9,11},{10,... | collective-permute-start | bytes 688136 | tf_op jit(solution)/shard_map/ppermute | solution.py:372
  129.1 14.8 %collective-permute-start.29 = (bf16[1,896,128]{2,1,0:T(8,128)(2,1)S(1)}, bf16[1,896,128]{2,1,0:T(8,128)(2,1)S(1)}, u32[]{:S(2)}, u32[]{:S(2)}) collective-permute-start(bf16[1,896,128]{2,1,0:T(8,128)(2,1)S(1)} %get-tuple-element.123), channel_id=1, source_target_pairs={{0,6},{1,7},{2,0},{3,1},{4,2},{5,3},{6,4},{7,5},{8,14},{9,15},{10,... | collective-permute-start | bytes 688136 | tf_op jit(solution)/shard_map/ppermute | solution.py:372
  144.8 20.4 %collective-permute-start.34 = (bf16[2,224,128]{2,1,0:T(8,128)(2,1)S(1)}, bf16[2,224,128]{2,1,0:T(8,128)(2,1)S(1)}, u32[]{:S(2)}, u32[]{:S(2)}) collective-permute-start(bf16[2,224,128]{2,1,0:T(8,128)(2,1)S(1)} %get-tuple-element.135), channel_id=1, source_target_pairs={{0,32},{1,33},{2,34},{3,35},{4,36},{5,37},{6,38},{7,39},{8,40},{9,... | collective-permute-start | bytes 344072 | tf_op jit(solution)/shard_map/ppermute | solution.py:372
  158.1 9.5 %collective-permute-start.35 = (bf16[2,224,128]{2,1,0:T(8,128)(2,1)S(1)}, bf16[2,224,128]{2,1,0:T(8,128)(2,1)S(1)}, u32[]{:S(2)}, u32[]{:S(2)}) collective-permute-start(bf16[2,224,128]{2,1,0:T(8,128)(2,1)S(1)} %get-tuple-element.136), channel_id=1, source_target_pairs={{0,16},{1,17},{2,18},{3,19},{4,20},{5,21},{6,22},{7,23},{8,24},{9,... | collective-permute-start | bytes 344072 | tf_op jit(solution)/shard_map/ppermute | solution.py:372
  158.1 9.5 %collective-permute-start.36 = (bf16[2,224,128]{2,1,0:T(8,128)(2,1)S(1)}, bf16[2,224,128]{2,1,0:T(8,128)(2,1)S(1)}, u32[]{:S(2)}, u32[]{:S(2)}) collective-permute-start(bf16[2,224,128]{2,1,0:T(8,128)(2,1)S(1)} %get-tuple-element.137), channel_id=1, source_target_pairs={{0,48},{1,49},{2,50},{3,51},{4,52},{5,53},{6,54},{7,55},{8,56},{9,... | collective-permute-start | bytes 344072 | tf_op jit(solution)/shard_map/ppermute | solution.py:372
  168.3 3.1 %collective-permute-start.37 = (bf16[2,112,128]{2,1,0:T(8,128)(2,1)S(1)}, bf16[2,112,128]{2,1,0:T(8,128)(2,1)S(1)}, u32[]{:S(2)}, u32[]{:S(2)}) collective-permute-start(bf16[2,112,128]{2,1,0:T(8,128)(2,1)S(1)} %get-tuple-element.139), channel_id=1, source_target_pairs={{0,8},{1,9},{2,10},{3,11},{4,12},{5,13},{6,14},{7,15},{8,0},{9,1},... | collective-permute-start | bytes 172040 | tf_op jit(solution)/shard_map/ppermute | solution.py:372
  171.4 3.1 %collective-permute-start.38 = (bf16[2,112,128]{2,1,0:T(8,128)(2,1)S(1)}, bf16[2,112,128]{2,1,0:T(8,128)(2,1)S(1)}, u32[]{:S(2)}, u32[]{:S(2)}) collective-permute-start(bf16[2,112,128]{2,1,0:T(8,128)(2,1)S(1)} %added.7.refs_1_), channel_id=1, source_target_pairs={{0,8},{1,9},{2,10},{3,11},{4,12},{5,13},{6,14},{7,15},{8,0},{9,1},... | collective-permute-start | bytes 172040 | tf_op jit(solution)/shard_map/ppermute | solution.py:372
  175.1 7.8 %collective-permute-start.41 = (bf16[2,224,128]{2,1,0:T(8,128)(2,1)S(1)}, bf16[2,224,128]{2,1,0:T(8,128)(2,1)S(1)}, u32[]{:S(2)}, u32[]{:S(2)}) collective-permute-start(bf16[2,224,128]{2,1,0:T(8,128)(2,1)S(1)} %bitcast.54), channel_id=1, source_target_pairs={{0,48},{1,49},{2,50},{3,51},{4,52},{5,53},{6,54},{7,55},{8,56},{9,... | collective-permute-start | bytes 344072 | tf_op jit(solution)/shard_map/ppermute | solution.py:372
  176.7 7.8 %collective-permute-start.40 = (bf16[2,224,128]{2,1,0:T(8,128)(2,1)S(1)}, bf16[2,224,128]{2,1,0:T(8,128)(2,1)S(1)}, u32[]{:S(2)}, u32[]{:S(2)}) collective-permute-start(bf16[2,224,128]{2,1,0:T(8,128)(2,1)S(1)} %bitcast.55), channel_id=1, source_target_pairs={{0,32},{1,33},{2,34},{3,35},{4,36},{5,37},{6,38},{7,39},{8,40},{9,... | collective-permute-start | bytes 344072 | tf_op jit(solution)/shard_map/ppermute | solution.py:372
  181.4 8.9 %collective-permute-start.39 = (bf16[2,224,128]{2,1,0:T(8,128)(2,1)S(1)}, bf16[2,224,128]{2,1,0:T(8,128)(2,1)S(1)}, u32[]{:S(2)}, u32[]{:S(2)}) collective-permute-start(bf16[2,224,128]{2,1,0:T(8,128)(2,1)S(1)} %bitcast.56), channel_id=1, source_target_pairs={{0,16},{1,17},{2,18},{3,19},{4,20},{5,21},{6,22},{7,23},{8,24},{9,... | collective-permute-start | bytes 344072 | tf_op jit(solution)/shard_map/ppermute | solution.py:372
  190.9 6.2 %collective-permute-start.42 = (bf16[896,128]{1,0:T(8,128)(2,1)S(1)}, bf16[896,128]{1,0:T(8,128)(2,1)S(1)}, u32[]{:S(2)}, u32[]{:S(2)}) collective-permute-start(bf16[896,128]{1,0:T(8,128)(2,1)S(1)} %bitcast.61), channel_id=1, source_target_pairs={{0,2},{1,3},{2,4},{3,5},{4,6},{5,7},{6,0},{7,1},{8,10},{9,11},{10,... | collective-permute-start | bytes 688136 | tf_op jit(solution)/shard_map/ppermute | solution.py:372
  191.0 6.1 %collective-permute-start.47 = (bf16[896,128]{1,0:T(8,128)(2,1)S(1)}, bf16[896,128]{1,0:T(8,128)(2,1)S(1)}, u32[]{:S(2)}, u32[]{:S(2)}) collective-permute-start(bf16[896,128]{1,0:T(8,128)(2,1)S(1)} %bitcast.58), channel_id=1, source_target_pairs={{0,6},{1,7},{2,0},{3,1},{4,2},{5,3},{6,4},{7,5},{8,14},{9,15},{10,... | collective-permute-start | bytes 688136 | tf_op jit(solution)/shard_map/ppermute | solution.py:372
  193.6 6.3 %collective-permute-start.44 = (bf16[896,128]{1,0:T(8,128)(2,1)S(1)}, bf16[896,128]{1,0:T(8,128)(2,1)S(1)}, u32[]{:S(2)}, u32[]{:S(2)}) collective-permute-start(bf16[896,128]{1,0:T(8,128)(2,1)S(1)} %bitcast.62), channel_id=1, source_target_pairs={{0,6},{1,7},{2,0},{3,1},{4,2},{5,3},{6,4},{7,5},{8,14},{9,15},{10,... | collective-permute-start | bytes 688136 | tf_op jit(solution)/shard_map/ppermute | solution.py:372
  197.0 6.4 %collective-permute-start.43 = (bf16[896,128]{1,0:T(8,128)(2,1)S(1)}, bf16[896,128]{1,0:T(8,128)(2,1)S(1)}, u32[]{:S(2)}, u32[]{:S(2)}) collective-permute-start(bf16[896,128]{1,0:T(8,128)(2,1)S(1)} %collective-permute-done.42.refs_1_), channel_id=1, source_target_pairs={{0,2},{1,3},{2,4},{3,5},{4,6},{5,7},{6,0},{7,1},{8,10},{9,11},{10,... | collective-permute-start | bytes 688136 | tf_op jit(solution)/shard_map/ppermute | solution.py:372
  197.0 12.8 %collective-permute-start.46 = (bf16[896,128]{1,0:T(8,128)(2,1)S(1)}, bf16[896,128]{1,0:T(8,128)(2,1)S(1)}, u32[]{:S(2)}, u32[]{:S(2)}) collective-permute-start(bf16[896,128]{1,0:T(8,128)(2,1)S(1)} %bitcast.59), channel_id=1, source_target_pairs={{0,2},{1,3},{2,4},{3,5},{4,6},{5,7},{6,0},{7,1},{8,10},{9,11},{10,... | collective-permute-start | bytes 688136 | tf_op jit(solution)/shard_map/ppermute | solution.py:372
  197.0 12.8 %collective-permute-start.48 = (bf16[896,128]{1,0:T(8,128)(2,1)S(1)}, bf16[896,128]{1,0:T(8,128)(2,1)S(1)}, u32[]{:S(2)}, u32[]{:S(2)}) collective-permute-start(bf16[896,128]{1,0:T(8,128)(2,1)S(1)} %collective-permute-done.47.refs_3_), channel_id=1, source_target_pairs={{0,6},{1,7},{2,0},{3,1},{4,2},{5,3},{6,4},{7,5},{8,14},{9,15},{10,... | collective-permute-start | bytes 688136 | tf_op jit(solution)/shard_map/ppermute | solution.py:372
  204.0 12.4 %collective-permute-start.45 = (bf16[4,896,128]{2,1,0:T(8,128)(2,1)S(1)}, bf16[4,896,128]{2,1,0:T(8,128)(2,1)S(1)}, u32[]{:S(2)}, u32[]{:S(2)}) collective-permute-start(bf16[4,896,128]{2,1,0:T(8,128)(2,1)S(1)} %join_y.2.refs_1_), channel_id=1, source_target_pairs={{0,1},{1,0},{2,3},{3,2},{4,5},{5,4},{6,7},{7,6},{8,9},{9,8},{10,11... | collective-permute-start | bytes 2752520 | tf_op jit(solution)/shard_map/ppermute | solution.py:372
  210.5 6.0 %collective-permute-start.49 = (bf16[4,896,128]{2,1,0:T(8,128)(2,1)S(1)}, bf16[4,896,128]{2,1,0:T(8,128)(2,1)}, u32[]{:S(2)}, u32[]{:S(2)}) collective-permute-start(bf16[4,896,128]{2,1,0:T(8,128)(2,1)S(1)} %join_y.3.refs_2_), channel_id=1, source_target_pairs={{0,1},{1,0},{2,3},{3,2},{4,5},{5,4},{6,7},{7,6},{8,9},{9,8},{10,11... | collective-permute-start | bytes 2752520 | tf_op jit(solution)/shard_map/ppermute | solution.py:372
  (4 other events, 49.4 us)

commit v2 on v1

--- a/solution.py
+++ b/solution.py
@@ -381,14 +381,14 @@
 
 
 def last_phases(place, totals):
-    pieces = split(place, totals, [], 2, 2 * PIECE, 4, z_high)
+    pieces = split(place, totals, [], 2, 4 * PIECE, 2, z_low)
+    own = added(F32, pieces[0], send(pieces[1], z_low_step, 1))
+    pieces = split(place, [own], [], 2, PIECE, 4, z_high)
     arrived = [send(pieces[step], z_high_step, step) for step in (2, 1, 3)]
-    own = added(F32, pieces[0], *arrived)
-    pieces = split(place, [own], [], 2, PIECE, 2, z_low)
-    whole = added(BF, pieces[0], send(pieces[1], z_low_step, 1))
-    whole = join(place, [whole, send(whole, z_low_step, 1)], z_low)
+    whole = added(BF, pieces[0], *arrived)
     moved = {step: send(whole, z_high_step, step) for step in (2, 1, 3)}
-    own = join_pair(place, [whole] + [moved[step] for step in range(1, 4)])
+    whole = join(place, [whole] + [moved[step] for step in range(1, 4)], z_high)
+    own = join_pair(place, [whole, send(whole, z_low_step, 1)])
     behind = [send(part, y_step, 1) for part in own]
     ahead = [send(part, y_step, 3) for part in own]
     across = [send(behind[0], y_step, 1), send(ahead[1], y_step, 3)]
@@ -398,25 +398,25 @@
 
 
 def join_pair_kernel(place_ref, *refs):
-    here = z_high(place_ref[0])
-    outs = refs[4:]
-    for step in range(4):
+    here = z_low(place_ref[0])
+    outs = refs[2:]
+    for step in range(2):
         for half in range(2):
-            outs[half][(here - step + 4) % 4] = refs[step][half]
+            outs[half][(here - step + 2) % 2] = refs[step][half]
 
 
 def join_pair(place, pieces):
     rows = pieces[0].shape[1]
-    shape = jax.ShapeDtypeStruct((4, rows, C), BF)
+    shape = jax.ShapeDtypeStruct((2, rows, C), BF)
     joined = pl.pallas_call(
         join_pair_kernel,
         out_shape=[shape, shape],
-        in_specs=[SMEM] + [VMEM] * 4,
+        in_specs=[SMEM] + [VMEM] * 2,
         out_specs=[VMEM] * 2,
         compiler_params=pltpu.CompilerParams(vmem_limit_bytes=8 << 20),
         name="join_pair",
     )(place, *pieces)
-    return [part.reshape(4 * rows, C) for part in joined]
+    return [part.reshape(2 * rows, C) for part in joined]
 
 
 def join_y_kernel(place_ref, *refs):
@@ -440,17 +440,14 @@
     weight_ref, bias_ref = refs[-2:]
 
     def write(ref):
-        def one(index, carry):
-            part, a = index // 3, index % 3
-            rows = pl.ds(pl.multiple_of(part * (C // PARTS), C // PARTS), C // PARTS)
+        first = 9 * pl.program_id(1)
+        for part in range(PARTS):
+            rows = slice(part * (C // PARTS), (part + 1) * (C // PARTS))
             for j in range(9):
-                row = pl.multiple_of((9 * a + j) * (C // PARTS), C // PARTS)
-                weight_ref[0, a, rows, j * C : (j + 1) * C] = ref[
+                row = pl.multiple_of((first + j) * (C // PARTS), C // PARTS)
+                weight_ref[0, 0, rows, j * C : (j + 1) * C] = ref[
                     part, pl.ds(row, C // PARTS), :
                 ].astype(F32)
-            return carry
-
-        lax.fori_loop(0, 3 * PARTS, one, 0)
         bias_ref[0] = ref[0, USED : USED + 16, :].astype(F32)[0:1]
 
     encoder = pl.program_id(0) == 0
@@ -459,7 +456,7 @@
 
 
 def unpack(place, flip, parts, onto=()):
-    def spot(block, place_ref):
+    def spot(block, a, place_ref):
         return 2 * block + (place_ref[0] + flip) % 2
 
     return pl.pallas_call(
@@ -470,10 +467,10 @@
         ],
         grid_spec=pltpu.PrefetchScalarGridSpec(
             num_scalar_prefetch=1,
-            grid=(2,),
+            grid=(2, 3),
             in_specs=[VMEM] * 2 + [ANY] * len(onto),
             out_specs=[
-                pl.BlockSpec((1, 3, C, 9 * C), lambda *at: (spot(*at), 0, 0, 0)),
+                pl.BlockSpec((1, 1, C, 9 * C), lambda *at: (spot(*at), at[1], 0, 0)),
                 pl.BlockSpec((1, 1, C), lambda *at: (spot(*at), 0, 0)),
             ],
         ),

time: 221 us -> 224 us (1.014)
  starting transfers between devices: 89.6 us -> 93.9 us
  waiting for transfers between devices: 86.7 us -> 83.4 us
    ppermute x24, starting transfers between devices: 48.2 us -> 52.5 us  [send(): lax.ppermute(array, 'space', [(place, move(place, step)) for place in ran...]
    ppermute x24, waiting for transfers between devices: 41.9 us -> 38.6 us  [send(): lax.ppermute(array, 'space', [(place, move(place, step)) for place in ran...]
  transfers between devices with their start and end apart: 50 -> 50, of which waited for: 20 -> 17; matrix products, arithmetic and copies ran while one was open for 2% -> 2% of each run, Pallas kernels for 8% -> 8%
where the time goes in v2:
time: 224 us; the launch traced here: 223 us
  starting transfers between devices  93.9 us (42%)
  waiting for transfers between devices  83.4 us (37%)
  Pallas kernels  35.6 us (16%)
  local copies, waits for them, and re-layouts  7.68 us (3%)
    ppermute x24, starting transfers between devices, send(): lax.ppermute(array, 'space', [(place, move(place, step)) for place in ran...  52.5 us
    ppermute x24, waiting for transfers between devices, send(): lax.ppermute(array, 'space', [(place, move(place, step)) for place in ran...  38.6 us
    ppermute x6, waiting for transfers between devices, hand_on(): before = lax.ppermute(high, GRID_AXES, shifted(source_section, by, 1))  35 us
    ppermute x8, starting transfers between devices, beside(): return lax.ppermute(array, 'space', pairs)  23.2 us
    pallas_call x8, Pallas kernels, tick(): pl.pallas_call(lambda *refs: tick_kernel(layer, turn, seeded, *refs), out...  10.1 us
    pallas_call x2, Pallas kernels, forward(): pl.pallas_call(kernel, out_shape=[sds(6, BF), sds(6, BF), sds(6, F32), sd...  8.25 us
    pallas_call x2, Pallas kernels, unpack(): pl.pallas_call(lambda *refs: unpack_kernel(*refs), out_shape=[jax.ShapeDt...  7.96 us
    ppermute x6, starting transfers between devices, hand_on(): middle = lax.ppermute(grad, GRID_AXES, shifted(source_section, by, 0))  7.09 us
  transfers between devices with their start and end apart: 50, of which 17 were waited for; matrix products, arithmetic and copies ran while one was open for 2% of the time, Pallas kernels for 8%

profile of v2, /device:TPU:1, one launch (start us, length us, event | category | flops | bytes accessed | tf_op | source)
XLA Modules:
  0.0 222.8 jit_solution(15197092254035355918)
XLA Ops:
  1.7 5.1 %collective-permute-start.2 = (bf16[256,256]{1,0:T(8,128)(2,1)S(1)}, bf16[256,256]{1,0:T(8,128)(2,1)S(1)}, u32[]{:S(2)}, u32[]{:S(2)}) collective-permute-start(bf16[256,256]{1,0:T(8,128)(2,1)S(1)} %bitcast.62), channel_id=1, source_target_pairs={{1,0},{2,1},{3,2},{4,3},{5,4},{6,5},{7,6},{8,7},{9,8},{10,9},{11,1... | collective-permute-start | bytes 393224 | tf_op jit(solution)/shard_map/ppermute | solution.py:226
  6.8 1.9 collective-permute-start.1
  9.7 2.7 %collective-permute-start = (bf16[128,256]{1,0:T(8,128)(2,1)S(1)}, bf16[128,256]{1,0:T(8,128)(2,1)S(1)}, u32[]{:S(2)}, u32[]{:S(2)}) collective-permute-start(bf16[128,256]{1,0:T(8,128)(2,1)S(1)} %bitcast.89), channel_id=1, source_target_pairs={{0,2},{1,3},{2,4},{3,5},{4,6},{5,7},{6,8},{7,9},{8,10},{9,11},{10,... | collective-permute-start | bytes 196616 | tf_op jit(solution)/shard_map/ppermute | solution.py:226
  12.5 1.3 collective-permute-start.3
  16.0 1.9 collective-permute-start.5
  18.8 3.7 %collective-permute-start.4 = (bf16[512,256]{1,0:T(8,128)(2,1)S(1)}, bf16[512,256]{1,0:T(8,128)(2,1)S(1)}, u32[]{:S(2)}, u32[]{:S(2)}) collective-permute-start(bf16[512,256]{1,0:T(8,128)(2,1)S(1)} %constant_dynamic-update-slice_fusion.own), channel_id=1, source_target_pairs={{0,1},{1,2},{2,3},{3,4},{4,5},{5,6},{6,7},{7,8},{8,9},{9,10},{10,1... | collective-permute-start | bytes 786440 | tf_op jit(solution)/shard_map/ppermute | solution.py:226
  22.5 2.0 copy-done
  24.5 4.7 %shard_map.84 = (bf16[384,256]{1,0:T(8,128)(2,1)S(1)}, bf16[384,256]{1,0:T(8,128)(2,1)S(1)}, f32[384,256]{1,0:T(8,128)S(1)}, f32[512,256]{1,0:T(8,128)S(1)}, bf16[768,256]{1,0:T(8,128)(2,1)S(1)}) custom-call(s32[2]{0:T(128)S(1)} %pad_add_fusion.place_ref.refs_0_, bf16[4,3,128,1152]{3,2,1,0:T(8,128)(2,1)S(1)} %bitcast.66, ...), custom_call_target="tpu_custom_call" | custom-call | flops 3000000000 | bytes 5242880 | tf_op jit(solution)/shard_map/pallas_call | solution.py:128
  29.3 3.6 %shard_map.85 = (bf16[384,256]{1,0:T(8,128)(2,1)S(1)}, bf16[384,256]{1,0:T(8,128)(2,1)S(1)}, f32[384,256]{1,0:T(8,128)S(1)}, f32[512,256]{1,0:T(8,128)S(1)}) custom-call(s32[2]{0:T(128)S(1)} %pad_add_fusion.place_ref.refs_0_, bf16[4,3,128,1152]{3,2,1,0:T(8,128)(2,1)S(1)} %bitcast.67, f32[4,256]{1,0:T(4,128)S(1)} %pad_maximum_fusion.bias_ref, ...), custom_call_target="tpu_custom_call" | custom-call | flops 3000000000 | bytes 5242880 | tf_op jit(solution)/shard_map/pallas_call | solution.py:128
  32.8 2.2 tick.8
  35.0 3.1 %collective-permute-start.7 = (bf16[256,256]{1,0:T(8,128)(2,1)S(1)}, bf16[256,256]{1,0:T(8,128)(2,1)S(1)}, u32[]{:S(2)}, u32[]{:S(2)}) collective-permute-start(bf16[256,256]{1,0:T(8,128)(2,1)S(1)} %get-tuple-element.81.refs_9_), channel_id=1, source_target_pairs={{0,64},{1,65},{2,66},{3,67},{4,68},{5,69},{6,70},{7,71},{8,72},{9,... | collective-permute-start | bytes 393224 | tf_op jit(solution)/shard_map/ppermute | solution.py:218
  38.1 1.6 collective-permute-start.6
  39.8 1.3 collective-permute-start.8
  48.6 4.6 %collective-permute-start.15 = (bf16[128,256]{1,0:T(8,128)(2,1)S(1)}, bf16[128,256]{1,0:T(8,128)(2,1)S(1)}, u32[]{:S(2)}, u32[]{:S(2)}) collective-permute-start(bf16[128,256]{1,0:T(8,128)(2,1)S(1)} %get-tuple-element.95), channel_id=1, source_target_pairs={{0,1},{1,2},{2,3},{3,4},{4,5},{5,6},{6,7},{7,8},{8,9},{9,10},{10,1... | collective-permute-start | bytes 196616 | tf_op jit(solution)/shard_map/ppermute | solution.py:226
  53.2 1.9 collective-permute-start.16
  55.1 3.6 %collective-permute-done.16.refs_6_.refs_9_ = bf16[128,256]{1,0:T(8,128)(2,1)S(1)} collective-permute-done((bf16[128,256]{1,0:T(8,128)(2,1)S(1)}, bf16[128,256]{1,0:T(8,128)(2,1)S(1)}, u32[]{:S(2)}, u32[]{:S(2)}) %collective-permute-start.16) | collective-permute-done | bytes 65568 | tf_op jit(solution)/shard_map/ppermute | solution.py:226
  58.8 2.1 tick.12
  66.4 1.4 collective-permute-start.23
  70.5 1.7 weights.3
  72.3 34.1 %collective-permute-done.23.refs_4_ = bf16[128,256]{1,0:T(8,128)(2,1)S(1)} collective-permute-done((bf16[128,256]{1,0:T(8,128)(2,1)S(1)}, bf16[128,256]{1,0:T(8,128)(2,1)S(1)}, u32[]{:S(2)}, u32[]{:S(2)}) %collective-permute-start.23) | collective-permute-done | bytes 65568 | tf_op jit(solution)/shard_map/ppermute | solution.py:219
  106.4 5.3 %collective-permute-done.25.refs_6_ = bf16[128,256]{1,0:T(8,128)(2,1)S(1)} collective-permute-done((bf16[128,256]{1,0:T(8,128)(2,1)S(1)}, bf16[128,256]{1,0:T(8,128)(2,1)S(1)}, u32[]{:S(2)}, u32[]{:S(2)}) %collective-permute-start.25) | collective-permute-done | bytes 65568 | tf_op jit(solution)/shard_map/ppermute | solution.py:220
  111.9 2.8 %tick.15 = (bf16[256,256]{1,0:T(8,128)(2,1)S(1)}, bf16[256,256]{1,0:T(8,128)(2,1)S(1)}, bf16[256,256]{1,0:T(8,128)(2,1)S(1)}, bf16[128,256]{1,0:T(8,128)(2,1)}, bf16[128,256]{1,0:T(8,128)(2,1)}) custom-call(s32[2]{0:T(128)S(1)} %pad_add_fusion.place_ref.refs_0_, bf16[4,3,128,1152]{3,2,1,0:T(8,128)(2,1)S(1)} %bitcast.75, ...), custom_call_target="tpu_custom_call" | custom-call | flops 3000000000 | bytes 4194304 | tf_op jit(solution)/shard_map/tick/pallas_call | solution.py:188
  114.7 1.7 weights.2
  117.5 5.7 %collective-permute-start.31 = (bf16[1,896,128]{2,1,0:T(8,128)(2,1)S(1)}, bf16[1,896,128]{2,1,0:T(8,128)(2,1)S(1)}, u32[]{:S(2)}, u32[]{:S(2)}) collective-permute-start(bf16[1,896,128]{2,1,0:T(8,128)(2,1)S(1)} %get-tuple-element.131), channel_id=1, source_target_pairs={{0,4},{1,5},{2,6},{3,7},{4,0},{5,1},{6,2},{7,3},{8,12},{9,13},{10,... | collective-permute-start | bytes 688136 | tf_op jit(solution)/shard_map/ppermute | solution.py:372
  123.5 2.3 %collective-permute-start.33 = (bf16[1,896,128]{2,1,0:T(8,128)(2,1)S(1)}, bf16[1,896,128]{2,1,0:T(8,128)(2,1)S(1)}, u32[]{:S(2)}, u32[]{:S(2)}) collective-permute-start(bf16[1,896,128]{2,1,0:T(8,128)(2,1)S(1)} %get-tuple-element.133), channel_id=1, source_target_pairs={{0,6},{1,7},{2,0},{3,1},{4,2},{5,3},{6,4},{7,5},{8,14},{9,15},{10,... | collective-permute-start | bytes 688136 | tf_op jit(solution)/shard_map/ppermute | solution.py:372
  127.4 1.7 collective-permute-done.31.refs_1_
  129.1 2.4 %collective-permute-start.29 = (bf16[1,896,128]{2,1,0:T(8,128)(2,1)S(1)}, bf16[1,896,128]{2,1,0:T(8,128)(2,1)S(1)}, u32[]{:S(2)}, u32[]{:S(2)}) collective-permute-start(bf16[1,896,128]{2,1,0:T(8,128)(2,1)S(1)} %get-tuple-element.123), channel_id=1, source_target_pairs={{0,6},{1,7},{2,0},{3,1},{4,2},{5,3},{6,4},{7,5},{8,14},{9,15},{10,... | collective-permute-start | bytes 688136 | tf_op jit(solution)/shard_map/ppermute | solution.py:372
  131.6 2.7 %collective-permute-done.32.refs_2_ = bf16[1,896,128]{2,1,0:T(8,128)(2,1)S(1)} collective-permute-done((bf16[1,896,128]{2,1,0:T(8,128)(2,1)S(1)}, bf16[1,896,128]{2,1,0:T(8,128)(2,1)S(1)}, u32[]{:S(2)}, u32[]{:S(2)}) %collective-permute-start.32) | collective-permute-done | bytes 229408 | tf_op jit(solution)/shard_map/ppermute | solution.py:372
  134.3 4.7 %collective-permute-done.27.refs_1_ = bf16[1,896,128]{2,1,0:T(8,128)(2,1)S(1)} collective-permute-done((bf16[1,896,128]{2,1,0:T(8,128)(2,1)S(1)}, bf16[1,896,128]{2,1,0:T(8,128)(2,1)S(1)}, u32[]{:S(2)}, u32[]{:S(2)}) %collective-permute-start.27) | collective-permute-done | bytes 229408 | tf_op jit(solution)/shard_map/ppermute | solution.py:372
  139.0 5.0 %collective-permute-done.28.refs_2_ = bf16[1,896,128]{2,1,0:T(8,128)(2,1)S(1)} collective-permute-done((bf16[1,896,128]{2,1,0:T(8,128)(2,1)S(1)}, bf16[1,896,128]{2,1,0:T(8,128)(2,1)S(1)}, u32[]{:S(2)}, u32[]{:S(2)}) %collective-permute-start.28) | collective-permute-done | bytes 229408 | tf_op jit(solution)/shard_map/ppermute | solution.py:372
  144.8 2.2 collective-permute-start.34
  147.0 5.2 %collective-permute-done.34.refs_1_ = bf16[2,448,128]{2,1,0:T(8,128)(2,1)S(1)} collective-permute-done((bf16[2,448,128]{2,1,0:T(8,128)(2,1)S(1)}, bf16[2,448,128]{2,1,0:T(8,128)(2,1)S(1)}, u32[]{:S(2)}, u32[]{:S(2)}) %collective-permute-start.34) | collective-permute-done | bytes 229408 | tf_op jit(solution)/shard_map/ppermute | solution.py:372
  152.8 12.5 %collective-permute-start.35 = (bf16[2,112,128]{2,1,0:T(8,128)(2,1)S(1)}, bf16[2,112,128]{2,1,0:T(8,128)(2,1)S(1)}, u32[]{:S(2)}, u32[]{:S(2)}) collective-permute-start(bf16[2,112,128]{2,1,0:T(8,128)(2,1)S(1)} %get-tuple-element.137), channel_id=1, source_target_pairs={{0,32},{1,33},{2,34},{3,35},{4,36},{5,37},{6,38},{7,39},{8,40},{9,... | collective-permute-start | bytes 172040 | tf_op jit(solution)/shard_map/ppermute | solution.py:372
  165.3 3.6 %collective-permute-start.37 = (bf16[2,112,128]{2,1,0:T(8,128)(2,1)S(1)}, bf16[2,112,128]{2,1,0:T(8,128)(2,1)S(1)}, u32[]{:S(2)}, u32[]{:S(2)}) collective-permute-start(bf16[2,112,128]{2,1,0:T(8,128)(2,1)S(1)} %get-tuple-element.139), channel_id=1, source_target_pairs={{0,48},{1,49},{2,50},{3,51},{4,52},{5,53},{6,54},{7,55},{8,56},{9,... | collective-permute-start | bytes 172040 | tf_op jit(solution)/shard_map/ppermute | solution.py:372
  168.9 2.0 collective-permute-done.36.refs_2_
  170.9 3.8 %collective-permute-start.40 = (bf16[2,112,128]{2,1,0:T(8,128)(2,1)S(1)}, bf16[2,112,128]{2,1,0:T(8,128)(2,1)S(1)}, u32[]{:S(2)}, u32[]{:S(2)}) collective-permute-start(bf16[2,112,128]{2,1,0:T(8,128)(2,1)S(1)} %added.7.refs_1_), channel_id=1, source_target_pairs={{0,48},{1,49},{2,50},{3,51},{4,52},{5,53},{6,54},{7,55},{8,56},{9,... | collective-permute-start | bytes 172040 | tf_op jit(solution)/shard_map/ppermute | solution.py:372
  174.7 1.6 collective-permute-start.39
  176.3 2.3 %collective-permute-start.38 = (bf16[2,112,128]{2,1,0:T(8,128)(2,1)S(1)}, bf16[2,112,128]{2,1,0:T(8,128)(2,1)S(1)}, u32[]{:S(2)}, u32[]{:S(2)}) collective-permute-start(bf16[2,112,128]{2,1,0:T(8,128)(2,1)S(1)} %added.7.refs_1_), channel_id=1, source_target_pairs={{0,16},{1,17},{2,18},{3,19},{4,20},{5,21},{6,22},{7,23},{8,24},{9,... | collective-permute-start | bytes 172040 | tf_op jit(solution)/shard_map/ppermute | solution.py:372
  178.6 3.2 %collective-permute-done.39.refs_3_ = bf16[2,112,128]{2,1,0:T(8,128)(2,1)S(1)} collective-permute-done((bf16[2,112,128]{2,1,0:T(8,128)(2,1)S(1)}, bf16[2,112,128]{2,1,0:T(8,128)(2,1)S(1)}, u32[]{:S(2)}, u32[]{:S(2)}) %collective-permute-start.39) | collective-permute-done | bytes 57376 | tf_op jit(solution)/shard_map/ppermute | solution.py:372
  183.1 4.9 %collective-permute-done.41.refs_1_ = bf16[2,448,128]{2,1,0:T(8,128)(2,1)S(1)} collective-permute-done((bf16[2,448,128]{2,1,0:T(8,128)(2,1)S(1)}, bf16[2,448,128]{2,1,0:T(8,128)(2,1)S(1)}, u32[]{:S(2)}, u32[]{:S(2)}) %collective-permute-start.41) | collective-permute-done | bytes 229408 | tf_op jit(solution)/shard_map/ppermute | solution.py:372
  188.7 2.7 %collective-permute-start.47 = (bf16[896,128]{1,0:T(8,128)(2,1)S(1)}, bf16[896,128]{1,0:T(8,128)(2,1)S(1)}, u32[]{:S(2)}, u32[]{:S(2)}) collective-permute-start(bf16[896,128]{1,0:T(8,128)(2,1)S(1)} %bitcast.56), channel_id=1, source_target_pairs={{0,6},{1,7},{2,0},{3,1},{4,2},{5,3},{6,4},{7,5},{8,14},{9,15},{10,... | collective-permute-start | bytes 688136 | tf_op jit(solution)/shard_map/ppermute | solution.py:372
  191.3 3.4 %collective-permute-done.42.refs_1_ = bf16[896,128]{1,0:T(8,128)(2,1)S(1)} collective-permute-done((bf16[896,128]{1,0:T(8,128)(2,1)S(1)}, bf16[896,128]{1,0:T(8,128)(2,1)S(1)}, u32[]{:S(2)}, u32[]{:S(2)}) %collective-permute-start.42) | collective-permute-done | bytes 229408 | tf_op jit(solution)/shard_map/ppermute | solution.py:372
  194.7 2.7 %collective-permute-start.48 = (bf16[896,128]{1,0:T(8,128)(2,1)S(1)}, bf16[896,128]{1,0:T(8,128)(2,1)S(1)}, u32[]{:S(2)}, u32[]{:S(2)}) collective-permute-start(bf16[896,128]{1,0:T(8,128)(2,1)S(1)} %collective-permute-done.47.refs_3_), channel_id=1, source_target_pairs={{0,6},{1,7},{2,0},{3,1},{4,2},{5,3},{6,4},{7,5},{8,14},{9,15},{10,... | collective-permute-start | bytes 688136 | tf_op jit(solution)/shard_map/ppermute | solution.py:372
  197.4 5.3 %collective-permute-done.43.refs_2_ = bf16[896,128]{1,0:T(8,128)(2,1)S(1)} collective-permute-done((bf16[896,128]{1,0:T(8,128)(2,1)S(1)}, bf16[896,128]{1,0:T(8,128)(2,1)S(1)}, u32[]{:S(2)}, u32[]{:S(2)}) %collective-permute-start.43) | collective-permute-done | bytes 229408 | tf_op jit(solution)/shard_map/ppermute | solution.py:372
  203.4 7.5 %collective-permute-start.45 = (bf16[4,896,128]{2,1,0:T(8,128)(2,1)S(1)}, bf16[4,896,128]{2,1,0:T(8,128)(2,1)S(1)}, u32[]{:S(2)}, u32[]{:S(2)}) collective-permute-start(bf16[4,896,128]{2,1,0:T(8,128)(2,1)S(1)} %join_y.2.refs_1_), channel_id=1, source_target_pairs={{0,1},{1,0},{2,3},{3,2},{4,5},{5,4},{6,7},{7,6},{8,9},{9,8},{10,11... | collective-permute-start | bytes 2752520 | tf_op jit(solution)/shard_map/ppermute | solution.py:372
  211.5 1.8 collective-permute-start.49
  214.8 3.4 %unpack.2 = (f32[4,3,128,1152]{3,2,1,0:T(8,128)}, f32[4,1,128]{2,1,0:T(1,128)}) custom-call(s32[2]{0:T(128)S(1)} %pad_add_fusion.place_ref.refs_0_, bf16[4,896,128]{2,1,0:T(8,128)(2,1)S(1)} %join_y.2.refs_1_, bf16[4,896,128]{2,1,0:T(8,128)(2,1)S(1)} %join_y.3.refs_2_), custom_call_target="tpu_custom_call" | custom-call | tf_op jit(solution)/shard_map/unpack/pallas_call | solution.py:462
  218.2 4.6 %unpack.3 = (f32[4,3,128,1152]{3,2,1,0:T(8,128)}, f32[4,1,128]{2,1,0:T(1,128)}) custom-call(s32[2]{0:T(128)S(1)} %pad_add_fusion.place_ref.refs_0_, bf16[4,896,128]{2,1,0:T(8,128)(2,1)S(1)} %collective-permute-done.45.refs_1_, bf16[4,896,128]{2,1,0:T(8,128)(2,1)} %collective-permute-done.49.refs_2_, ...), custom_call_target="tpu_custom_call", output_to_operand_aliasing={{0}: (3, {}), {1}: (4, {})} | custom-call | tf_op jit(solution)/shard_map/unpack/pallas_call | solution.py:462
  (102 shorter events, 30.0 us)
Async XLA Ops:
  1.7 20.8 %collective-permute-start.2 = (bf16[256,256]{1,0:T(8,128)(2,1)S(1)}, bf16[256,256]{1,0:T(8,128)(2,1)S(1)}, u32[]{:S(2)}, u32[]{:S(2)}) collective-permute-start(bf16[256,256]{1,0:T(8,128)(2,1)S(1)} %bitcast.62), channel_id=1, source_target_pairs={{1,0},{2,1},{3,2},{4,3},{5,4},{6,5},{7,6},{8,7},{9,8},{10,9},{11,1... | collective-permute-start | bytes 393224 | tf_op jit(solution)/shard_map/ppermute | solution.py:226
  6.8 15.7 %collective-permute-start.1 = (bf16[256,256]{1,0:T(8,128)(2,1)S(1)}, bf16[256,256]{1,0:T(8,128)(2,1)S(1)}, u32[]{:S(2)}, u32[]{:S(2)}) collective-permute-start(bf16[256,256]{1,0:T(8,128)(2,1)S(1)} %bitcast.63), channel_id=1, source_target_pairs={{0,1},{1,2},{2,3},{3,4},{4,5},{5,6},{6,7},{7,8},{8,9},{9,10},{10,1... | collective-permute-start | bytes 393224 | tf_op jit(solution)/shard_map/ppermute | solution.py:226
  9.7 9.0 %collective-permute-start = (bf16[128,256]{1,0:T(8,128)(2,1)S(1)}, bf16[128,256]{1,0:T(8,128)(2,1)S(1)}, u32[]{:S(2)}, u32[]{:S(2)}) collective-permute-start(bf16[128,256]{1,0:T(8,128)(2,1)S(1)} %bitcast.89), channel_id=1, source_target_pairs={{0,2},{1,3},{2,4},{3,5},{4,6},{5,7},{6,8},{7,9},{8,10},{9,11},{10,... | collective-permute-start | bytes 196616 | tf_op jit(solution)/shard_map/ppermute | solution.py:226
  12.5 10.0 %collective-permute-start.3 = (bf16[128,256]{1,0:T(8,128)(2,1)S(1)}, bf16[128,256]{1,0:T(8,128)(2,1)S(1)}, u32[]{:S(2)}, u32[]{:S(2)}) collective-permute-start(bf16[128,256]{1,0:T(8,128)(2,1)S(1)} %bitcast.90), channel_id=1, source_target_pairs={{2,0},{3,1},{4,2},{5,3},{6,4},{7,5},{8,6},{9,7},{10,8},{11,9},{12,... | collective-permute-start | bytes 196616 | tf_op jit(solution)/shard_map/ppermute | solution.py:226
  16.0 13.3 %collective-permute-start.5 = (bf16[512,256]{1,0:T(8,128)(2,1)S(1)}, bf16[512,256]{1,0:T(8,128)(2,1)S(1)}, u32[]{:S(2)}, u32[]{:S(2)}) collective-permute-start(bf16[512,256]{1,0:T(8,128)(2,1)S(1)} %constant_dynamic-update-slice_fusion.own), channel_id=1, source_target_pairs={{1,0},{2,1},{3,2},{4,3},{5,4},{6,5},{7,6},{8,7},{9,8},{10,9},{11,1... | collective-permute-start | bytes 786440 | tf_op jit(solution)/shard_map/ppermute | solution.py:226
  18.8 10.5 %collective-permute-start.4 = (bf16[512,256]{1,0:T(8,128)(2,1)S(1)}, bf16[512,256]{1,0:T(8,128)(2,1)S(1)}, u32[]{:S(2)}, u32[]{:S(2)}) collective-permute-start(bf16[512,256]{1,0:T(8,128)(2,1)S(1)} %constant_dynamic-update-slice_fusion.own), channel_id=1, source_target_pairs={{0,1},{1,2},{2,3},{3,4},{4,5},{5,6},{6,7},{7,8},{8,9},{9,10},{10,1... | collective-permute-start | bytes 786440 | tf_op jit(solution)/shard_map/ppermute | solution.py:226
  35.0 7.7 %collective-permute-start.7 = (bf16[256,256]{1,0:T(8,128)(2,1)S(1)}, bf16[256,256]{1,0:T(8,128)(2,1)S(1)}, u32[]{:S(2)}, u32[]{:S(2)}) collective-permute-start(bf16[256,256]{1,0:T(8,128)(2,1)S(1)} %get-tuple-element.81.refs_9_), channel_id=1, source_target_pairs={{0,64},{1,65},{2,66},{3,67},{4,68},{5,69},{6,70},{7,71},{8,72},{9,... | collective-permute-start | bytes 393224 | tf_op jit(solution)/shard_map/ppermute | solution.py:218
  38.1 3.9 %collective-permute-start.6 = (bf16[128,256]{1,0:T(8,128)(2,1)S(1)}, bf16[128,256]{1,0:T(8,128)(2,1)S(1)}, u32[]{:S(2)}, u32[]{:S(2)}) collective-permute-start(bf16[128,256]{1,0:T(8,128)(2,1)S(1)} %get-tuple-element.80.refs_11_), channel_id=1, source_target_pairs={{0,65},{1,66},{2,67},{3,68},{4,69},{5,70},{6,71},{7,72},{8,73},{9,... | collective-permute-start | bytes 196616 | tf_op jit(solution)/shard_map/ppermute | solution.py:219
  39.8 2.9 %collective-permute-start.8 = (bf16[128,256]{1,0:T(8,128)(2,1)S(1)}, bf16[128,256]{1,0:T(8,128)(2,1)S(1)}, u32[]{:S(2)}, u32[]{:S(2)}) collective-permute-start(bf16[128,256]{1,0:T(8,128)(2,1)S(1)} %get-tuple-element.82.refs_10_), channel_id=1, source_target_pairs={{1,64},{2,65},{3,66},{4,67},{5,68},{6,69},{7,70},{8,71},{9,72},{10... | collective-permute-start | bytes 196616 | tf_op jit(solution)/shard_map/ppermute | solution.py:220
  43.3 2.0 collective-permute-start.10
  44.0 1.3 collective-permute-start.9
  44.6 0.7 collective-permute-start.11
  45.9 2.0 collective-permute-start.13
  46.6 1.3 collective-permute-start.12
  48.6 6.5 %collective-permute-start.15 = (bf16[128,256]{1,0:T(8,128)(2,1)S(1)}, bf16[128,256]{1,0:T(8,128)(2,1)S(1)}, u32[]{:S(2)}, u32[]{:S(2)}) collective-permute-start(bf16[128,256]{1,0:T(8,128)(2,1)S(1)} %get-tuple-element.95), channel_id=1, source_target_pairs={{0,1},{1,2},{2,3},{3,4},{4,5},{5,6},{6,7},{7,8},{8,9},{9,10},{10,1... | collective-permute-start | bytes 196616 | tf_op jit(solution)/shard_map/ppermute | solution.py:226
  53.2 5.6 %collective-permute-start.16 = (bf16[128,256]{1,0:T(8,128)(2,1)S(1)}, bf16[128,256]{1,0:T(8,128)(2,1)S(1)}, u32[]{:S(2)}, u32[]{:S(2)}) collective-permute-start(bf16[128,256]{1,0:T(8,128)(2,1)S(1)} %get-tuple-element.97), channel_id=1, source_target_pairs={{1,0},{2,1},{3,2},{4,3},{5,4},{6,5},{7,6},{8,7},{9,8},{10,9},{11,1... | collective-permute-start | bytes 196616 | tf_op jit(solution)/shard_map/ppermute | solution.py:226
  60.9 2.2 collective-permute-start.18
  61.6 1.5 collective-permute-start.17
  62.5 0.7 collective-permute-start.19
  63.8 2.0 collective-permute-start.21
  64.4 1.3 collective-permute-start.20
  66.4 39.9 %collective-permute-start.23 = (bf16[128,256]{1,0:T(8,128)(2,1)S(1)}, bf16[128,256]{1,0:T(8,128)(2,1)S(1)}, u32[]{:S(2)}, u32[]{:S(2)}) collective-permute-start(bf16[128,256]{1,0:T(8,128)(2,1)S(1)} %get-tuple-element.108.refs_14_), channel_id=1, source_target_pairs={{64,1},{65,2},{66,3},{67,4},{68,5},{69,6},{70,7},{71,8},{72,9},{73... | collective-permute-start | bytes 196616 | tf_op jit(solution)/shard_map/ppermute | solution.py:219
  67.9 43.8 %collective-permute-start.25 = (bf16[128,256]{1,0:T(8,128)(2,1)S(1)}, bf16[128,256]{1,0:T(8,128)(2,1)S(1)}, u32[]{:S(2)}, u32[]{:S(2)}) collective-permute-start(bf16[128,256]{1,0:T(8,128)(2,1)S(1)} %get-tuple-element.110.refs_13_), channel_id=1, source_target_pairs={{65,0},{66,1},{67,2},{68,3},{69,4},{70,5},{71,6},{72,7},{73,8},{74... | collective-permute-start | bytes 196616 | tf_op jit(solution)/shard_map/ppermute | solution.py:220
  69.2 42.7 %collective-permute-start.24 = (bf16[256,256]{1,0:T(8,128)(2,1)S(1)}, bf16[256,256]{1,0:T(8,128)(2,1)S(1)}, u32[]{:S(2)}, u32[]{:S(2)}) collective-permute-start(bf16[256,256]{1,0:T(8,128)(2,1)S(1)} %get-tuple-element.109.refs_12_), channel_id=1, source_target_pairs={{64,0},{65,1},{66,2},{67,3},{68,4},{69,5},{70,6},{71,7},{72,8},{73... | collective-permute-start | bytes 393224 | tf_op jit(solution)/shard_map/ppermute | solution.py:218
  72.2 44.3 %collective-permute-start.30 = (bf16[4,896,128]{2,1,0:T(8,128)(2,1)S(1)}, bf16[4,896,128]{2,1,0:T(8,128)(2,1)S(1)}, u32[]{:S(2)}, u32[]{:S(2)}) collective-permute-start(bf16[4,896,128]{2,1,0:T(8,128)(2,1)S(1)} %get-tuple-element.129), channel_id=1, source_target_pairs={{0,1},{1,0},{2,3},{3,2},{4,5},{5,4},{6,7},{7,6},{8,9},{9,8},{10,11... | collective-permute-start | bytes 2752520 | tf_op jit(solution)/shard_map/ppermute | solution.py:372
  116.4 9.4 %collective-permute-start.26 = (bf16[4,896,128]{2,1,0:T(8,128)(2,1)S(1)}, bf16[4,896,128]{2,1,0:T(8,128)(2,1)S(1)}, u32[]{:S(2)}, u32[]{:S(2)}) collective-permute-start(bf16[4,896,128]{2,1,0:T(8,128)(2,1)S(1)} %get-tuple-element.119), channel_id=1, source_target_pairs={{0,1},{1,0},{2,3},{3,2},{4,5},{5,4},{6,7},{7,6},{8,9},{9,8},{10,11... | collective-permute-start | bytes 2752520 | tf_op jit(solution)/shard_map/ppermute | solution.py:372
  117.5 11.7 %collective-permute-start.31 = (bf16[1,896,128]{2,1,0:T(8,128)(2,1)S(1)}, bf16[1,896,128]{2,1,0:T(8,128)(2,1)S(1)}, u32[]{:S(2)}, u32[]{:S(2)}) collective-permute-start(bf16[1,896,128]{2,1,0:T(8,128)(2,1)S(1)} %get-tuple-element.131), channel_id=1, source_target_pairs={{0,4},{1,5},{2,6},{3,7},{4,0},{5,1},{6,2},{7,3},{8,12},{9,13},{10,... | collective-permute-start | bytes 688136 | tf_op jit(solution)/shard_map/ppermute | solution.py:372
  123.1 11.1 %collective-permute-start.32 = (bf16[1,896,128]{2,1,0:T(8,128)(2,1)S(1)}, bf16[1,896,128]{2,1,0:T(8,128)(2,1)S(1)}, u32[]{:S(2)}, u32[]{:S(2)}) collective-permute-start(bf16[1,896,128]{2,1,0:T(8,128)(2,1)S(1)} %get-tuple-element.132), channel_id=1, source_target_pairs={{0,2},{1,3},{2,4},{3,5},{4,6},{5,7},{6,0},{7,1},{8,10},{9,11},{10,... | collective-permute-start | bytes 688136 | tf_op jit(solution)/shard_map/ppermute | solution.py:372
  123.5 10.8 %collective-permute-start.33 = (bf16[1,896,128]{2,1,0:T(8,128)(2,1)S(1)}, bf16[1,896,128]{2,1,0:T(8,128)(2,1)S(1)}, u32[]{:S(2)}, u32[]{:S(2)}) collective-permute-start(bf16[1,896,128]{2,1,0:T(8,128)(2,1)S(1)} %get-tuple-element.133), channel_id=1, source_target_pairs={{0,6},{1,7},{2,0},{3,1},{4,2},{5,3},{6,4},{7,5},{8,14},{9,15},{10,... | collective-permute-start | bytes 688136 | tf_op jit(solution)/shard_map/ppermute | solution.py:372
  126.7 12.3 %collective-permute-start.27 = (bf16[1,896,128]{2,1,0:T(8,128)(2,1)S(1)}, bf16[1,896,128]{2,1,0:T(8,128)(2,1)S(1)}, u32[]{:S(2)}, u32[]{:S(2)}) collective-permute-start(bf16[1,896,128]{2,1,0:T(8,128)(2,1)S(1)} %get-tuple-element.121), channel_id=1, source_target_pairs={{0,4},{1,5},{2,6},{3,7},{4,0},{5,1},{6,2},{7,3},{8,12},{9,13},{10,... | collective-permute-start | bytes 688136 | tf_op jit(solution)/shard_map/ppermute | solution.py:372
  126.8 17.1 %collective-permute-start.28 = (bf16[1,896,128]{2,1,0:T(8,128)(2,1)S(1)}, bf16[1,896,128]{2,1,0:T(8,128)(2,1)S(1)}, u32[]{:S(2)}, u32[]{:S(2)}) collective-permute-start(bf16[1,896,128]{2,1,0:T(8,128)(2,1)S(1)} %get-tuple-element.122), channel_id=1, source_target_pairs={{0,2},{1,3},{2,4},{3,5},{4,6},{5,7},{6,0},{7,1},{8,10},{9,11},{10,... | collective-permute-start | bytes 688136 | tf_op jit(solution)/shard_map/ppermute | solution.py:372
  129.1 14.8 %collective-permute-start.29 = (bf16[1,896,128]{2,1,0:T(8,128)(2,1)S(1)}, bf16[1,896,128]{2,1,0:T(8,128)(2,1)S(1)}, u32[]{:S(2)}, u32[]{:S(2)}) collective-permute-start(bf16[1,896,128]{2,1,0:T(8,128)(2,1)S(1)} %get-tuple-element.123), channel_id=1, source_target_pairs={{0,6},{1,7},{2,0},{3,1},{4,2},{5,3},{6,4},{7,5},{8,14},{9,15},{10,... | collective-permute-start | bytes 688136 | tf_op jit(solution)/shard_map/ppermute | solution.py:372
  144.8 7.4 %collective-permute-start.34 = (bf16[2,448,128]{2,1,0:T(8,128)(2,1)S(1)}, bf16[2,448,128]{2,1,0:T(8,128)(2,1)S(1)}, u32[]{:S(2)}, u32[]{:S(2)}) collective-permute-start(bf16[2,448,128]{2,1,0:T(8,128)(2,1)S(1)} %get-tuple-element.135), channel_id=1, source_target_pairs={{0,8},{1,9},{2,10},{3,11},{4,12},{5,13},{6,14},{7,15},{8,0},{9,1},... | collective-permute-start | bytes 688136 | tf_op jit(solution)/shard_map/ppermute | solution.py:372
  152.8 16.1 %collective-permute-start.35 = (bf16[2,112,128]{2,1,0:T(8,128)(2,1)S(1)}, bf16[2,112,128]{2,1,0:T(8,128)(2,1)S(1)}, u32[]{:S(2)}, u32[]{:S(2)}) collective-permute-start(bf16[2,112,128]{2,1,0:T(8,128)(2,1)S(1)} %get-tuple-element.137), channel_id=1, source_target_pairs={{0,32},{1,33},{2,34},{3,35},{4,36},{5,37},{6,38},{7,39},{8,40},{9,... | collective-permute-start | bytes 172040 | tf_op jit(solution)/shard_map/ppermute | solution.py:372
  165.3 5.6 %collective-permute-start.36 = (bf16[2,112,128]{2,1,0:T(8,128)(2,1)S(1)}, bf16[2,112,128]{2,1,0:T(8,128)(2,1)S(1)}, u32[]{:S(2)}, u32[]{:S(2)}) collective-permute-start(bf16[2,112,128]{2,1,0:T(8,128)(2,1)S(1)} %get-tuple-element.138), channel_id=1, source_target_pairs={{0,16},{1,17},{2,18},{3,19},{4,20},{5,21},{6,22},{7,23},{8,24},{9,... | collective-permute-start | bytes 172040 | tf_op jit(solution)/shard_map/ppermute | solution.py:372
  165.3 5.6 %collective-permute-start.37 = (bf16[2,112,128]{2,1,0:T(8,128)(2,1)S(1)}, bf16[2,112,128]{2,1,0:T(8,128)(2,1)S(1)}, u32[]{:S(2)}, u32[]{:S(2)}) collective-permute-start(bf16[2,112,128]{2,1,0:T(8,128)(2,1)S(1)} %get-tuple-element.139), channel_id=1, source_target_pairs={{0,48},{1,49},{2,50},{3,51},{4,52},{5,53},{6,54},{7,55},{8,56},{9,... | collective-permute-start | bytes 172040 | tf_op jit(solution)/shard_map/ppermute | solution.py:372
  170.9 7.7 %collective-permute-start.40 = (bf16[2,112,128]{2,1,0:T(8,128)(2,1)S(1)}, bf16[2,112,128]{2,1,0:T(8,128)(2,1)S(1)}, u32[]{:S(2)}, u32[]{:S(2)}) collective-permute-start(bf16[2,112,128]{2,1,0:T(8,128)(2,1)S(1)} %added.7.refs_1_), channel_id=1, source_target_pairs={{0,48},{1,49},{2,50},{3,51},{4,52},{5,53},{6,54},{7,55},{8,56},{9,... | collective-permute-start | bytes 172040 | tf_op jit(solution)/shard_map/ppermute | solution.py:372
  174.7 7.0 %collective-permute-start.39 = (bf16[2,112,128]{2,1,0:T(8,128)(2,1)S(1)}, bf16[2,112,128]{2,1,0:T(8,128)(2,1)S(1)}, u32[]{:S(2)}, u32[]{:S(2)}) collective-permute-start(bf16[2,112,128]{2,1,0:T(8,128)(2,1)S(1)} %added.7.refs_1_), channel_id=1, source_target_pairs={{0,32},{1,33},{2,34},{3,35},{4,36},{5,37},{6,38},{7,39},{8,40},{9,... | collective-permute-start | bytes 172040 | tf_op jit(solution)/shard_map/ppermute | solution.py:372
  176.3 6.1 %collective-permute-start.38 = (bf16[2,112,128]{2,1,0:T(8,128)(2,1)S(1)}, bf16[2,112,128]{2,1,0:T(8,128)(2,1)S(1)}, u32[]{:S(2)}, u32[]{:S(2)}) collective-permute-start(bf16[2,112,128]{2,1,0:T(8,128)(2,1)S(1)} %added.7.refs_1_), channel_id=1, source_target_pairs={{0,16},{1,17},{2,18},{3,19},{4,20},{5,21},{6,22},{7,23},{8,24},{9,... | collective-permute-start | bytes 172040 | tf_op jit(solution)/shard_map/ppermute | solution.py:372
  183.0 5.0 %collective-permute-start.41 = (bf16[2,448,128]{2,1,0:T(8,128)(2,1)S(1)}, bf16[2,448,128]{2,1,0:T(8,128)(2,1)S(1)}, u32[]{:S(2)}, u32[]{:S(2)}) collective-permute-start(bf16[2,448,128]{2,1,0:T(8,128)(2,1)S(1)} %bitcast.54), channel_id=1, source_target_pairs={{0,8},{1,9},{2,10},{3,11},{4,12},{5,13},{6,14},{7,15},{8,0},{9,1},... | collective-permute-start | bytes 688136 | tf_op jit(solution)/shard_map/ppermute | solution.py:372
  188.6 6.2 %collective-permute-start.42 = (bf16[896,128]{1,0:T(8,128)(2,1)S(1)}, bf16[896,128]{1,0:T(8,128)(2,1)S(1)}, u32[]{:S(2)}, u32[]{:S(2)}) collective-permute-start(bf16[896,128]{1,0:T(8,128)(2,1)S(1)} %bitcast.59), channel_id=1, source_target_pairs={{0,2},{1,3},{2,4},{3,5},{4,6},{5,7},{6,0},{7,1},{8,10},{9,11},{10,... | collective-permute-start | bytes 688136 | tf_op jit(solution)/shard_map/ppermute | solution.py:372
  188.7 6.1 %collective-permute-start.47 = (bf16[896,128]{1,0:T(8,128)(2,1)S(1)}, bf16[896,128]{1,0:T(8,128)(2,1)S(1)}, u32[]{:S(2)}, u32[]{:S(2)}) collective-permute-start(bf16[896,128]{1,0:T(8,128)(2,1)S(1)} %bitcast.56), channel_id=1, source_target_pairs={{0,6},{1,7},{2,0},{3,1},{4,2},{5,3},{6,4},{7,5},{8,14},{9,15},{10,... | collective-permute-start | bytes 688136 | tf_op jit(solution)/shard_map/ppermute | solution.py:372
  191.3 6.1 %collective-permute-start.44 = (bf16[896,128]{1,0:T(8,128)(2,1)S(1)}, bf16[896,128]{1,0:T(8,128)(2,1)S(1)}, u32[]{:S(2)}, u32[]{:S(2)}) collective-permute-start(bf16[896,128]{1,0:T(8,128)(2,1)S(1)} %bitcast.60), channel_id=1, source_target_pairs={{0,6},{1,7},{2,0},{3,1},{4,2},{5,3},{6,4},{7,5},{8,14},{9,15},{10,... | collective-permute-start | bytes 688136 | tf_op jit(solution)/shard_map/ppermute | solution.py:372
  194.7 8.0 %collective-permute-start.43 = (bf16[896,128]{1,0:T(8,128)(2,1)S(1)}, bf16[896,128]{1,0:T(8,128)(2,1)S(1)}, u32[]{:S(2)}, u32[]{:S(2)}) collective-permute-start(bf16[896,128]{1,0:T(8,128)(2,1)S(1)} %collective-permute-done.42.refs_1_), channel_id=1, source_target_pairs={{0,2},{1,3},{2,4},{3,5},{4,6},{5,7},{6,0},{7,1},{8,10},{9,11},{10,... | collective-permute-start | bytes 688136 | tf_op jit(solution)/shard_map/ppermute | solution.py:372
  194.7 16.2 %collective-permute-start.46 = (bf16[896,128]{1,0:T(8,128)(2,1)S(1)}, bf16[896,128]{1,0:T(8,128)(2,1)S(1)}, u32[]{:S(2)}, u32[]{:S(2)}) collective-permute-start(bf16[896,128]{1,0:T(8,128)(2,1)S(1)} %bitcast.57), channel_id=1, source_target_pairs={{0,2},{1,3},{2,4},{3,5},{4,6},{5,7},{6,0},{7,1},{8,10},{9,11},{10,... | collective-permute-start | bytes 688136 | tf_op jit(solution)/shard_map/ppermute | solution.py:372
  194.7 16.2 %collective-permute-start.48 = (bf16[896,128]{1,0:T(8,128)(2,1)S(1)}, bf16[896,128]{1,0:T(8,128)(2,1)S(1)}, u32[]{:S(2)}, u32[]{:S(2)}) collective-permute-start(bf16[896,128]{1,0:T(8,128)(2,1)S(1)} %collective-permute-done.47.refs_3_), channel_id=1, source_target_pairs={{0,6},{1,7},{2,0},{3,1},{4,2},{5,3},{6,4},{7,5},{8,14},{9,15},{10,... | collective-permute-start | bytes 688136 | tf_op jit(solution)/shard_map/ppermute | solution.py:372
  203.4 14.8 %collective-permute-start.45 = (bf16[4,896,128]{2,1,0:T(8,128)(2,1)S(1)}, bf16[4,896,128]{2,1,0:T(8,128)(2,1)S(1)}, u32[]{:S(2)}, u32[]{:S(2)}) collective-permute-start(bf16[4,896,128]{2,1,0:T(8,128)(2,1)S(1)} %join_y.2.refs_1_), channel_id=1, source_target_pairs={{0,1},{1,0},{2,3},{3,2},{4,5},{5,4},{6,7},{7,6},{8,9},{9,8},{10,11... | collective-permute-start | bytes 2752520 | tf_op jit(solution)/shard_map/ppermute | solution.py:372
  211.5 6.6 %collective-permute-start.49 = (bf16[4,896,128]{2,1,0:T(8,128)(2,1)S(1)}, bf16[4,896,128]{2,1,0:T(8,128)(2,1)}, u32[]{:S(2)}, u32[]{:S(2)}) collective-permute-start(bf16[4,896,128]{2,1,0:T(8,128)(2,1)S(1)} %join_y.3.refs_2_), channel_id=1, source_target_pairs={{0,1},{1,0},{2,3},{3,2},{4,5},{5,4},{6,7},{7,6},{8,9},{9,8},{10,11... | collective-permute-start | bytes 2752520 | tf_op jit(solution)/shard_map/ppermute | solution.py:372
  (4 other events, 49.4 us)

commit v3 on v2

--- a/solution.py
+++ b/solution.py
@@ -440,14 +440,17 @@
     weight_ref, bias_ref = refs[-2:]
 
     def write(ref):
-        first = 9 * pl.program_id(1)
-        for part in range(PARTS):
-            rows = slice(part * (C // PARTS), (part + 1) * (C // PARTS))
+        def one(index, carry):
+            part, a = index // 3, index % 3
+            rows = pl.ds(pl.multiple_of(part * (C // PARTS), C // PARTS), C // PARTS)
             for j in range(9):
-                row = pl.multiple_of((first + j) * (C // PARTS), C // PARTS)
-                weight_ref[0, 0, rows, j * C : (j + 1) * C] = ref[
+                row = pl.multiple_of((9 * a + j) * (C // PARTS), C // PARTS)
+                weight_ref[0, a, rows, j * C : (j + 1) * C] = ref[
                     part, pl.ds(row, C // PARTS), :
                 ].astype(F32)
+            return carry
+
+        lax.fori_loop(0, 3 * PARTS, one, 0)
         bias_ref[0] = ref[0, USED : USED + 16, :].astype(F32)[0:1]
 
     encoder = pl.program_id(0) == 0
@@ -456,7 +459,7 @@
 
 
 def unpack(place, flip, parts, onto=()):
-    def spot(block, a, place_ref):
+    def spot(block, place_ref):
         return 2 * block + (place_ref[0] + flip) % 2
 
     return pl.pallas_call(
@@ -467,10 +470,10 @@
         ],
         grid_spec=pltpu.PrefetchScalarGridSpec(
             num_scalar_prefetch=1,
-            grid=(2, 3),
+            grid=(2,),
             in_specs=[VMEM] * 2 + [ANY] * len(onto),
             out_specs=[
-                pl.BlockSpec((1, 1, C, 9 * C), lambda *at: (spot(*at), at[1], 0, 0)),
+                pl.BlockSpec((1, 3, C, 9 * C), lambda *at: (spot(*at), 0, 0, 0)),
                 pl.BlockSpec((1, 1, C), lambda *at: (spot(*at), 0, 0)),
             ],
         ),
@@ -530,13 +533,14 @@
             dec_total = first_phases(place, (upper[1], dec_v, upper[0], dec_h))
         state = tick(0, turn, place, kernels, slopes, cot, skip=skip, state=state)
     enc_total = first_phases(place, (state[1], enc_v, state[0], enc_h))
+    encoder_grad, upper_grad = from_cells(state[2]), from_cells(upper[2])
     mine = last_phases(place, [enc_total, dec_total])
     other = [send(part, core_step, 1) for part in mine]
     totals = unpack(place, 0, mine)
     weight_total, bias_total = unpack(place, 1, other, totals)
     return (
-        from_cells(state[2]),
-        from_cells(upper[2]),
+        encoder_grad,
+        upper_grad,
         weight_total[None],
         bias_total.reshape(1, 4, C),
     )

time: 224 us -> 222 us (level)
  no operation moved by 1% of the time
where the time goes in v3:
time: 222 us; the launch traced here: 221 us
  starting transfers between devices  93.9 us (42%)
  waiting for transfers between devices  83.4 us (38%)
  Pallas kernels  34.2 us (15%)
  local copies, waits for them, and re-layouts  7.68 us (3%)
    ppermute x24, starting transfers between devices, send(): lax.ppermute(array, 'space', [(place, move(place, step)) for place in ran...  52.5 us
    ppermute x24, waiting for transfers between devices, send(): lax.ppermute(array, 'space', [(place, move(place, step)) for place in ran...  38.6 us
    ppermute x6, waiting for transfers between devices, hand_on(): before = lax.ppermute(high, GRID_AXES, shifted(source_section, by, 1))  35 us
    ppermute x8, starting transfers between devices, beside(): return lax.ppermute(array, 'space', pairs)  23.2 us
    pallas_call x8, Pallas kernels, tick(): pl.pallas_call(lambda *refs: tick_kernel(layer, turn, seeded, *refs), out...  10.1 us
    pallas_call x2, Pallas kernels, forward(): pl.pallas_call(kernel, out_shape=[sds(6, BF), sds(6, BF), sds(6, F32), sd...  8.25 us
    ppermute x6, starting transfers between devices, hand_on(): middle = lax.ppermute(grad, GRID_AXES, shifted(source_section, by, 0))  7.09 us
    pallas_call x2, Pallas kernels, unpack(): pl.pallas_call(lambda *refs: unpack_kernel(*refs), out_shape=[jax.ShapeDt...  6.61 us
  transfers between devices with their start and end apart: 50, of which 17 were waited for; matrix products, arithmetic and copies ran while one was open for 2% of the time, Pallas kernels for 8%

profile of v3, /device:TPU:1, one launch (start us, length us, event | category | flops | bytes accessed | tf_op | source)
XLA Modules:
  0.0 221.4 jit_solution(1161581525217445580)
XLA Ops:
  1.7 5.1 %collective-permute-start.2 = (bf16[256,256]{1,0:T(8,128)(2,1)S(1)}, bf16[256,256]{1,0:T(8,128)(2,1)S(1)}, u32[]{:S(2)}, u32[]{:S(2)}) collective-permute-start(bf16[256,256]{1,0:T(8,128)(2,1)S(1)} %bitcast.62), channel_id=1, source_target_pairs={{1,0},{2,1},{3,2},{4,3},{5,4},{6,5},{7,6},{8,7},{9,8},{10,9},{11,1... | collective-permute-start | bytes 393224 | tf_op jit(solution)/shard_map/ppermute | solution.py:226
  6.8 1.9 collective-permute-start.1
  9.7 2.7 %collective-permute-start = (bf16[128,256]{1,0:T(8,128)(2,1)S(1)}, bf16[128,256]{1,0:T(8,128)(2,1)S(1)}, u32[]{:S(2)}, u32[]{:S(2)}) collective-permute-start(bf16[128,256]{1,0:T(8,128)(2,1)S(1)} %bitcast.89), channel_id=1, source_target_pairs={{0,2},{1,3},{2,4},{3,5},{4,6},{5,7},{6,8},{7,9},{8,10},{9,11},{10,... | collective-permute-start | bytes 196616 | tf_op jit(solution)/shard_map/ppermute | solution.py:226
  12.5 1.3 collective-permute-start.3
  16.0 1.9 collective-permute-start.5
  18.8 3.7 %collective-permute-start.4 = (bf16[512,256]{1,0:T(8,128)(2,1)S(1)}, bf16[512,256]{1,0:T(8,128)(2,1)S(1)}, u32[]{:S(2)}, u32[]{:S(2)}) collective-permute-start(bf16[512,256]{1,0:T(8,128)(2,1)S(1)} %constant_dynamic-update-slice_fusion.own), channel_id=1, source_target_pairs={{0,1},{1,2},{2,3},{3,4},{4,5},{5,6},{6,7},{7,8},{8,9},{9,10},{10,1... | collective-permute-start | bytes 786440 | tf_op jit(solution)/shard_map/ppermute | solution.py:226
  22.5 2.0 copy-done
  24.5 4.7 %shard_map.84 = (bf16[384,256]{1,0:T(8,128)(2,1)S(1)}, bf16[384,256]{1,0:T(8,128)(2,1)S(1)}, f32[384,256]{1,0:T(8,128)S(1)}, f32[512,256]{1,0:T(8,128)S(1)}, bf16[768,256]{1,0:T(8,128)(2,1)S(1)}) custom-call(s32[2]{0:T(128)S(1)} %pad_add_fusion.place_ref.refs_0_, bf16[4,3,128,1152]{3,2,1,0:T(8,128)(2,1)S(1)} %bitcast.66, ...), custom_call_target="tpu_custom_call" | custom-call | flops 3000000000 | bytes 5242880 | tf_op jit(solution)/shard_map/pallas_call | solution.py:128
  29.3 3.6 %shard_map.85 = (bf16[384,256]{1,0:T(8,128)(2,1)S(1)}, bf16[384,256]{1,0:T(8,128)(2,1)S(1)}, f32[384,256]{1,0:T(8,128)S(1)}, f32[512,256]{1,0:T(8,128)S(1)}) custom-call(s32[2]{0:T(128)S(1)} %pad_add_fusion.place_ref.refs_0_, bf16[4,3,128,1152]{3,2,1,0:T(8,128)(2,1)S(1)} %bitcast.67, f32[4,256]{1,0:T(4,128)S(1)} %pad_maximum_fusion.bias_ref, ...), custom_call_target="tpu_custom_call" | custom-call | flops 3000000000 | bytes 5242880 | tf_op jit(solution)/shard_map/pallas_call | solution.py:128
  32.8 2.2 tick.8
  35.0 3.1 %collective-permute-start.7 = (bf16[256,256]{1,0:T(8,128)(2,1)S(1)}, bf16[256,256]{1,0:T(8,128)(2,1)S(1)}, u32[]{:S(2)}, u32[]{:S(2)}) collective-permute-start(bf16[256,256]{1,0:T(8,128)(2,1)S(1)} %get-tuple-element.81.refs_9_), channel_id=1, source_target_pairs={{0,64},{1,65},{2,66},{3,67},{4,68},{5,69},{6,70},{7,71},{8,72},{9,... | collective-permute-start | bytes 393224 | tf_op jit(solution)/shard_map/ppermute | solution.py:218
  38.1 1.6 collective-permute-start.6
  39.8 1.3 collective-permute-start.8
  48.6 4.6 %collective-permute-start.15 = (bf16[128,256]{1,0:T(8,128)(2,1)S(1)}, bf16[128,256]{1,0:T(8,128)(2,1)S(1)}, u32[]{:S(2)}, u32[]{:S(2)}) collective-permute-start(bf16[128,256]{1,0:T(8,128)(2,1)S(1)} %get-tuple-element.95), channel_id=1, source_target_pairs={{0,1},{1,2},{2,3},{3,4},{4,5},{5,6},{6,7},{7,8},{8,9},{9,10},{10,1... | collective-permute-start | bytes 196616 | tf_op jit(solution)/shard_map/ppermute | solution.py:226
  53.2 1.9 collective-permute-start.16
  55.1 3.6 %collective-permute-done.16.refs_6_.refs_9_ = bf16[128,256]{1,0:T(8,128)(2,1)S(1)} collective-permute-done((bf16[128,256]{1,0:T(8,128)(2,1)S(1)}, bf16[128,256]{1,0:T(8,128)(2,1)S(1)}, u32[]{:S(2)}, u32[]{:S(2)}) %collective-permute-start.16) | collective-permute-done | bytes 65568 | tf_op jit(solution)/shard_map/ppermute | solution.py:226
  58.8 2.1 tick.12
  66.4 1.4 collective-permute-start.23
  70.5 1.7 weights.3
  72.3 34.1 %collective-permute-done.23.refs_4_ = bf16[128,256]{1,0:T(8,128)(2,1)S(1)} collective-permute-done((bf16[128,256]{1,0:T(8,128)(2,1)S(1)}, bf16[128,256]{1,0:T(8,128)(2,1)S(1)}, u32[]{:S(2)}, u32[]{:S(2)}) %collective-permute-start.23) | collective-permute-done | bytes 65568 | tf_op jit(solution)/shard_map/ppermute | solution.py:219
  106.4 5.3 %collective-permute-done.25.refs_6_ = bf16[128,256]{1,0:T(8,128)(2,1)S(1)} collective-permute-done((bf16[128,256]{1,0:T(8,128)(2,1)S(1)}, bf16[128,256]{1,0:T(8,128)(2,1)S(1)}, u32[]{:S(2)}, u32[]{:S(2)}) %collective-permute-start.25) | collective-permute-done | bytes 65568 | tf_op jit(solution)/shard_map/ppermute | solution.py:220
  111.9 2.8 %tick.15 = (bf16[256,256]{1,0:T(8,128)(2,1)S(1)}, bf16[256,256]{1,0:T(8,128)(2,1)S(1)}, bf16[256,256]{1,0:T(8,128)(2,1)S(1)}, bf16[128,256]{1,0:T(8,128)(2,1)}, bf16[128,256]{1,0:T(8,128)(2,1)}) custom-call(s32[2]{0:T(128)S(1)} %pad_add_fusion.place_ref.refs_0_, bf16[4,3,128,1152]{3,2,1,0:T(8,128)(2,1)S(1)} %bitcast.75, ...), custom_call_target="tpu_custom_call" | custom-call | flops 3000000000 | bytes 4194304 | tf_op jit(solution)/shard_map/tick/pallas_call | solution.py:188
  114.7 1.7 weights.2
  117.5 5.7 %collective-permute-start.31 = (bf16[1,896,128]{2,1,0:T(8,128)(2,1)S(1)}, bf16[1,896,128]{2,1,0:T(8,128)(2,1)S(1)}, u32[]{:S(2)}, u32[]{:S(2)}) collective-permute-start(bf16[1,896,128]{2,1,0:T(8,128)(2,1)S(1)} %get-tuple-element.131), channel_id=1, source_target_pairs={{0,4},{1,5},{2,6},{3,7},{4,0},{5,1},{6,2},{7,3},{8,12},{9,13},{10,... | collective-permute-start | bytes 688136 | tf_op jit(solution)/shard_map/ppermute | solution.py:372
  123.5 2.3 %collective-permute-start.33 = (bf16[1,896,128]{2,1,0:T(8,128)(2,1)S(1)}, bf16[1,896,128]{2,1,0:T(8,128)(2,1)S(1)}, u32[]{:S(2)}, u32[]{:S(2)}) collective-permute-start(bf16[1,896,128]{2,1,0:T(8,128)(2,1)S(1)} %get-tuple-element.133), channel_id=1, source_target_pairs={{0,6},{1,7},{2,0},{3,1},{4,2},{5,3},{6,4},{7,5},{8,14},{9,15},{10,... | collective-permute-start | bytes 688136 | tf_op jit(solution)/shard_map/ppermute | solution.py:372
  127.4 1.7 collective-permute-done.31.refs_1_
  129.1 2.4 %collective-permute-start.29 = (bf16[1,896,128]{2,1,0:T(8,128)(2,1)S(1)}, bf16[1,896,128]{2,1,0:T(8,128)(2,1)S(1)}, u32[]{:S(2)}, u32[]{:S(2)}) collective-permute-start(bf16[1,896,128]{2,1,0:T(8,128)(2,1)S(1)} %get-tuple-element.123), channel_id=1, source_target_pairs={{0,6},{1,7},{2,0},{3,1},{4,2},{5,3},{6,4},{7,5},{8,14},{9,15},{10,... | collective-permute-start | bytes 688136 | tf_op jit(solution)/shard_map/ppermute | solution.py:372
  131.6 2.7 %collective-permute-done.32.refs_2_ = bf16[1,896,128]{2,1,0:T(8,128)(2,1)S(1)} collective-permute-done((bf16[1,896,128]{2,1,0:T(8,128)(2,1)S(1)}, bf16[1,896,128]{2,1,0:T(8,128)(2,1)S(1)}, u32[]{:S(2)}, u32[]{:S(2)}) %collective-permute-start.32) | collective-permute-done | bytes 229408 | tf_op jit(solution)/shard_map/ppermute | solution.py:372
  134.3 4.7 %collective-permute-done.27.refs_1_ = bf16[1,896,128]{2,1,0:T(8,128)(2,1)S(1)} collective-permute-done((bf16[1,896,128]{2,1,0:T(8,128)(2,1)S(1)}, bf16[1,896,128]{2,1,0:T(8,128)(2,1)S(1)}, u32[]{:S(2)}, u32[]{:S(2)}) %collective-permute-start.27) | collective-permute-done | bytes 229408 | tf_op jit(solution)/shard_map/ppermute | solution.py:372
  139.0 5.0 %collective-permute-done.28.refs_2_ = bf16[1,896,128]{2,1,0:T(8,128)(2,1)S(1)} collective-permute-done((bf16[1,896,128]{2,1,0:T(8,128)(2,1)S(1)}, bf16[1,896,128]{2,1,0:T(8,128)(2,1)S(1)}, u32[]{:S(2)}, u32[]{:S(2)}) %collective-permute-start.28) | collective-permute-done | bytes 229408 | tf_op jit(solution)/shard_map/ppermute | solution.py:372
  144.8 2.2 collective-permute-start.34
  147.0 5.2 %collective-permute-done.34.refs_1_ = bf16[2,448,128]{2,1,0:T(8,128)(2,1)S(1)} collective-permute-done((bf16[2,448,128]{2,1,0:T(8,128)(2,1)S(1)}, bf16[2,448,128]{2,1,0:T(8,128)(2,1)S(1)}, u32[]{:S(2)}, u32[]{:S(2)}) %collective-permute-start.34) | collective-permute-done | bytes 229408 | tf_op jit(solution)/shard_map/ppermute | solution.py:372
  152.8 12.5 %collective-permute-start.35 = (bf16[2,112,128]{2,1,0:T(8,128)(2,1)S(1)}, bf16[2,112,128]{2,1,0:T(8,128)(2,1)S(1)}, u32[]{:S(2)}, u32[]{:S(2)}) collective-permute-start(bf16[2,112,128]{2,1,0:T(8,128)(2,1)S(1)} %get-tuple-element.137), channel_id=1, source_target_pairs={{0,32},{1,33},{2,34},{3,35},{4,36},{5,37},{6,38},{7,39},{8,40},{9,... | collective-permute-start | bytes 172040 | tf_op jit(solution)/shard_map/ppermute | solution.py:372
  165.3 3.6 %collective-permute-start.37 = (bf16[2,112,128]{2,1,0:T(8,128)(2,1)S(1)}, bf16[2,112,128]{2,1,0:T(8,128)(2,1)S(1)}, u32[]{:S(2)}, u32[]{:S(2)}) collective-permute-start(bf16[2,112,128]{2,1,0:T(8,128)(2,1)S(1)} %get-tuple-element.139), channel_id=1, source_target_pairs={{0,48},{1,49},{2,50},{3,51},{4,52},{5,53},{6,54},{7,55},{8,56},{9,... | collective-permute-start | bytes 172040 | tf_op jit(solution)/shard_map/ppermute | solution.py:372
  168.9 2.0 collective-permute-done.36.refs_2_
  170.9 3.8 %collective-permute-start.40 = (bf16[2,112,128]{2,1,0:T(8,128)(2,1)S(1)}, bf16[2,112,128]{2,1,0:T(8,128)(2,1)S(1)}, u32[]{:S(2)}, u32[]{:S(2)}) collective-permute-start(bf16[2,112,128]{2,1,0:T(8,128)(2,1)S(1)} %added.7.refs_1_), channel_id=1, source_target_pairs={{0,48},{1,49},{2,50},{3,51},{4,52},{5,53},{6,54},{7,55},{8,56},{9,... | collective-permute-start | bytes 172040 | tf_op jit(solution)/shard_map/ppermute | solution.py:372
  174.7 1.6 collective-permute-start.39
  176.3 2.3 %collective-permute-start.38 = (bf16[2,112,128]{2,1,0:T(8,128)(2,1)S(1)}, bf16[2,112,128]{2,1,0:T(8,128)(2,1)S(1)}, u32[]{:S(2)}, u32[]{:S(2)}) collective-permute-start(bf16[2,112,128]{2,1,0:T(8,128)(2,1)S(1)} %added.7.refs_1_), channel_id=1, source_target_pairs={{0,16},{1,17},{2,18},{3,19},{4,20},{5,21},{6,22},{7,23},{8,24},{9,... | collective-permute-start | bytes 172040 | tf_op jit(solution)/shard_map/ppermute | solution.py:372
  178.6 3.2 %collective-permute-done.39.refs_3_ = bf16[2,112,128]{2,1,0:T(8,128)(2,1)S(1)} collective-permute-done((bf16[2,112,128]{2,1,0:T(8,128)(2,1)S(1)}, bf16[2,112,128]{2,1,0:T(8,128)(2,1)S(1)}, u32[]{:S(2)}, u32[]{:S(2)}) %collective-permute-start.39) | collective-permute-done | bytes 57376 | tf_op jit(solution)/shard_map/ppermute | solution.py:372
  183.1 4.9 %collective-permute-done.41.refs_1_ = bf16[2,448,128]{2,1,0:T(8,128)(2,1)S(1)} collective-permute-done((bf16[2,448,128]{2,1,0:T(8,128)(2,1)S(1)}, bf16[2,448,128]{2,1,0:T(8,128)(2,1)S(1)}, u32[]{:S(2)}, u32[]{:S(2)}) %collective-permute-start.41) | collective-permute-done | bytes 229408 | tf_op jit(solution)/shard_map/ppermute | solution.py:372
  188.7 2.7 %collective-permute-start.47 = (bf16[896,128]{1,0:T(8,128)(2,1)S(1)}, bf16[896,128]{1,0:T(8,128)(2,1)S(1)}, u32[]{:S(2)}, u32[]{:S(2)}) collective-permute-start(bf16[896,128]{1,0:T(8,128)(2,1)S(1)} %bitcast.56), channel_id=1, source_target_pairs={{0,6},{1,7},{2,0},{3,1},{4,2},{5,3},{6,4},{7,5},{8,14},{9,15},{10,... | collective-permute-start | bytes 688136 | tf_op jit(solution)/shard_map/ppermute | solution.py:372
  191.3 3.4 %collective-permute-done.42.refs_1_ = bf16[896,128]{1,0:T(8,128)(2,1)S(1)} collective-permute-done((bf16[896,128]{1,0:T(8,128)(2,1)S(1)}, bf16[896,128]{1,0:T(8,128)(2,1)S(1)}, u32[]{:S(2)}, u32[]{:S(2)}) %collective-permute-start.42) | collective-permute-done | bytes 229408 | tf_op jit(solution)/shard_map/ppermute | solution.py:372
  194.7 2.7 %collective-permute-start.48 = (bf16[896,128]{1,0:T(8,128)(2,1)S(1)}, bf16[896,128]{1,0:T(8,128)(2,1)S(1)}, u32[]{:S(2)}, u32[]{:S(2)}) collective-permute-start(bf16[896,128]{1,0:T(8,128)(2,1)S(1)} %collective-permute-done.47.refs_3_), channel_id=1, source_target_pairs={{0,6},{1,7},{2,0},{3,1},{4,2},{5,3},{6,4},{7,5},{8,14},{9,15},{10,... | collective-permute-start | bytes 688136 | tf_op jit(solution)/shard_map/ppermute | solution.py:372
  197.4 5.3 %collective-permute-done.43.refs_2_ = bf16[896,128]{1,0:T(8,128)(2,1)S(1)} collective-permute-done((bf16[896,128]{1,0:T(8,128)(2,1)S(1)}, bf16[896,128]{1,0:T(8,128)(2,1)S(1)}, u32[]{:S(2)}, u32[]{:S(2)}) %collective-permute-start.43) | collective-permute-done | bytes 229408 | tf_op jit(solution)/shard_map/ppermute | solution.py:372
  203.4 7.5 %collective-permute-start.45 = (bf16[4,896,128]{2,1,0:T(8,128)(2,1)S(1)}, bf16[4,896,128]{2,1,0:T(8,128)(2,1)S(1)}, u32[]{:S(2)}, u32[]{:S(2)}) collective-permute-start(bf16[4,896,128]{2,1,0:T(8,128)(2,1)S(1)} %join_y.2.refs_1_), channel_id=1, source_target_pairs={{0,1},{1,0},{2,3},{3,2},{4,5},{5,4},{6,7},{7,6},{8,9},{9,8},{10,11... | collective-permute-start | bytes 2752520 | tf_op jit(solution)/shard_map/ppermute | solution.py:372
  211.5 1.8 collective-permute-start.49
  214.8 2.7 %unpack.2 = (f32[4,3,128,1152]{3,2,1,0:T(8,128)}, f32[4,1,128]{2,1,0:T(1,128)}) custom-call(s32[2]{0:T(128)S(1)} %pad_add_fusion.place_ref.refs_0_, bf16[4,896,128]{2,1,0:T(8,128)(2,1)S(1)} %join_y.2.refs_1_, bf16[4,896,128]{2,1,0:T(8,128)(2,1)S(1)} %join_y.3.refs_2_), custom_call_target="tpu_custom_call" | custom-call | tf_op jit(solution)/shard_map/unpack/pallas_call | solution.py:465
  217.5 3.9 %unpack.3 = (f32[4,3,128,1152]{3,2,1,0:T(8,128)}, f32[4,1,128]{2,1,0:T(1,128)}) custom-call(s32[2]{0:T(128)S(1)} %pad_add_fusion.place_ref.refs_0_, bf16[4,896,128]{2,1,0:T(8,128)(2,1)S(1)} %collective-permute-done.45.refs_1_, bf16[4,896,128]{2,1,0:T(8,128)(2,1)} %collective-permute-done.49.refs_2_, ...), custom_call_target="tpu_custom_call", output_to_operand_aliasing={{0}: (3, {}), {1}: (4, {})} | custom-call | tf_op jit(solution)/shard_map/unpack/pallas_call | solution.py:465
  (102 shorter events, 30.0 us)
Async XLA Ops:
  1.7 20.8 %collective-permute-start.2 = (bf16[256,256]{1,0:T(8,128)(2,1)S(1)}, bf16[256,256]{1,0:T(8,128)(2,1)S(1)}, u32[]{:S(2)}, u32[]{:S(2)}) collective-permute-start(bf16[256,256]{1,0:T(8,128)(2,1)S(1)} %bitcast.62), channel_id=1, source_target_pairs={{1,0},{2,1},{3,2},{4,3},{5,4},{6,5},{7,6},{8,7},{9,8},{10,9},{11,1... | collective-permute-start | bytes 393224 | tf_op jit(solution)/shard_map/ppermute | solution.py:226
  6.8 15.7 %collective-permute-start.1 = (bf16[256,256]{1,0:T(8,128)(2,1)S(1)}, bf16[256,256]{1,0:T(8,128)(2,1)S(1)}, u32[]{:S(2)}, u32[]{:S(2)}) collective-permute-start(bf16[256,256]{1,0:T(8,128)(2,1)S(1)} %bitcast.63), channel_id=1, source_target_pairs={{0,1},{1,2},{2,3},{3,4},{4,5},{5,6},{6,7},{7,8},{8,9},{9,10},{10,1... | collective-permute-start | bytes 393224 | tf_op jit(solution)/shard_map/ppermute | solution.py:226
  9.7 9.0 %collective-permute-start = (bf16[128,256]{1,0:T(8,128)(2,1)S(1)}, bf16[128,256]{1,0:T(8,128)(2,1)S(1)}, u32[]{:S(2)}, u32[]{:S(2)}) collective-permute-start(bf16[128,256]{1,0:T(8,128)(2,1)S(1)} %bitcast.89), channel_id=1, source_target_pairs={{0,2},{1,3},{2,4},{3,5},{4,6},{5,7},{6,8},{7,9},{8,10},{9,11},{10,... | collective-permute-start | bytes 196616 | tf_op jit(solution)/shard_map/ppermute | solution.py:226
  12.5 10.0 %collective-permute-start.3 = (bf16[128,256]{1,0:T(8,128)(2,1)S(1)}, bf16[128,256]{1,0:T(8,128)(2,1)S(1)}, u32[]{:S(2)}, u32[]{:S(2)}) collective-permute-start(bf16[128,256]{1,0:T(8,128)(2,1)S(1)} %bitcast.90), channel_id=1, source_target_pairs={{2,0},{3,1},{4,2},{5,3},{6,4},{7,5},{8,6},{9,7},{10,8},{11,9},{12,... | collective-permute-start | bytes 196616 | tf_op jit(solution)/shard_map/ppermute | solution.py:226
  16.0 13.3 %collective-permute-start.5 = (bf16[512,256]{1,0:T(8,128)(2,1)S(1)}, bf16[512,256]{1,0:T(8,128)(2,1)S(1)}, u32[]{:S(2)}, u32[]{:S(2)}) collective-permute-start(bf16[512,256]{1,0:T(8,128)(2,1)S(1)} %constant_dynamic-update-slice_fusion.own), channel_id=1, source_target_pairs={{1,0},{2,1},{3,2},{4,3},{5,4},{6,5},{7,6},{8,7},{9,8},{10,9},{11,1... | collective-permute-start | bytes 786440 | tf_op jit(solution)/shard_map/ppermute | solution.py:226
  18.8 10.5 %collective-permute-start.4 = (bf16[512,256]{1,0:T(8,128)(2,1)S(1)}, bf16[512,256]{1,0:T(8,128)(2,1)S(1)}, u32[]{:S(2)}, u32[]{:S(2)}) collective-permute-start(bf16[512,256]{1,0:T(8,128)(2,1)S(1)} %constant_dynamic-update-slice_fusion.own), channel_id=1, source_target_pairs={{0,1},{1,2},{2,3},{3,4},{4,5},{5,6},{6,7},{7,8},{8,9},{9,10},{10,1... | collective-permute-start | bytes 786440 | tf_op jit(solution)/shard_map/ppermute | solution.py:226
  35.0 7.7 %collective-permute-start.7 = (bf16[256,256]{1,0:T(8,128)(2,1)S(1)}, bf16[256,256]{1,0:T(8,128)(2,1)S(1)}, u32[]{:S(2)}, u32[]{:S(2)}) collective-permute-start(bf16[256,256]{1,0:T(8,128)(2,1)S(1)} %get-tuple-element.81.refs_9_), channel_id=1, source_target_pairs={{0,64},{1,65},{2,66},{3,67},{4,68},{5,69},{6,70},{7,71},{8,72},{9,... | collective-permute-start | bytes 393224 | tf_op jit(solution)/shard_map/ppermute | solution.py:218
  38.1 3.9 %collective-permute-start.6 = (bf16[128,256]{1,0:T(8,128)(2,1)S(1)}, bf16[128,256]{1,0:T(8,128)(2,1)S(1)}, u32[]{:S(2)}, u32[]{:S(2)}) collective-permute-start(bf16[128,256]{1,0:T(8,128)(2,1)S(1)} %get-tuple-element.80.refs_11_), channel_id=1, source_target_pairs={{0,65},{1,66},{2,67},{3,68},{4,69},{5,70},{6,71},{7,72},{8,73},{9,... | collective-permute-start | bytes 196616 | tf_op jit(solution)/shard_map/ppermute | solution.py:219
  39.8 2.9 %collective-permute-start.8 = (bf16[128,256]{1,0:T(8,128)(2,1)S(1)}, bf16[128,256]{1,0:T(8,128)(2,1)S(1)}, u32[]{:S(2)}, u32[]{:S(2)}) collective-permute-start(bf16[128,256]{1,0:T(8,128)(2,1)S(1)} %get-tuple-element.82.refs_10_), channel_id=1, source_target_pairs={{1,64},{2,65},{3,66},{4,67},{5,68},{6,69},{7,70},{8,71},{9,72},{10... | collective-permute-start | bytes 196616 | tf_op jit(solution)/shard_map/ppermute | solution.py:220
  43.3 2.0 collective-permute-start.10
  44.0 1.3 collective-permute-start.9
  44.6 0.7 collective-permute-start.11
  45.9 2.0 collective-permute-start.13
  46.6 1.3 collective-permute-start.12
  48.6 6.5 %collective-permute-start.15 = (bf16[128,256]{1,0:T(8,128)(2,1)S(1)}, bf16[128,256]{1,0:T(8,128)(2,1)S(1)}, u32[]{:S(2)}, u32[]{:S(2)}) collective-permute-start(bf16[128,256]{1,0:T(8,128)(2,1)S(1)} %get-tuple-element.95), channel_id=1, source_target_pairs={{0,1},{1,2},{2,3},{3,4},{4,5},{5,6},{6,7},{7,8},{8,9},{9,10},{10,1... | collective-permute-start | bytes 196616 | tf_op jit(solution)/shard_map/ppermute | solution.py:226
  53.2 5.6 %collective-permute-start.16 = (bf16[128,256]{1,0:T(8,128)(2,1)S(1)}, bf16[128,256]{1,0:T(8,128)(2,1)S(1)}, u32[]{:S(2)}, u32[]{:S(2)}) collective-permute-start(bf16[128,256]{1,0:T(8,128)(2,1)S(1)} %get-tuple-element.97), channel_id=1, source_target_pairs={{1,0},{2,1},{3,2},{4,3},{5,4},{6,5},{7,6},{8,7},{9,8},{10,9},{11,1... | collective-permute-start | bytes 196616 | tf_op jit(solution)/shard_map/ppermute | solution.py:226
  60.9 2.2 %collective-permute-start.18 = (bf16[256,256]{1,0:T(8,128)(2,1)S(1)}, bf16[256,256]{1,0:T(8,128)(2,1)S(1)}, u32[]{:S(2)}, u32[]{:S(2)}) collective-permute-start(bf16[256,256]{1,0:T(8,128)(2,1)S(1)} %get-tuple-element.99.refs_12_), channel_id=1, source_target_pairs={{192,128},{193,129},{194,130},{195,131},{196,132},{197,133},{198,1... | collective-permute-start | bytes 393224 | tf_op jit(solution)/shard_map/ppermute | solution.py:218
  61.6 1.5 collective-permute-start.17
  62.5 0.7 collective-permute-start.19
  63.8 2.0 collective-permute-start.21
  64.4 1.3 collective-permute-start.20
  66.4 39.9 %collective-permute-start.23 = (bf16[128,256]{1,0:T(8,128)(2,1)S(1)}, bf16[128,256]{1,0:T(8,128)(2,1)S(1)}, u32[]{:S(2)}, u32[]{:S(2)}) collective-permute-start(bf16[128,256]{1,0:T(8,128)(2,1)S(1)} %get-tuple-element.108.refs_14_), channel_id=1, source_target_pairs={{64,1},{65,2},{66,3},{67,4},{68,5},{69,6},{70,7},{71,8},{72,9},{73... | collective-permute-start | bytes 196616 | tf_op jit(solution)/shard_map/ppermute | solution.py:219
  67.9 43.8 %collective-permute-start.25 = (bf16[128,256]{1,0:T(8,128)(2,1)S(1)}, bf16[128,256]{1,0:T(8,128)(2,1)S(1)}, u32[]{:S(2)}, u32[]{:S(2)}) collective-permute-start(bf16[128,256]{1,0:T(8,128)(2,1)S(1)} %get-tuple-element.110.refs_13_), channel_id=1, source_target_pairs={{65,0},{66,1},{67,2},{68,3},{69,4},{70,5},{71,6},{72,7},{73,8},{74... | collective-permute-start | bytes 196616 | tf_op jit(solution)/shard_map/ppermute | solution.py:220
  69.2 42.7 %collective-permute-start.24 = (bf16[256,256]{1,0:T(8,128)(2,1)S(1)}, bf16[256,256]{1,0:T(8,128)(2,1)S(1)}, u32[]{:S(2)}, u32[]{:S(2)}) collective-permute-start(bf16[256,256]{1,0:T(8,128)(2,1)S(1)} %get-tuple-element.109.refs_12_), channel_id=1, source_target_pairs={{64,0},{65,1},{66,2},{67,3},{68,4},{69,5},{70,6},{71,7},{72,8},{73... | collective-permute-start | bytes 393224 | tf_op jit(solution)/shard_map/ppermute | solution.py:218
  72.2 44.3 %collective-permute-start.30 = (bf16[4,896,128]{2,1,0:T(8,128)(2,1)S(1)}, bf16[4,896,128]{2,1,0:T(8,128)(2,1)S(1)}, u32[]{:S(2)}, u32[]{:S(2)}) collective-permute-start(bf16[4,896,128]{2,1,0:T(8,128)(2,1)S(1)} %get-tuple-element.129), channel_id=1, source_target_pairs={{0,1},{1,0},{2,3},{3,2},{4,5},{5,4},{6,7},{7,6},{8,9},{9,8},{10,11... | collective-permute-start | bytes 2752520 | tf_op jit(solution)/shard_map/ppermute | solution.py:372
  116.4 9.4 %collective-permute-start.26 = (bf16[4,896,128]{2,1,0:T(8,128)(2,1)S(1)}, bf16[4,896,128]{2,1,0:T(8,128)(2,1)S(1)}, u32[]{:S(2)}, u32[]{:S(2)}) collective-permute-start(bf16[4,896,128]{2,1,0:T(8,128)(2,1)S(1)} %get-tuple-element.119), channel_id=1, source_target_pairs={{0,1},{1,0},{2,3},{3,2},{4,5},{5,4},{6,7},{7,6},{8,9},{9,8},{10,11... | collective-permute-start | bytes 2752520 | tf_op jit(solution)/shard_map/ppermute | solution.py:372
  117.5 11.7 %collective-permute-start.31 = (bf16[1,896,128]{2,1,0:T(8,128)(2,1)S(1)}, bf16[1,896,128]{2,1,0:T(8,128)(2,1)S(1)}, u32[]{:S(2)}, u32[]{:S(2)}) collective-permute-start(bf16[1,896,128]{2,1,0:T(8,128)(2,1)S(1)} %get-tuple-element.131), channel_id=1, source_target_pairs={{0,4},{1,5},{2,6},{3,7},{4,0},{5,1},{6,2},{7,3},{8,12},{9,13},{10,... | collective-permute-start | bytes 688136 | tf_op jit(solution)/shard_map/ppermute | solution.py:372
  123.1 11.1 %collective-permute-start.32 = (bf16[1,896,128]{2,1,0:T(8,128)(2,1)S(1)}, bf16[1,896,128]{2,1,0:T(8,128)(2,1)S(1)}, u32[]{:S(2)}, u32[]{:S(2)}) collective-permute-start(bf16[1,896,128]{2,1,0:T(8,128)(2,1)S(1)} %get-tuple-element.132), channel_id=1, source_target_pairs={{0,2},{1,3},{2,4},{3,5},{4,6},{5,7},{6,0},{7,1},{8,10},{9,11},{10,... | collective-permute-start | bytes 688136 | tf_op jit(solution)/shard_map/ppermute | solution.py:372
  123.5 10.8 %collective-permute-start.33 = (bf16[1,896,128]{2,1,0:T(8,128)(2,1)S(1)}, bf16[1,896,128]{2,1,0:T(8,128)(2,1)S(1)}, u32[]{:S(2)}, u32[]{:S(2)}) collective-permute-start(bf16[1,896,128]{2,1,0:T(8,128)(2,1)S(1)} %get-tuple-element.133), channel_id=1, source_target_pairs={{0,6},{1,7},{2,0},{3,1},{4,2},{5,3},{6,4},{7,5},{8,14},{9,15},{10,... | collective-permute-start | bytes 688136 | tf_op jit(solution)/shard_map/ppermute | solution.py:372
  126.7 12.3 %collective-permute-start.27 = (bf16[1,896,128]{2,1,0:T(8,128)(2,1)S(1)}, bf16[1,896,128]{2,1,0:T(8,128)(2,1)S(1)}, u32[]{:S(2)}, u32[]{:S(2)}) collective-permute-start(bf16[1,896,128]{2,1,0:T(8,128)(2,1)S(1)} %get-tuple-element.121), channel_id=1, source_target_pairs={{0,4},{1,5},{2,6},{3,7},{4,0},{5,1},{6,2},{7,3},{8,12},{9,13},{10,... | collective-permute-start | bytes 688136 | tf_op jit(solution)/shard_map/ppermute | solution.py:372
  126.8 17.1 %collective-permute-start.28 = (bf16[1,896,128]{2,1,0:T(8,128)(2,1)S(1)}, bf16[1,896,128]{2,1,0:T(8,128)(2,1)S(1)}, u32[]{:S(2)}, u32[]{:S(2)}) collective-permute-start(bf16[1,896,128]{2,1,0:T(8,128)(2,1)S(1)} %get-tuple-element.122), channel_id=1, source_target_pairs={{0,2},{1,3},{2,4},{3,5},{4,6},{5,7},{6,0},{7,1},{8,10},{9,11},{10,... | collective-permute-start | bytes 688136 | tf_op jit(solution)/shard_map/ppermute | solution.py:372
  129.1 14.8 %collective-permute-start.29 = (bf16[1,896,128]{2,1,0:T(8,128)(2,1)S(1)}, bf16[1,896,128]{2,1,0:T(8,128)(2,1)S(1)}, u32[]{:S(2)}, u32[]{:S(2)}) collective-permute-start(bf16[1,896,128]{2,1,0:T(8,128)(2,1)S(1)} %get-tuple-element.123), channel_id=1, source_target_pairs={{0,6},{1,7},{2,0},{3,1},{4,2},{5,3},{6,4},{7,5},{8,14},{9,15},{10,... | collective-permute-start | bytes 688136 | tf_op jit(solution)/shard_map/ppermute | solution.py:372
  144.8 7.4 %collective-permute-start.34 = (bf16[2,448,128]{2,1,0:T(8,128)(2,1)S(1)}, bf16[2,448,128]{2,1,0:T(8,128)(2,1)S(1)}, u32[]{:S(2)}, u32[]{:S(2)}) collective-permute-start(bf16[2,448,128]{2,1,0:T(8,128)(2,1)S(1)} %get-tuple-element.135), channel_id=1, source_target_pairs={{0,8},{1,9},{2,10},{3,11},{4,12},{5,13},{6,14},{7,15},{8,0},{9,1},... | collective-permute-start | bytes 688136 | tf_op jit(solution)/shard_map/ppermute | solution.py:372
  152.8 16.1 %collective-permute-start.35 = (bf16[2,112,128]{2,1,0:T(8,128)(2,1)S(1)}, bf16[2,112,128]{2,1,0:T(8,128)(2,1)S(1)}, u32[]{:S(2)}, u32[]{:S(2)}) collective-permute-start(bf16[2,112,128]{2,1,0:T(8,128)(2,1)S(1)} %get-tuple-element.137), channel_id=1, source_target_pairs={{0,32},{1,33},{2,34},{3,35},{4,36},{5,37},{6,38},{7,39},{8,40},{9,... | collective-permute-start | bytes 172040 | tf_op jit(solution)/shard_map/ppermute | solution.py:372
  165.3 5.6 %collective-permute-start.36 = (bf16[2,112,128]{2,1,0:T(8,128)(2,1)S(1)}, bf16[2,112,128]{2,1,0:T(8,128)(2,1)S(1)}, u32[]{:S(2)}, u32[]{:S(2)}) collective-permute-start(bf16[2,112,128]{2,1,0:T(8,128)(2,1)S(1)} %get-tuple-element.138), channel_id=1, source_target_pairs={{0,16},{1,17},{2,18},{3,19},{4,20},{5,21},{6,22},{7,23},{8,24},{9,... | collective-permute-start | bytes 172040 | tf_op jit(solution)/shard_map/ppermute | solution.py:372
  165.3 5.6 %collective-permute-start.37 = (bf16[2,112,128]{2,1,0:T(8,128)(2,1)S(1)}, bf16[2,112,128]{2,1,0:T(8,128)(2,1)S(1)}, u32[]{:S(2)}, u32[]{:S(2)}) collective-permute-start(bf16[2,112,128]{2,1,0:T(8,128)(2,1)S(1)} %get-tuple-element.139), channel_id=1, source_target_pairs={{0,48},{1,49},{2,50},{3,51},{4,52},{5,53},{6,54},{7,55},{8,56},{9,... | collective-permute-start | bytes 172040 | tf_op jit(solution)/shard_map/ppermute | solution.py:372
  170.9 7.7 %collective-permute-start.40 = (bf16[2,112,128]{2,1,0:T(8,128)(2,1)S(1)}, bf16[2,112,128]{2,1,0:T(8,128)(2,1)S(1)}, u32[]{:S(2)}, u32[]{:S(2)}) collective-permute-start(bf16[2,112,128]{2,1,0:T(8,128)(2,1)S(1)} %added.7.refs_1_), channel_id=1, source_target_pairs={{0,48},{1,49},{2,50},{3,51},{4,52},{5,53},{6,54},{7,55},{8,56},{9,... | collective-permute-start | bytes 172040 | tf_op jit(solution)/shard_map/ppermute | solution.py:372
  174.7 7.0 %collective-permute-start.39 = (bf16[2,112,128]{2,1,0:T(8,128)(2,1)S(1)}, bf16[2,112,128]{2,1,0:T(8,128)(2,1)S(1)}, u32[]{:S(2)}, u32[]{:S(2)}) collective-permute-start(bf16[2,112,128]{2,1,0:T(8,128)(2,1)S(1)} %added.7.refs_1_), channel_id=1, source_target_pairs={{0,32},{1,33},{2,34},{3,35},{4,36},{5,37},{6,38},{7,39},{8,40},{9,... | collective-permute-start | bytes 172040 | tf_op jit(solution)/shard_map/ppermute | solution.py:372
  176.3 6.1 %collective-permute-start.38 = (bf16[2,112,128]{2,1,0:T(8,128)(2,1)S(1)}, bf16[2,112,128]{2,1,0:T(8,128)(2,1)S(1)}, u32[]{:S(2)}, u32[]{:S(2)}) collective-permute-start(bf16[2,112,128]{2,1,0:T(8,128)(2,1)S(1)} %added.7.refs_1_), channel_id=1, source_target_pairs={{0,16},{1,17},{2,18},{3,19},{4,20},{5,21},{6,22},{7,23},{8,24},{9,... | collective-permute-start | bytes 172040 | tf_op jit(solution)/shard_map/ppermute | solution.py:372
  183.0 5.0 %collective-permute-start.41 = (bf16[2,448,128]{2,1,0:T(8,128)(2,1)S(1)}, bf16[2,448,128]{2,1,0:T(8,128)(2,1)S(1)}, u32[]{:S(2)}, u32[]{:S(2)}) collective-permute-start(bf16[2,448,128]{2,1,0:T(8,128)(2,1)S(1)} %bitcast.54), channel_id=1, source_target_pairs={{0,8},{1,9},{2,10},{3,11},{4,12},{5,13},{6,14},{7,15},{8,0},{9,1},... | collective-permute-start | bytes 688136 | tf_op jit(solution)/shard_map/ppermute | solution.py:372
  188.6 6.2 %collective-permute-start.42 = (bf16[896,128]{1,0:T(8,128)(2,1)S(1)}, bf16[896,128]{1,0:T(8,128)(2,1)S(1)}, u32[]{:S(2)}, u32[]{:S(2)}) collective-permute-start(bf16[896,128]{1,0:T(8,128)(2,1)S(1)} %bitcast.59), channel_id=1, source_target_pairs={{0,2},{1,3},{2,4},{3,5},{4,6},{5,7},{6,0},{7,1},{8,10},{9,11},{10,... | collective-permute-start | bytes 688136 | tf_op jit(solution)/shard_map/ppermute | solution.py:372
  188.7 6.1 %collective-permute-start.47 = (bf16[896,128]{1,0:T(8,128)(2,1)S(1)}, bf16[896,128]{1,0:T(8,128)(2,1)S(1)}, u32[]{:S(2)}, u32[]{:S(2)}) collective-permute-start(bf16[896,128]{1,0:T(8,128)(2,1)S(1)} %bitcast.56), channel_id=1, source_target_pairs={{0,6},{1,7},{2,0},{3,1},{4,2},{5,3},{6,4},{7,5},{8,14},{9,15},{10,... | collective-permute-start | bytes 688136 | tf_op jit(solution)/shard_map/ppermute | solution.py:372
  191.3 6.1 %collective-permute-start.44 = (bf16[896,128]{1,0:T(8,128)(2,1)S(1)}, bf16[896,128]{1,0:T(8,128)(2,1)S(1)}, u32[]{:S(2)}, u32[]{:S(2)}) collective-permute-start(bf16[896,128]{1,0:T(8,128)(2,1)S(1)} %bitcast.60), channel_id=1, source_target_pairs={{0,6},{1,7},{2,0},{3,1},{4,2},{5,3},{6,4},{7,5},{8,14},{9,15},{10,... | collective-permute-start | bytes 688136 | tf_op jit(solution)/shard_map/ppermute | solution.py:372
  194.7 8.0 %collective-permute-start.43 = (bf16[896,128]{1,0:T(8,128)(2,1)S(1)}, bf16[896,128]{1,0:T(8,128)(2,1)S(1)}, u32[]{:S(2)}, u32[]{:S(2)}) collective-permute-start(bf16[896,128]{1,0:T(8,128)(2,1)S(1)} %collective-permute-done.42.refs_1_), channel_id=1, source_target_pairs={{0,2},{1,3},{2,4},{3,5},{4,6},{5,7},{6,0},{7,1},{8,10},{9,11},{10,... | collective-permute-start | bytes 688136 | tf_op jit(solution)/shard_map/ppermute | solution.py:372
  194.7 16.2 %collective-permute-start.46 = (bf16[896,128]{1,0:T(8,128)(2,1)S(1)}, bf16[896,128]{1,0:T(8,128)(2,1)S(1)}, u32[]{:S(2)}, u32[]{:S(2)}) collective-permute-start(bf16[896,128]{1,0:T(8,128)(2,1)S(1)} %bitcast.57), channel_id=1, source_target_pairs={{0,2},{1,3},{2,4},{3,5},{4,6},{5,7},{6,0},{7,1},{8,10},{9,11},{10,... | collective-permute-start | bytes 688136 | tf_op jit(solution)/shard_map/ppermute | solution.py:372
  194.7 16.2 %collective-permute-start.48 = (bf16[896,128]{1,0:T(8,128)(2,1)S(1)}, bf16[896,128]{1,0:T(8,128)(2,1)S(1)}, u32[]{:S(2)}, u32[]{:S(2)}) collective-permute-start(bf16[896,128]{1,0:T(8,128)(2,1)S(1)} %collective-permute-done.47.refs_3_), channel_id=1, source_target_pairs={{0,6},{1,7},{2,0},{3,1},{4,2},{5,3},{6,4},{7,5},{8,14},{9,15},{10,... | collective-permute-start | bytes 688136 | tf_op jit(solution)/shard_map/ppermute | solution.py:372
  203.4 14.1 %collective-permute-start.45 = (bf16[4,896,128]{2,1,0:T(8,128)(2,1)S(1)}, bf16[4,896,128]{2,1,0:T(8,128)(2,1)S(1)}, u32[]{:S(2)}, u32[]{:S(2)}) collective-permute-start(bf16[4,896,128]{2,1,0:T(8,128)(2,1)S(1)} %join_y.2.refs_1_), channel_id=1, source_target_pairs={{0,1},{1,0},{2,3},{3,2},{4,5},{5,4},{6,7},{7,6},{8,9},{9,8},{10,11... | collective-permute-start | bytes 2752520 | tf_op jit(solution)/shard_map/ppermute | solution.py:372
  211.5 6.0 %collective-permute-start.49 = (bf16[4,896,128]{2,1,0:T(8,128)(2,1)S(1)}, bf16[4,896,128]{2,1,0:T(8,128)(2,1)}, u32[]{:S(2)}, u32[]{:S(2)}) collective-permute-start(bf16[4,896,128]{2,1,0:T(8,128)(2,1)S(1)} %join_y.3.refs_2_), channel_id=1, source_target_pairs={{0,1},{1,0},{2,3},{3,2},{4,5},{5,4},{6,7},{7,6},{8,9},{9,8},{10,11... | collective-permute-start | bytes 2752520 | tf_op jit(solution)/shard_map/ppermute | solution.py:372
  (4 other events, 49.4 us)

commit v4 on v3

--- a/solution.py
+++ b/solution.py
@@ -175,6 +175,65 @@
     mine = place_ref[1] == turn
     pl.when(mine)(run)
     pl.when(jnp.logical_not(mine))(carry)
+
+
+def final_kernel(place_ref, w_ref, s1_ref, s2_ref, *refs):
+    cots, skips, state, outs = refs[0:3], refs[3:6], refs[6:8], refs[8:11]
+    mine = place_ref[1] == 0
+
+    @pl.when(mine)
+    def _():
+        g = jnp.concatenate([ref[...] for ref in cots], axis=0).astype(F32)
+        g = g + jnp.concatenate([ref[...] for ref in skips], axis=0).astype(F32)
+        second = (g.astype(BF).astype(F32) * s2_ref[...]).astype(BF)
+        outs[0][...] = second[2 * Z : 2 * Z + CELLS]
+        first = conv_adjoint(second, w_ref.at[1], 6) * s1_ref[...]
+        first = jnp.where(row_mask(6, -1, place_ref[0]), first, 0.0).astype(BF)
+        outs[1][...] = first[Z : Z + CELLS]
+        outs[2][...] = first
+
+    @pl.when(jnp.logical_not(mine))
+    def _():
+        outs[0][...] = state[0][...]
+        outs[1][...] = state[1][...]
+        outs[2][...] = jnp.zeros_like(outs[2])
+
+
+def final_tick(place, weights, slopes, cot, skip, state):
+    args = [place, weights, *slopes, *cot, *skip, *state[0:2]]
+    return pl.pallas_call(
+        final_kernel,
+        out_shape=[sds(4, BF), sds(4, BF), sds(6, BF)],
+        in_specs=[SMEM] + [VMEM] * (len(args) - 1),
+        out_specs=[VMEM] * 3,
+        compiler_params=pltpu.CompilerParams(vmem_limit_bytes=16 << 20),
+        cost_estimate=pl.CostEstimate(flops=2 * 10**9, bytes_accessed=4 << 20, transcendentals=0),
+        name="final_tick",
+    )(*args)
+
+
+def late_kernel(place_ref, w_ref, first_ref, state_ref, out_ref):
+    mine = place_ref[1] == 0
+
+    @pl.when(mine)
+    def _():
+        out_ref[...] = conv_adjoint(first_ref[...], w_ref.at[0], 4).astype(BF)
+
+    @pl.when(jnp.logical_not(mine))
+    def _():
+        out_ref[...] = state_ref[...]
+
+
+def late_input_grad(place, weights, first, grad):
+    return pl.pallas_call(
+        late_kernel,
+        out_shape=sds(4, BF),
+        in_specs=[SMEM] + [VMEM] * 3,
+        out_specs=VMEM,
+        compiler_params=pltpu.CompilerParams(vmem_limit_bytes=16 << 20),
+        cost_estimate=pl.CostEstimate(flops=10**9, bytes_accessed=2 << 20, transcendentals=0),
+        name="late",
+    )(place, weights, first, grad)
 
 
 def tick(layer, turn, place, weights, slopes, cot, skip=None, state=None):
@@ -531,9 +590,12 @@
         cot = hand_on(state, turn + 1, -1)
         if turn == 1:
             dec_total = first_phases(place, (upper[1], dec_v, upper[0], dec_h))
-        state = tick(0, turn, place, kernels, slopes, cot, skip=skip, state=state)
-    enc_total = first_phases(place, (state[1], enc_v, state[0], enc_h))
-    encoder_grad, upper_grad = from_cells(state[2]), from_cells(upper[2])
+        if turn > 0:
+            state = tick(0, turn, place, kernels, slopes, cot, skip=skip, state=state)
+    second, first, wide = final_tick(place, kernels, slopes, cot, skip, state)
+    enc_total = first_phases(place, (first, enc_v, second, enc_h))
+    last_grad = late_input_grad(place, kernels, wide, state[2])
+    encoder_grad, upper_grad = from_cells(last_grad), from_cells(upper[2])
     mine = last_phases(place, [enc_total, dec_total])
     other = [send(part, core_step, 1) for part in mine]
     totals = unpack(place, 0, mine)

time: 222 us -> 224 us (level)
    pallas_call x8 -> x7, Pallas kernels: 10.1 us -> 7.28 us  [tick(): pl.pallas_call(lambda *refs: tick_kernel(layer, turn, seeded, *refs), out...]
  transfers between devices with their start and end apart: 50 -> 50, of which waited for: 17 -> 16; matrix products, arithmetic and copies ran while one was open for 2% -> 2% of each run, Pallas kernels for 8% -> 7%
where the time goes in v4:
time: 224 us
  starting transfers between devices  94.2 us (42%)
  waiting for transfers between devices  83.9 us (37%)
  Pallas kernels  33.7 us (15%)
  local copies, waits for them, and re-layouts  9.68 us (4%)
    ppermute x24, starting transfers between devices, send(): lax.ppermute(array, 'space', [(place, move(place, step)) for place in ran...  52.8 us
    ppermute x24, waiting for transfers between devices, send(): lax.ppermute(array, 'space', [(place, move(place, step)) for place in ran...  39 us
    ppermute x6, waiting for transfers between devices, hand_on(): before = lax.ppermute(high, GRID_AXES, shifted(source_section, by, 1))  35.1 us
    ppermute x8, starting transfers between devices, beside(): return lax.ppermute(array, 'space', pairs)  23.2 us
    pallas_call x2, Pallas kernels, forward(): pl.pallas_call(kernel, out_shape=[sds(6, BF), sds(6, BF), sds(6, F32), sd...  8.26 us
    pallas_call x7, Pallas kernels, tick(): pl.pallas_call(lambda *refs: tick_kernel(layer, turn, seeded, *refs), out...  7.28 us
    ppermute x6, starting transfers between devices, hand_on(): middle = lax.ppermute(grad, GRID_AXES, shifted(source_section, by, 0))  7.09 us
    pallas_call x2, Pallas kernels, unpack(): pl.pallas_call(lambda *refs: unpack_kernel(*refs), out_shape=[jax.ShapeDt...  6.61 us
  transfers between devices with their start and end apart: 50, of which 16 were waited for; matrix products, arithmetic and copies ran while one was open for 2% of the time, Pallas kernels for 7%

profile of v4, /device:TPU:1, one launch (start us, length us, event | category | flops | bytes accessed | tf_op | source)
XLA Modules:
  0.0 223.6 jit_solution(7615840990940570808)
XLA Ops:
  1.7 5.1 %collective-permute-start.2 = (bf16[256,256]{1,0:T(8,128)(2,1)S(1)}, bf16[256,256]{1,0:T(8,128)(2,1)S(1)}, u32[]{:S(2)}, u32[]{:S(2)}) collective-permute-start(bf16[256,256]{1,0:T(8,128)(2,1)S(1)} %bitcast.73), channel_id=1, source_target_pairs={{1,0},{2,1},{3,2},{4,3},{5,4},{6,5},{7,6},{8,7},{9,8},{10,9},{11,1... | collective-permute-start | bytes 393224 | tf_op jit(solution)/shard_map/ppermute | solution.py:285
  6.8 1.9 collective-permute-start.1
  9.7 2.7 %collective-permute-start = (bf16[128,256]{1,0:T(8,128)(2,1)S(1)}, bf16[128,256]{1,0:T(8,128)(2,1)S(1)}, u32[]{:S(2)}, u32[]{:S(2)}) collective-permute-start(bf16[128,256]{1,0:T(8,128)(2,1)S(1)} %bitcast.90), channel_id=1, source_target_pairs={{0,2},{1,3},{2,4},{3,5},{4,6},{5,7},{6,8},{7,9},{8,10},{9,11},{10,... | collective-permute-start | bytes 196616 | tf_op jit(solution)/shard_map/ppermute | solution.py:285
  12.5 1.3 collective-permute-start.3
  16.0 1.9 collective-permute-start.5
  18.8 3.7 %collective-permute-start.4 = (bf16[512,256]{1,0:T(8,128)(2,1)S(1)}, bf16[512,256]{1,0:T(8,128)(2,1)S(1)}, u32[]{:S(2)}, u32[]{:S(2)}) collective-permute-start(bf16[512,256]{1,0:T(8,128)(2,1)S(1)} %constant_dynamic-update-slice_fusion.own), channel_id=1, source_target_pairs={{0,1},{1,2},{2,3},{3,4},{4,5},{5,6},{6,7},{7,8},{8,9},{9,10},{10,1... | collective-permute-start | bytes 786440 | tf_op jit(solution)/shard_map/ppermute | solution.py:285
  22.5 2.0 copy-done
  24.5 4.7 %shard_map.84 = (bf16[384,256]{1,0:T(8,128)(2,1)S(1)}, bf16[384,256]{1,0:T(8,128)(2,1)S(1)}, f32[384,256]{1,0:T(8,128)S(1)}, f32[512,256]{1,0:T(8,128)S(1)}, bf16[768,256]{1,0:T(8,128)(2,1)S(1)}) custom-call(s32[2]{0:T(128)S(1)} %pad_add_fusion.place_ref.refs_0_, bf16[4,3,128,1152]{3,2,1,0:T(8,128)(2,1)S(1)} %bitcast.54, ...), custom_call_target="tpu_custom_call" | custom-call | flops 3000000000 | bytes 5242880 | tf_op jit(solution)/shard_map/pallas_call | solution.py:128
  29.3 3.6 %shard_map.85 = (bf16[384,256]{1,0:T(8,128)(2,1)S(1)}, bf16[384,256]{1,0:T(8,128)(2,1)S(1)}, f32[384,256]{1,0:T(8,128)S(1)}, f32[512,256]{1,0:T(8,128)S(1)}) custom-call(s32[2]{0:T(128)S(1)} %pad_add_fusion.place_ref.refs_0_, bf16[4,3,128,1152]{3,2,1,0:T(8,128)(2,1)S(1)} %bitcast.55, f32[4,256]{1,0:T(4,128)S(1)} %pad_maximum_fusion.bias_ref, ...), custom_call_target="tpu_custom_call" | custom-call | flops 3000000000 | bytes 5242880 | tf_op jit(solution)/shard_map/pallas_call | solution.py:128
  32.9 2.2 tick.7
  35.0 3.1 %collective-permute-start.7 = (bf16[256,256]{1,0:T(8,128)(2,1)S(1)}, bf16[256,256]{1,0:T(8,128)(2,1)S(1)}, u32[]{:S(2)}, u32[]{:S(2)}) collective-permute-start(bf16[256,256]{1,0:T(8,128)(2,1)S(1)} %get-tuple-element.81.refs_9_), channel_id=1, source_target_pairs={{0,64},{1,65},{2,66},{3,67},{4,68},{5,69},{6,70},{7,71},{8,72},{9,... | collective-permute-start | bytes 393224 | tf_op jit(solution)/shard_map/ppermute | solution.py:277
  38.2 1.6 collective-permute-start.6
  39.8 1.3 collective-permute-start.8
  48.6 4.6 %collective-permute-start.15 = (bf16[128,256]{1,0:T(8,128)(2,1)S(1)}, bf16[128,256]{1,0:T(8,128)(2,1)S(1)}, u32[]{:S(2)}, u32[]{:S(2)}) collective-permute-start(bf16[128,256]{1,0:T(8,128)(2,1)S(1)} %get-tuple-element.95), channel_id=1, source_target_pairs={{0,1},{1,2},{2,3},{3,4},{4,5},{5,6},{6,7},{7,8},{8,9},{9,10},{10,1... | collective-permute-start | bytes 196616 | tf_op jit(solution)/shard_map/ppermute | solution.py:285
  53.2 1.9 collective-permute-start.16
  55.1 3.6 %collective-permute-done.16.refs_6_.refs_9_.refs_5_ = bf16[128,256]{1,0:T(8,128)(2,1)S(1)} collective-permute-done((bf16[128,256]{1,0:T(8,128)(2,1)S(1)}, bf16[128,256]{1,0:T(8,128)(2,1)S(1)}, u32[]{:S(2)}, u32[]{:S(2)}) %collective-permute-start.16) | collective-permute-done | bytes 65568 | tf_op jit(solution)/shard_map/ppermute | solution.py:285
  58.8 2.2 tick.11
  66.5 1.4 collective-permute-start.23
  67.9 1.3 collective-permute-start.25
  70.5 1.7 weights.3
  72.3 34.1 %collective-permute-done.23.refs_0_ = bf16[128,256]{1,0:T(8,128)(2,1)S(1)} collective-permute-done((bf16[128,256]{1,0:T(8,128)(2,1)S(1)}, bf16[128,256]{1,0:T(8,128)(2,1)S(1)}, u32[]{:S(2)}, u32[]{:S(2)}) %collective-permute-start.23) | collective-permute-done | bytes 65568 | tf_op jit(solution)/shard_map/ppermute | solution.py:278
  106.4 5.2 %collective-permute-done.25.refs_2_ = bf16[128,256]{1,0:T(8,128)(2,1)S(1)} collective-permute-done((bf16[128,256]{1,0:T(8,128)(2,1)S(1)}, bf16[128,256]{1,0:T(8,128)(2,1)S(1)}, u32[]{:S(2)}, u32[]{:S(2)}) %collective-permute-start.25) | collective-permute-done | bytes 65568 | tf_op jit(solution)/shard_map/ppermute | solution.py:279
  113.1 1.7 weights.2
  115.9 5.7 %collective-permute-start.31 = (bf16[1,896,128]{2,1,0:T(8,128)(2,1)S(1)}, bf16[1,896,128]{2,1,0:T(8,128)(2,1)S(1)}, u32[]{:S(2)}, u32[]{:S(2)}) collective-permute-start(bf16[1,896,128]{2,1,0:T(8,128)(2,1)S(1)} %get-tuple-element.131), channel_id=1, source_target_pairs={{0,4},{1,5},{2,6},{3,7},{4,0},{5,1},{6,2},{7,3},{8,12},{9,13},{10,... | collective-permute-start | bytes 688136 | tf_op jit(solution)/shard_map/ppermute | solution.py:431
  121.9 2.4 %collective-permute-start.33 = (bf16[1,896,128]{2,1,0:T(8,128)(2,1)S(1)}, bf16[1,896,128]{2,1,0:T(8,128)(2,1)S(1)}, u32[]{:S(2)}, u32[]{:S(2)}) collective-permute-start(bf16[1,896,128]{2,1,0:T(8,128)(2,1)S(1)} %get-tuple-element.133), channel_id=1, source_target_pairs={{0,6},{1,7},{2,0},{3,1},{4,2},{5,3},{6,4},{7,5},{8,14},{9,15},{10,... | collective-permute-start | bytes 688136 | tf_op jit(solution)/shard_map/ppermute | solution.py:431
  125.9 1.7 collective-permute-done.31.refs_1_
  127.6 2.4 %collective-permute-start.29 = (bf16[1,896,128]{2,1,0:T(8,128)(2,1)S(1)}, bf16[1,896,128]{2,1,0:T(8,128)(2,1)S(1)}, u32[]{:S(2)}, u32[]{:S(2)}) collective-permute-start(bf16[1,896,128]{2,1,0:T(8,128)(2,1)S(1)} %get-tuple-element.123), channel_id=1, source_target_pairs={{0,6},{1,7},{2,0},{3,1},{4,2},{5,3},{6,4},{7,5},{8,14},{9,15},{10,... | collective-permute-start | bytes 688136 | tf_op jit(solution)/shard_map/ppermute | solution.py:431
  130.0 2.7 %collective-permute-done.32.refs_2_ = bf16[1,896,128]{2,1,0:T(8,128)(2,1)S(1)} collective-permute-done((bf16[1,896,128]{2,1,0:T(8,128)(2,1)S(1)}, bf16[1,896,128]{2,1,0:T(8,128)(2,1)S(1)}, u32[]{:S(2)}, u32[]{:S(2)}) %collective-permute-start.32) | collective-permute-done | bytes 229408 | tf_op jit(solution)/shard_map/ppermute | solution.py:431
  132.8 4.7 %collective-permute-done.27.refs_1_ = bf16[1,896,128]{2,1,0:T(8,128)(2,1)S(1)} collective-permute-done((bf16[1,896,128]{2,1,0:T(8,128)(2,1)S(1)}, bf16[1,896,128]{2,1,0:T(8,128)(2,1)S(1)}, u32[]{:S(2)}, u32[]{:S(2)}) %collective-permute-start.27) | collective-permute-done | bytes 229408 | tf_op jit(solution)/shard_map/ppermute | solution.py:431
  137.5 5.0 %collective-permute-done.28.refs_2_ = bf16[1,896,128]{2,1,0:T(8,128)(2,1)S(1)} collective-permute-done((bf16[1,896,128]{2,1,0:T(8,128)(2,1)S(1)}, bf16[1,896,128]{2,1,0:T(8,128)(2,1)S(1)}, u32[]{:S(2)}, u32[]{:S(2)}) %collective-permute-start.28) | collective-permute-done | bytes 229408 | tf_op jit(solution)/shard_map/ppermute | solution.py:431
  143.2 2.4 %collective-permute-start.34 = (bf16[2,448,128]{2,1,0:T(8,128)(2,1)S(1)}, bf16[2,448,128]{2,1,0:T(8,128)(2,1)S(1)}, u32[]{:S(2)}, u32[]{:S(2)}) collective-permute-start(bf16[2,448,128]{2,1,0:T(8,128)(2,1)S(1)} %get-tuple-element.135), channel_id=1, source_target_pairs={{0,8},{1,9},{2,10},{3,11},{4,12},{5,13},{6,14},{7,15},{8,0},{9,1},... | collective-permute-start | bytes 688136 | tf_op jit(solution)/shard_map/ppermute | solution.py:431
  145.7 5.2 %collective-permute-done.34.refs_1_ = bf16[2,448,128]{2,1,0:T(8,128)(2,1)S(1)} collective-permute-done((bf16[2,448,128]{2,1,0:T(8,128)(2,1)S(1)}, bf16[2,448,128]{2,1,0:T(8,128)(2,1)S(1)}, u32[]{:S(2)}, u32[]{:S(2)}) %collective-permute-start.34) | collective-permute-done | bytes 229408 | tf_op jit(solution)/shard_map/ppermute | solution.py:431
  151.5 12.5 %collective-permute-start.35 = (bf16[2,112,128]{2,1,0:T(8,128)(2,1)S(1)}, bf16[2,112,128]{2,1,0:T(8,128)(2,1)S(1)}, u32[]{:S(2)}, u32[]{:S(2)}) collective-permute-start(bf16[2,112,128]{2,1,0:T(8,128)(2,1)S(1)} %get-tuple-element.137), channel_id=1, source_target_pairs={{0,32},{1,33},{2,34},{3,35},{4,36},{5,37},{6,38},{7,39},{8,40},{9,... | collective-permute-start | bytes 172040 | tf_op jit(solution)/shard_map/ppermute | solution.py:431
  164.0 3.6 %collective-permute-start.37 = (bf16[2,112,128]{2,1,0:T(8,128)(2,1)S(1)}, bf16[2,112,128]{2,1,0:T(8,128)(2,1)S(1)}, u32[]{:S(2)}, u32[]{:S(2)}) collective-permute-start(bf16[2,112,128]{2,1,0:T(8,128)(2,1)S(1)} %get-tuple-element.139), channel_id=1, source_target_pairs={{0,48},{1,49},{2,50},{3,51},{4,52},{5,53},{6,54},{7,55},{8,56},{9,... | collective-permute-start | bytes 172040 | tf_op jit(solution)/shard_map/ppermute | solution.py:431
  167.6 2.0 collective-permute-done.36.refs_2_
  169.6 3.8 %collective-permute-start.40 = (bf16[2,112,128]{2,1,0:T(8,128)(2,1)S(1)}, bf16[2,112,128]{2,1,0:T(8,128)(2,1)S(1)}, u32[]{:S(2)}, u32[]{:S(2)}) collective-permute-start(bf16[2,112,128]{2,1,0:T(8,128)(2,1)S(1)} %added.7.refs_1_), channel_id=1, source_target_pairs={{0,48},{1,49},{2,50},{3,51},{4,52},{5,53},{6,54},{7,55},{8,56},{9,... | collective-permute-start | bytes 172040 | tf_op jit(solution)/shard_map/ppermute | solution.py:431
  174.4 2.3 %collective-permute-start.38 = (bf16[2,112,128]{2,1,0:T(8,128)(2,1)S(1)}, bf16[2,112,128]{2,1,0:T(8,128)(2,1)S(1)}, u32[]{:S(2)}, u32[]{:S(2)}) collective-permute-start(bf16[2,112,128]{2,1,0:T(8,128)(2,1)S(1)} %added.7.refs_1_), channel_id=1, source_target_pairs={{0,16},{1,17},{2,18},{3,19},{4,20},{5,21},{6,22},{7,23},{8,24},{9,... | collective-permute-start | bytes 172040 | tf_op jit(solution)/shard_map/ppermute | solution.py:431
  176.7 3.7 %collective-permute-done.39.refs_3_ = bf16[2,112,128]{2,1,0:T(8,128)(2,1)S(1)} collective-permute-done((bf16[2,112,128]{2,1,0:T(8,128)(2,1)S(1)}, bf16[2,112,128]{2,1,0:T(8,128)(2,1)S(1)}, u32[]{:S(2)}, u32[]{:S(2)}) %collective-permute-start.39) | collective-permute-done | bytes 57376 | tf_op jit(solution)/shard_map/ppermute | solution.py:431
  181.1 4.8 %collective-permute-done.41.refs_1_ = bf16[2,448,128]{2,1,0:T(8,128)(2,1)S(1)} collective-permute-done((bf16[2,448,128]{2,1,0:T(8,128)(2,1)S(1)}, bf16[2,448,128]{2,1,0:T(8,128)(2,1)S(1)}, u32[]{:S(2)}, u32[]{:S(2)}) %collective-permute-start.41) | collective-permute-done | bytes 229408 | tf_op jit(solution)/shard_map/ppermute | solution.py:431
  186.8 2.5 %collective-permute-start.47 = (bf16[896,128]{1,0:T(8,128)(2,1)S(1)}, bf16[896,128]{1,0:T(8,128)(2,1)S(1)}, u32[]{:S(2)}, u32[]{:S(2)}) collective-permute-start(bf16[896,128]{1,0:T(8,128)(2,1)S(1)} %bitcast.67), channel_id=1, source_target_pairs={{0,6},{1,7},{2,0},{3,1},{4,2},{5,3},{6,4},{7,5},{8,14},{9,15},{10,... | collective-permute-start | bytes 688136 | tf_op jit(solution)/shard_map/ppermute | solution.py:431
  189.4 3.3 %collective-permute-done.42.refs_1_ = bf16[896,128]{1,0:T(8,128)(2,1)S(1)} collective-permute-done((bf16[896,128]{1,0:T(8,128)(2,1)S(1)}, bf16[896,128]{1,0:T(8,128)(2,1)S(1)}, u32[]{:S(2)}, u32[]{:S(2)}) %collective-permute-start.42) | collective-permute-done | bytes 229408 | tf_op jit(solution)/shard_map/ppermute | solution.py:431
  192.7 2.7 %collective-permute-start.48 = (bf16[896,128]{1,0:T(8,128)(2,1)S(1)}, bf16[896,128]{1,0:T(8,128)(2,1)S(1)}, u32[]{:S(2)}, u32[]{:S(2)}) collective-permute-start(bf16[896,128]{1,0:T(8,128)(2,1)S(1)} %collective-permute-done.47.refs_3_), channel_id=1, source_target_pairs={{0,6},{1,7},{2,0},{3,1},{4,2},{5,3},{6,4},{7,5},{8,14},{9,15},{10,... | collective-permute-start | bytes 688136 | tf_op jit(solution)/shard_map/ppermute | solution.py:431
  195.4 5.9 %collective-permute-done.43.refs_2_ = bf16[896,128]{1,0:T(8,128)(2,1)S(1)} collective-permute-done((bf16[896,128]{1,0:T(8,128)(2,1)S(1)}, bf16[896,128]{1,0:T(8,128)(2,1)S(1)}, u32[]{:S(2)}, u32[]{:S(2)}) %collective-permute-start.43) | collective-permute-done | bytes 229408 | tf_op jit(solution)/shard_map/ppermute | solution.py:431
  202.0 8.1 %collective-permute-start.45 = (bf16[4,896,128]{2,1,0:T(8,128)(2,1)S(1)}, bf16[4,896,128]{2,1,0:T(8,128)(2,1)S(1)}, u32[]{:S(2)}, u32[]{:S(2)}) collective-permute-start(bf16[4,896,128]{2,1,0:T(8,128)(2,1)S(1)} %join_y.2.refs_1_), channel_id=1, source_target_pairs={{0,1},{1,0},{2,3},{3,2},{4,5},{5,4},{6,7},{7,6},{8,9},{9,8},{10,11... | collective-permute-start | bytes 2752520 | tf_op jit(solution)/shard_map/ppermute | solution.py:431
  210.7 1.8 collective-permute-start.49
  213.3 2.0 copy-done.2
  217.0 2.7 %unpack.2 = (f32[4,3,128,1152]{3,2,1,0:T(8,128)}, f32[4,1,128]{2,1,0:T(1,128)}) custom-call(s32[2]{0:T(128)S(1)} %pad_add_fusion.place_ref.refs_0_, bf16[4,896,128]{2,1,0:T(8,128)(2,1)S(1)} %join_y.2.refs_1_, bf16[4,896,128]{2,1,0:T(8,128)(2,1)S(1)} %join_y.3.refs_2_), custom_call_target="tpu_custom_call" | custom-call | tf_op jit(solution)/shard_map/unpack/pallas_call | solution.py:524
  219.7 3.9 %unpack.3 = (f32[4,3,128,1152]{3,2,1,0:T(8,128)}, f32[4,1,128]{2,1,0:T(1,128)}) custom-call(s32[2]{0:T(128)S(1)} %pad_add_fusion.place_ref.refs_0_, bf16[4,896,128]{2,1,0:T(8,128)(2,1)S(1)} %collective-permute-done.45.refs_1_, bf16[4,896,128]{2,1,0:T(8,128)(2,1)} %collective-permute-done.49.refs_2_, ...), custom_call_target="tpu_custom_call", output_to_operand_aliasing={{0}: (3, {}), {1}: (4, {})} | custom-call | tf_op jit(solution)/shard_map/unpack/pallas_call | solution.py:524
  (105 shorter events, 31.6 us)
Async XLA Ops:
  1.7 20.8 %collective-permute-start.2 = (bf16[256,256]{1,0:T(8,128)(2,1)S(1)}, bf16[256,256]{1,0:T(8,128)(2,1)S(1)}, u32[]{:S(2)}, u32[]{:S(2)}) collective-permute-start(bf16[256,256]{1,0:T(8,128)(2,1)S(1)} %bitcast.73), channel_id=1, source_target_pairs={{1,0},{2,1},{3,2},{4,3},{5,4},{6,5},{7,6},{8,7},{9,8},{10,9},{11,1... | collective-permute-start | bytes 393224 | tf_op jit(solution)/shard_map/ppermute | solution.py:285
  6.8 15.7 %collective-permute-start.1 = (bf16[256,256]{1,0:T(8,128)(2,1)S(1)}, bf16[256,256]{1,0:T(8,128)(2,1)S(1)}, u32[]{:S(2)}, u32[]{:S(2)}) collective-permute-start(bf16[256,256]{1,0:T(8,128)(2,1)S(1)} %bitcast.74), channel_id=1, source_target_pairs={{0,1},{1,2},{2,3},{3,4},{4,5},{5,6},{6,7},{7,8},{8,9},{9,10},{10,1... | collective-permute-start | bytes 393224 | tf_op jit(solution)/shard_map/ppermute | solution.py:285
  9.7 9.0 %collective-permute-start = (bf16[128,256]{1,0:T(8,128)(2,1)S(1)}, bf16[128,256]{1,0:T(8,128)(2,1)S(1)}, u32[]{:S(2)}, u32[]{:S(2)}) collective-permute-start(bf16[128,256]{1,0:T(8,128)(2,1)S(1)} %bitcast.90), channel_id=1, source_target_pairs={{0,2},{1,3},{2,4},{3,5},{4,6},{5,7},{6,8},{7,9},{8,10},{9,11},{10,... | collective-permute-start | bytes 196616 | tf_op jit(solution)/shard_map/ppermute | solution.py:285
  12.5 10.0 %collective-permute-start.3 = (bf16[128,256]{1,0:T(8,128)(2,1)S(1)}, bf16[128,256]{1,0:T(8,128)(2,1)S(1)}, u32[]{:S(2)}, u32[]{:S(2)}) collective-permute-start(bf16[128,256]{1,0:T(8,128)(2,1)S(1)} %bitcast.91), channel_id=1, source_target_pairs={{2,0},{3,1},{4,2},{5,3},{6,4},{7,5},{8,6},{9,7},{10,8},{11,9},{12,... | collective-permute-start | bytes 196616 | tf_op jit(solution)/shard_map/ppermute | solution.py:285
  16.0 13.3 %collective-permute-start.5 = (bf16[512,256]{1,0:T(8,128)(2,1)S(1)}, bf16[512,256]{1,0:T(8,128)(2,1)S(1)}, u32[]{:S(2)}, u32[]{:S(2)}) collective-permute-start(bf16[512,256]{1,0:T(8,128)(2,1)S(1)} %constant_dynamic-update-slice_fusion.own), channel_id=1, source_target_pairs={{1,0},{2,1},{3,2},{4,3},{5,4},{6,5},{7,6},{8,7},{9,8},{10,9},{11,1... | collective-permute-start | bytes 786440 | tf_op jit(solution)/shard_map/ppermute | solution.py:285
  18.8 10.5 %collective-permute-start.4 = (bf16[512,256]{1,0:T(8,128)(2,1)S(1)}, bf16[512,256]{1,0:T(8,128)(2,1)S(1)}, u32[]{:S(2)}, u32[]{:S(2)}) collective-permute-start(bf16[512,256]{1,0:T(8,128)(2,1)S(1)} %constant_dynamic-update-slice_fusion.own), channel_id=1, source_target_pairs={{0,1},{1,2},{2,3},{3,4},{4,5},{5,6},{6,7},{7,8},{8,9},{9,10},{10,1... | collective-permute-start | bytes 786440 | tf_op jit(solution)/shard_map/ppermute | solution.py:285
  35.0 7.7 %collective-permute-start.7 = (bf16[256,256]{1,0:T(8,128)(2,1)S(1)}, bf16[256,256]{1,0:T(8,128)(2,1)S(1)}, u32[]{:S(2)}, u32[]{:S(2)}) collective-permute-start(bf16[256,256]{1,0:T(8,128)(2,1)S(1)} %get-tuple-element.81.refs_9_), channel_id=1, source_target_pairs={{0,64},{1,65},{2,66},{3,67},{4,68},{5,69},{6,70},{7,71},{8,72},{9,... | collective-permute-start | bytes 393224 | tf_op jit(solution)/shard_map/ppermute | solution.py:277
  38.2 3.9 %collective-permute-start.6 = (bf16[128,256]{1,0:T(8,128)(2,1)S(1)}, bf16[128,256]{1,0:T(8,128)(2,1)S(1)}, u32[]{:S(2)}, u32[]{:S(2)}) collective-permute-start(bf16[128,256]{1,0:T(8,128)(2,1)S(1)} %get-tuple-element.80.refs_11_), channel_id=1, source_target_pairs={{0,65},{1,66},{2,67},{3,68},{4,69},{5,70},{6,71},{7,72},{8,73},{9,... | collective-permute-start | bytes 196616 | tf_op jit(solution)/shard_map/ppermute | solution.py:278
  39.8 2.9 %collective-permute-start.8 = (bf16[128,256]{1,0:T(8,128)(2,1)S(1)}, bf16[128,256]{1,0:T(8,128)(2,1)S(1)}, u32[]{:S(2)}, u32[]{:S(2)}) collective-permute-start(bf16[128,256]{1,0:T(8,128)(2,1)S(1)} %get-tuple-element.82.refs_10_), channel_id=1, source_target_pairs={{1,64},{2,65},{3,66},{4,67},{5,68},{6,69},{7,70},{8,71},{9,72},{10... | collective-permute-start | bytes 196616 | tf_op jit(solution)/shard_map/ppermute | solution.py:279
  43.3 2.0 collective-permute-start.10
  44.0 1.3 collective-permute-start.9
  45.9 2.0 collective-permute-start.13
  46.6 1.3 collective-permute-start.12
  48.6 6.5 %collective-permute-start.15 = (bf16[128,256]{1,0:T(8,128)(2,1)S(1)}, bf16[128,256]{1,0:T(8,128)(2,1)S(1)}, u32[]{:S(2)}, u32[]{:S(2)}) collective-permute-start(bf16[128,256]{1,0:T(8,128)(2,1)S(1)} %get-tuple-element.95), channel_id=1, source_target_pairs={{0,1},{1,2},{2,3},{3,4},{4,5},{5,6},{6,7},{7,8},{8,9},{9,10},{10,1... | collective-permute-start | bytes 196616 | tf_op jit(solution)/shard_map/ppermute | solution.py:285
  53.2 5.6 %collective-permute-start.16 = (bf16[128,256]{1,0:T(8,128)(2,1)S(1)}, bf16[128,256]{1,0:T(8,128)(2,1)S(1)}, u32[]{:S(2)}, u32[]{:S(2)}) collective-permute-start(bf16[128,256]{1,0:T(8,128)(2,1)S(1)} %get-tuple-element.97), channel_id=1, source_target_pairs={{1,0},{2,1},{3,2},{4,3},{5,4},{6,5},{7,6},{8,7},{9,8},{10,9},{11,1... | collective-permute-start | bytes 196616 | tf_op jit(solution)/shard_map/ppermute | solution.py:285
  61.0 2.2 collective-permute-start.18
  61.6 1.5 collective-permute-start.17
  62.5 0.7 collective-permute-start.19
  63.8 2.0 collective-permute-start.21
  64.5 1.3 collective-permute-start.20
  65.1 0.7 collective-permute-start.22
  66.5 40.0 %collective-permute-start.23 = (bf16[128,256]{1,0:T(8,128)(2,1)S(1)}, bf16[128,256]{1,0:T(8,128)(2,1)S(1)}, u32[]{:S(2)}, u32[]{:S(2)}) collective-permute-start(bf16[128,256]{1,0:T(8,128)(2,1)S(1)} %get-tuple-element.108), channel_id=1, source_target_pairs={{64,1},{65,2},{66,3},{67,4},{68,5},{69,6},{70,7},{71,8},{72,9},{73... | collective-permute-start | bytes 196616 | tf_op jit(solution)/shard_map/ppermute | solution.py:278
  67.9 43.8 %collective-permute-start.25 = (bf16[128,256]{1,0:T(8,128)(2,1)S(1)}, bf16[128,256]{1,0:T(8,128)(2,1)S(1)}, u32[]{:S(2)}, u32[]{:S(2)}) collective-permute-start(bf16[128,256]{1,0:T(8,128)(2,1)S(1)} %get-tuple-element.110), channel_id=1, source_target_pairs={{65,0},{66,1},{67,2},{68,3},{69,4},{70,5},{71,6},{72,7},{73,8},{74... | collective-permute-start | bytes 196616 | tf_op jit(solution)/shard_map/ppermute | solution.py:279
  69.2 42.7 %collective-permute-start.24 = (bf16[256,256]{1,0:T(8,128)(2,1)S(1)}, bf16[256,256]{1,0:T(8,128)(2,1)S(1)}, u32[]{:S(2)}, u32[]{:S(2)}) collective-permute-start(bf16[256,256]{1,0:T(8,128)(2,1)S(1)} %get-tuple-element.109.state_ref), channel_id=1, source_target_pairs={{64,0},{65,1},{66,2},{67,3},{68,4},{69,5},{70,6},{71,7},{72,8},{73... | collective-permute-start | bytes 393224 | tf_op jit(solution)/shard_map/ppermute | solution.py:277
  72.2 42.8 %collective-permute-start.30 = (bf16[4,896,128]{2,1,0:T(8,128)(2,1)S(1)}, bf16[4,896,128]{2,1,0:T(8,128)(2,1)S(1)}, u32[]{:S(2)}, u32[]{:S(2)}) collective-permute-start(bf16[4,896,128]{2,1,0:T(8,128)(2,1)S(1)} %get-tuple-element.129), channel_id=1, source_target_pairs={{0,1},{1,0},{2,3},{3,2},{4,5},{5,4},{6,7},{7,6},{8,9},{9,8},{10,11... | collective-permute-start | bytes 2752520 | tf_op jit(solution)/shard_map/ppermute | solution.py:431
  114.9 9.4 %collective-permute-start.26 = (bf16[4,896,128]{2,1,0:T(8,128)(2,1)S(1)}, bf16[4,896,128]{2,1,0:T(8,128)(2,1)S(1)}, u32[]{:S(2)}, u32[]{:S(2)}) collective-permute-start(bf16[4,896,128]{2,1,0:T(8,128)(2,1)S(1)} %get-tuple-element.119), channel_id=1, source_target_pairs={{0,1},{1,0},{2,3},{3,2},{4,5},{5,4},{6,7},{7,6},{8,9},{9,8},{10,11... | collective-permute-start | bytes 2752520 | tf_op jit(solution)/shard_map/ppermute | solution.py:431
  115.9 11.7 %collective-permute-start.31 = (bf16[1,896,128]{2,1,0:T(8,128)(2,1)S(1)}, bf16[1,896,128]{2,1,0:T(8,128)(2,1)S(1)}, u32[]{:S(2)}, u32[]{:S(2)}) collective-permute-start(bf16[1,896,128]{2,1,0:T(8,128)(2,1)S(1)} %get-tuple-element.131), channel_id=1, source_target_pairs={{0,4},{1,5},{2,6},{3,7},{4,0},{5,1},{6,2},{7,3},{8,12},{9,13},{10,... | collective-permute-start | bytes 688136 | tf_op jit(solution)/shard_map/ppermute | solution.py:431
  121.6 11.1 %collective-permute-start.32 = (bf16[1,896,128]{2,1,0:T(8,128)(2,1)S(1)}, bf16[1,896,128]{2,1,0:T(8,128)(2,1)S(1)}, u32[]{:S(2)}, u32[]{:S(2)}) collective-permute-start(bf16[1,896,128]{2,1,0:T(8,128)(2,1)S(1)} %get-tuple-element.132), channel_id=1, source_target_pairs={{0,2},{1,3},{2,4},{3,5},{4,6},{5,7},{6,0},{7,1},{8,10},{9,11},{10,... | collective-permute-start | bytes 688136 | tf_op jit(solution)/shard_map/ppermute | solution.py:431
  121.9 10.8 %collective-permute-start.33 = (bf16[1,896,128]{2,1,0:T(8,128)(2,1)S(1)}, bf16[1,896,128]{2,1,0:T(8,128)(2,1)S(1)}, u32[]{:S(2)}, u32[]{:S(2)}) collective-permute-start(bf16[1,896,128]{2,1,0:T(8,128)(2,1)S(1)} %get-tuple-element.133), channel_id=1, source_target_pairs={{0,6},{1,7},{2,0},{3,1},{4,2},{5,3},{6,4},{7,5},{8,14},{9,15},{10,... | collective-permute-start | bytes 688136 | tf_op jit(solution)/shard_map/ppermute | solution.py:431
  125.2 12.3 %collective-permute-start.27 = (bf16[1,896,128]{2,1,0:T(8,128)(2,1)S(1)}, bf16[1,896,128]{2,1,0:T(8,128)(2,1)S(1)}, u32[]{:S(2)}, u32[]{:S(2)}) collective-permute-start(bf16[1,896,128]{2,1,0:T(8,128)(2,1)S(1)} %get-tuple-element.121), channel_id=1, source_target_pairs={{0,4},{1,5},{2,6},{3,7},{4,0},{5,1},{6,2},{7,3},{8,12},{9,13},{10,... | collective-permute-start | bytes 688136 | tf_op jit(solution)/shard_map/ppermute | solution.py:431
  125.3 17.1 %collective-permute-start.28 = (bf16[1,896,128]{2,1,0:T(8,128)(2,1)S(1)}, bf16[1,896,128]{2,1,0:T(8,128)(2,1)S(1)}, u32[]{:S(2)}, u32[]{:S(2)}) collective-permute-start(bf16[1,896,128]{2,1,0:T(8,128)(2,1)S(1)} %get-tuple-element.122), channel_id=1, source_target_pairs={{0,2},{1,3},{2,4},{3,5},{4,6},{5,7},{6,0},{7,1},{8,10},{9,11},{10,... | collective-permute-start | bytes 688136 | tf_op jit(solution)/shard_map/ppermute | solution.py:431
  127.6 14.8 %collective-permute-start.29 = (bf16[1,896,128]{2,1,0:T(8,128)(2,1)S(1)}, bf16[1,896,128]{2,1,0:T(8,128)(2,1)S(1)}, u32[]{:S(2)}, u32[]{:S(2)}) collective-permute-start(bf16[1,896,128]{2,1,0:T(8,128)(2,1)S(1)} %get-tuple-element.123), channel_id=1, source_target_pairs={{0,6},{1,7},{2,0},{3,1},{4,2},{5,3},{6,4},{7,5},{8,14},{9,15},{10,... | collective-permute-start | bytes 688136 | tf_op jit(solution)/shard_map/ppermute | solution.py:431
  143.2 7.6 %collective-permute-start.34 = (bf16[2,448,128]{2,1,0:T(8,128)(2,1)S(1)}, bf16[2,448,128]{2,1,0:T(8,128)(2,1)S(1)}, u32[]{:S(2)}, u32[]{:S(2)}) collective-permute-start(bf16[2,448,128]{2,1,0:T(8,128)(2,1)S(1)} %get-tuple-element.135), channel_id=1, source_target_pairs={{0,8},{1,9},{2,10},{3,11},{4,12},{5,13},{6,14},{7,15},{8,0},{9,1},... | collective-permute-start | bytes 688136 | tf_op jit(solution)/shard_map/ppermute | solution.py:431
  151.5 16.1 %collective-permute-start.35 = (bf16[2,112,128]{2,1,0:T(8,128)(2,1)S(1)}, bf16[2,112,128]{2,1,0:T(8,128)(2,1)S(1)}, u32[]{:S(2)}, u32[]{:S(2)}) collective-permute-start(bf16[2,112,128]{2,1,0:T(8,128)(2,1)S(1)} %get-tuple-element.137), channel_id=1, source_target_pairs={{0,32},{1,33},{2,34},{3,35},{4,36},{5,37},{6,38},{7,39},{8,40},{9,... | collective-permute-start | bytes 172040 | tf_op jit(solution)/shard_map/ppermute | solution.py:431
  164.0 5.6 %collective-permute-start.36 = (bf16[2,112,128]{2,1,0:T(8,128)(2,1)S(1)}, bf16[2,112,128]{2,1,0:T(8,128)(2,1)S(1)}, u32[]{:S(2)}, u32[]{:S(2)}) collective-permute-start(bf16[2,112,128]{2,1,0:T(8,128)(2,1)S(1)} %get-tuple-element.138), channel_id=1, source_target_pairs={{0,16},{1,17},{2,18},{3,19},{4,20},{5,21},{6,22},{7,23},{8,24},{9,... | collective-permute-start | bytes 172040 | tf_op jit(solution)/shard_map/ppermute | solution.py:431
  164.0 5.6 %collective-permute-start.37 = (bf16[2,112,128]{2,1,0:T(8,128)(2,1)S(1)}, bf16[2,112,128]{2,1,0:T(8,128)(2,1)S(1)}, u32[]{:S(2)}, u32[]{:S(2)}) collective-permute-start(bf16[2,112,128]{2,1,0:T(8,128)(2,1)S(1)} %get-tuple-element.139), channel_id=1, source_target_pairs={{0,48},{1,49},{2,50},{3,51},{4,52},{5,53},{6,54},{7,55},{8,56},{9,... | collective-permute-start | bytes 172040 | tf_op jit(solution)/shard_map/ppermute | solution.py:431
  169.6 7.1 %collective-permute-start.40 = (bf16[2,112,128]{2,1,0:T(8,128)(2,1)S(1)}, bf16[2,112,128]{2,1,0:T(8,128)(2,1)S(1)}, u32[]{:S(2)}, u32[]{:S(2)}) collective-permute-start(bf16[2,112,128]{2,1,0:T(8,128)(2,1)S(1)} %added.7.refs_1_), channel_id=1, source_target_pairs={{0,48},{1,49},{2,50},{3,51},{4,52},{5,53},{6,54},{7,55},{8,56},{9,... | collective-permute-start | bytes 172040 | tf_op jit(solution)/shard_map/ppermute | solution.py:431
  173.4 7.0 %collective-permute-start.39 = (bf16[2,112,128]{2,1,0:T(8,128)(2,1)S(1)}, bf16[2,112,128]{2,1,0:T(8,128)(2,1)S(1)}, u32[]{:S(2)}, u32[]{:S(2)}) collective-permute-start(bf16[2,112,128]{2,1,0:T(8,128)(2,1)S(1)} %added.7.refs_1_), channel_id=1, source_target_pairs={{0,32},{1,33},{2,34},{3,35},{4,36},{5,37},{6,38},{7,39},{8,40},{9,... | collective-permute-start | bytes 172040 | tf_op jit(solution)/shard_map/ppermute | solution.py:431
  174.4 6.0 %collective-permute-start.38 = (bf16[2,112,128]{2,1,0:T(8,128)(2,1)S(1)}, bf16[2,112,128]{2,1,0:T(8,128)(2,1)S(1)}, u32[]{:S(2)}, u32[]{:S(2)}) collective-permute-start(bf16[2,112,128]{2,1,0:T(8,128)(2,1)S(1)} %added.7.refs_1_), channel_id=1, source_target_pairs={{0,16},{1,17},{2,18},{3,19},{4,20},{5,21},{6,22},{7,23},{8,24},{9,... | collective-permute-start | bytes 172040 | tf_op jit(solution)/shard_map/ppermute | solution.py:431
  181.0 5.0 %collective-permute-start.41 = (bf16[2,448,128]{2,1,0:T(8,128)(2,1)S(1)}, bf16[2,448,128]{2,1,0:T(8,128)(2,1)S(1)}, u32[]{:S(2)}, u32[]{:S(2)}) collective-permute-start(bf16[2,448,128]{2,1,0:T(8,128)(2,1)S(1)} %bitcast.65), channel_id=1, source_target_pairs={{0,8},{1,9},{2,10},{3,11},{4,12},{5,13},{6,14},{7,15},{8,0},{9,1},... | collective-permute-start | bytes 688136 | tf_op jit(solution)/shard_map/ppermute | solution.py:431
  186.5 6.2 %collective-permute-start.42 = (bf16[896,128]{1,0:T(8,128)(2,1)S(1)}, bf16[896,128]{1,0:T(8,128)(2,1)S(1)}, u32[]{:S(2)}, u32[]{:S(2)}) collective-permute-start(bf16[896,128]{1,0:T(8,128)(2,1)S(1)} %bitcast.70), channel_id=1, source_target_pairs={{0,2},{1,3},{2,4},{3,5},{4,6},{5,7},{6,0},{7,1},{8,10},{9,11},{10,... | collective-permute-start | bytes 688136 | tf_op jit(solution)/shard_map/ppermute | solution.py:431
  186.8 5.9 %collective-permute-start.47 = (bf16[896,128]{1,0:T(8,128)(2,1)S(1)}, bf16[896,128]{1,0:T(8,128)(2,1)S(1)}, u32[]{:S(2)}, u32[]{:S(2)}) collective-permute-start(bf16[896,128]{1,0:T(8,128)(2,1)S(1)} %bitcast.67), channel_id=1, source_target_pairs={{0,6},{1,7},{2,0},{3,1},{4,2},{5,3},{6,4},{7,5},{8,14},{9,15},{10,... | collective-permute-start | bytes 688136 | tf_op jit(solution)/shard_map/ppermute | solution.py:431
  189.3 6.1 %collective-permute-start.44 = (bf16[896,128]{1,0:T(8,128)(2,1)S(1)}, bf16[896,128]{1,0:T(8,128)(2,1)S(1)}, u32[]{:S(2)}, u32[]{:S(2)}) collective-permute-start(bf16[896,128]{1,0:T(8,128)(2,1)S(1)} %bitcast.71), channel_id=1, source_target_pairs={{0,6},{1,7},{2,0},{3,1},{4,2},{5,3},{6,4},{7,5},{8,14},{9,15},{10,... | collective-permute-start | bytes 688136 | tf_op jit(solution)/shard_map/ppermute | solution.py:431
  192.7 8.6 %collective-permute-start.43 = (bf16[896,128]{1,0:T(8,128)(2,1)S(1)}, bf16[896,128]{1,0:T(8,128)(2,1)S(1)}, u32[]{:S(2)}, u32[]{:S(2)}) collective-permute-start(bf16[896,128]{1,0:T(8,128)(2,1)S(1)} %collective-permute-done.42.refs_1_), channel_id=1, source_target_pairs={{0,2},{1,3},{2,4},{3,5},{4,6},{5,7},{6,0},{7,1},{8,10},{9,11},{10,... | collective-permute-start | bytes 688136 | tf_op jit(solution)/shard_map/ppermute | solution.py:431
  192.7 17.4 %collective-permute-start.46 = (bf16[896,128]{1,0:T(8,128)(2,1)S(1)}, bf16[896,128]{1,0:T(8,128)(2,1)S(1)}, u32[]{:S(2)}, u32[]{:S(2)}) collective-permute-start(bf16[896,128]{1,0:T(8,128)(2,1)S(1)} %bitcast.68), channel_id=1, source_target_pairs={{0,2},{1,3},{2,4},{3,5},{4,6},{5,7},{6,0},{7,1},{8,10},{9,11},{10,... | collective-permute-start | bytes 688136 | tf_op jit(solution)/shard_map/ppermute | solution.py:431
  192.7 17.4 %collective-permute-start.48 = (bf16[896,128]{1,0:T(8,128)(2,1)S(1)}, bf16[896,128]{1,0:T(8,128)(2,1)S(1)}, u32[]{:S(2)}, u32[]{:S(2)}) collective-permute-start(bf16[896,128]{1,0:T(8,128)(2,1)S(1)} %collective-permute-done.47.refs_3_), channel_id=1, source_target_pairs={{0,6},{1,7},{2,0},{3,1},{4,2},{5,3},{6,4},{7,5},{8,14},{9,15},{10,... | collective-permute-start | bytes 688136 | tf_op jit(solution)/shard_map/ppermute | solution.py:431
  202.0 17.8 %collective-permute-start.45 = (bf16[4,896,128]{2,1,0:T(8,128)(2,1)S(1)}, bf16[4,896,128]{2,1,0:T(8,128)(2,1)S(1)}, u32[]{:S(2)}, u32[]{:S(2)}) collective-permute-start(bf16[4,896,128]{2,1,0:T(8,128)(2,1)S(1)} %join_y.2.refs_1_), channel_id=1, source_target_pairs={{0,1},{1,0},{2,3},{3,2},{4,5},{5,4},{6,7},{7,6},{8,9},{9,8},{10,11... | collective-permute-start | bytes 2752520 | tf_op jit(solution)/shard_map/ppermute | solution.py:431
  210.7 9.0 %collective-permute-start.49 = (bf16[4,896,128]{2,1,0:T(8,128)(2,1)S(1)}, bf16[4,896,128]{2,1,0:T(8,128)(2,1)}, u32[]{:S(2)}, u32[]{:S(2)}) collective-permute-start(bf16[4,896,128]{2,1,0:T(8,128)(2,1)S(1)} %join_y.3.refs_2_), channel_id=1, source_target_pairs={{0,1},{1,0},{2,3},{3,2},{4,5},{5,4},{6,7},{7,6},{8,9},{9,8},{10,11... | collective-permute-start | bytes 2752520 | tf_op jit(solution)/shard_map/ppermute | solution.py:431
  (5 other events, 51.5 us)
